TPU v7x, 128 devices: a whole 4x4x4 slice. The times are simulated.
128 devices in a mesh: space: 16 (over y, z_hi, core), band: 8 (over x, z_lo).
Axes of the slice: x: 4, y: 4, z: 4 (z_hi: 2, z_lo: 2; z = z_hi * 2 + z_lo), core: 2. Of those that a mesh axis runs over, the one named last changes fastest.
Arguments:
- states: bfloat16 [165888, 1024], P('space', 'band'), may hold values from -12 to 12, as said below
- potential: float32 [165888], P('space'), may hold values from 0 to 2, as said below
- cell_matrix: bfloat16 [512, 512], replicated, may hold values from -1 to 1, as said below
- cell_scale: float32 [400], P('space'), may hold values from 0.5 to 1.5
- connectivity: int32 [400, 512], P('space'), may hold values from 0 to 10367, as said below
- lower_bound: float32 [1], replicated, may hold values from 0.4 to 0.8
- upper_bound: float32 [1], replicated, may hold values from 16 to 20
Outputs:
- filtered: bfloat16 [165888, 1024], P('space', 'band')
- projected: float32 [1024, 1024], P('band', 'space')
Inputs may be any that keep to these rules, and one draw needn't show every extreme that they name: `connectivity`: each slab is a block of 5 x 5 x 1 hexahedral cells with 8 nodes along each edge, slabs stacked along the third dimension. Cell c of a slab is the cell at position (c % 5, (c // 5) % 5, c // 25), and its entry j is its node at corner offset (j % 8, (j // 8) % 8, j // 64). Nodes shared by cells get the same row. The nodes of node plane k along the third dimension have rows k * 1296 to (k + 1) * 1296 - 1 of the slab, in an order of their own. `states`: the copies of a node on a face shared by two slabs carry equal values. `potential`: the copies of a node on a face shared by two slabs carry equal values. `cell_matrix`: symmetric positive definite.
All inputs are finite; a program needn't handle non-finite values.
Results may differ from a plain program's by a relative error of at most 0.012.
The roundings to bfloat16 on the way count: a program that leaves them out, or rounds other values in their place, can miss the bound.
Values may be sent and summed in bfloat16 or wider, within the bound.
No kernel may reach another device: no remote copies, remote signals or barrier semaphores. Data moves between devices by JAX's collectives and lax.ppermute only.
A program may use at most 128 MiB of HBM per device.

v0:
```python
import jax
import jax.numpy as jnp
from jax import lax
from jax.sharding import PartitionSpec as P

EDGE = 8
SLAB_XY = 5
SLAB_Z = 1
STEPS = 4
CELLS_DEV = 25


def with_halo(cells, sides, width):
    for axis, dim in sides:
        count = lax.axis_size(axis)
        ends = count - 1
        head = lax.slice_in_dim(cells, 0, width, axis=dim)
        tail = lax.slice_in_dim(cells, cells.shape[dim] - width, cells.shape[dim], axis=dim)
        cells = jnp.concatenate(
            [
                lax.ppermute(tail, axis, [(i, (i + 1) % count) for i in range(ends)]),
                cells,
                lax.ppermute(head, axis, [((i + 1) % count, i) for i in range(ends)]),
            ],
            axis=dim,
        )
    return cells


def in_blocks(x, dim, peers):
    dims = x.shape
    blocks = x.reshape(*dims[:dim], peers, dims[dim] // peers, *dims[dim + 1 :])
    return jnp.moveaxis(blocks, dim, 0)


def summed_on_arrival(x, axis, dim):
    blocks = in_blocks(x, dim, lax.axis_size(axis))
    arrived = lax.all_to_all(blocks, axis, split_axis=0, concat_axis=0, tiled=True)
    return arrived.astype(jnp.float32).sum(axis=0)


def settle(values):
    return lax.optimization_barrier(values.astype(jnp.bfloat16))


def plain_index():
    side_nodes = (EDGE - 1) * SLAB_XY + 1
    corner = jnp.arange(EDGE, dtype=jnp.int32)
    cell_ids = jnp.arange(CELLS_DEV, dtype=jnp.int32)
    cell_x = cell_ids % SLAB_XY
    cell_y = cell_ids // SLAB_XY % SLAB_XY
    cell_z = cell_ids // (SLAB_XY * SLAB_XY)
    index_x = cell_x[:, None, None, None] * (EDGE - 1) + corner[None, None, None, :]
    index_y = cell_y[:, None, None, None] * (EDGE - 1) + corner[None, None, :, None]
    index_z = cell_z[:, None, None, None] * (EDGE - 1) + corner[None, :, None, None]
    return ((index_z * side_nodes + index_y) * side_nodes + index_x).reshape(-1)


def cut_cells(field, axis, count):
    pieces = [
        lax.slice_in_dim(field, start * (EDGE - 1), start * (EDGE - 1) + EDGE, axis=axis)
        for start in range(count)
    ]
    return jnp.stack(pieces, axis=axis)


def fold_cells(blocks, axis, count, length):
    total = None
    for start in range(count):
        piece = lax.index_in_dim(blocks, start, axis=axis, keepdims=False)
        widths = [(0, 0)] * piece.ndim
        widths[axis] = (start * (EDGE - 1), length - start * (EDGE - 1) - EDGE)
        padded = jnp.pad(piece, widths)
        total = padded if total is None else total + padded
    return total


def local(states, potential, cell_matrix, cell_scale, connectivity, lower_bound, upper_bound):
    side_nodes = (EDGE - 1) * SLAB_XY + 1
    face_size = side_nodes * side_nodes
    layer_count = (EDGE - 1) * SLAB_Z + 1
    node_count = states.shape[0]
    columns = states.shape[1]
    ordered = jnp.zeros((node_count,), jnp.int32).at[plain_index()].set(connectivity.reshape(-1))
    start_states = states[ordered]
    potential_plane = potential[ordered]
    center = (lower_bound[0] + upper_bound[0]) * 0.5
    half_width = (upper_bound[0] - lower_bound[0]) * 0.5

    def apply_h(values):
        grid = values.reshape(layer_count, side_nodes, side_nodes, columns)
        blocks = cut_cells(grid, 0, SLAB_Z)
        blocks = cut_cells(blocks, 2, SLAB_XY)
        blocks = cut_cells(blocks, 4, SLAB_XY)
        blocks = blocks.transpose(0, 2, 4, 1, 3, 5, 6).reshape(-1, EDGE * EDGE * EDGE, columns)
        products = jnp.einsum(
            "ij,cjs->cis", cell_matrix, blocks, preferred_element_type=jnp.float32
        )
        products = products * cell_scale[:, None, None]
        products = products.reshape(SLAB_Z, SLAB_XY, SLAB_XY, EDGE, EDGE, EDGE, columns).transpose(
            0, 3, 1, 4, 2, 5, 6
        )
        summed = fold_cells(products, 4, SLAB_XY, side_nodes)
        summed = fold_cells(summed, 2, SLAB_XY, side_nodes)
        summed = fold_cells(summed, 0, SLAB_Z, layer_count)
        assembled = summed.reshape(node_count, columns)
        face_vals = jnp.stack([assembled[:face_size], assembled[node_count - face_size :]], axis=0)
        padded = with_halo(face_vals, (("space", 0),), 1)
        assembled = jnp.concatenate(
            [
                assembled[:face_size] + padded[0],
                assembled[face_size : node_count - face_size],
                assembled[node_count - face_size :] + padded[3],
            ],
            axis=0,
        )
        return assembled + potential_plane[:, None] * values.astype(jnp.float32)

    previous = start_states
    current = settle((apply_h(previous) - center * previous.astype(jnp.float32)) / half_width)
    for repeat in range(STEPS - 1):
        following = settle(
            2.0 * ((apply_h(current) - center * current.astype(jnp.float32)) / half_width)
            - previous.astype(jnp.float32)
        )
        previous, current = (current, following)
    image = settle(apply_h(current))
    position = lax.axis_index("space")
    slab_count = lax.axis_size("space")
    low_w = jnp.where(position > 0, 0.5, 1.0).astype(jnp.float32)
    up_w = jnp.where(position < slab_count - 1, 0.5, 1.0).astype(jnp.float32)
    image_f = image.astype(jnp.float32)
    weighted = settle(
        jnp.concatenate(
            [
                image_f[:face_size] * low_w,
                image_f[face_size : node_count - face_size],
                image_f[node_count - face_size :] * up_w,
            ],
            axis=0,
        )
    )
    global_count = face_size * ((EDGE - 1) * SLAB_Z * slab_count + 1)
    contract_rows = (((0,), (0,)), ((), ()))
    node_states, node_images = (
        lax.all_to_all(current, "band", split_axis=0, concat_axis=1, tiled=True),
        lax.all_to_all(weighted, "band", split_axis=0, concat_axis=1, tiled=True),
    )
    partial_matrix = lax.dot_general(
        node_states, node_images, contract_rows, preferred_element_type=jnp.float32
    )
    row_sums = summed_on_arrival(partial_matrix.astype(jnp.bfloat16), "band", 0)
    totals = summed_on_arrival(row_sums.astype(jnp.bfloat16), "space", 1)
    filtered = jnp.zeros_like(states).at[ordered].set(current)
    return (filtered, totals / global_count)


def solution(mesh):
    placed = (P("space", "band"), P("space"), P(), P("space"), P("space", None), P(), P())
    return jax.shard_map(
        local,
        mesh=mesh,
        in_specs=placed,
        out_specs=(P("space", "band"), P("band", "space")),
        check_vma=False,
    )
```

profile of v0, /device:TPU:1, one launch (start us, length us, event | category | flops | bytes accessed | tf_op | source)
XLA Modules:
  0.0 654.3 jit_solution(2693255487922485711)
XLA Ops:
  2.7 47.3 %scatter_custom_fusion = s32[10368]{0:T(1024)S(1)} fusion(s32[12800]{0:T(1024)S(1)} %fusion.89, s32[12800]{0:T(1024)S(1)} %reshape.277, s32[]{:T(128)} %constant.49.clone.1), kind=kCustom, calls=%fused_computation.261 | custom fusion | bytes 41476 | tf_op jit(solution)/shard_map/scatter | solution.py:84
  50.6 21.9 %gather_fusion = bf16[10368,128]{1,0:T(8,128)(2,1)} fusion(bf16[10368,128]{1,0:T(8,128)(2,1)S(1)} %copy-done, s32[11264]{0:T(1024)S(1)} %pad_clamp_fusion), kind=kCustom, calls=%fused_computation | custom fusion | bytes 5349888 | tf_op jit(solution)/shard_map/gather | solution.py:85
  72.5 5.1 stack_reshape.15
  85.9 5.4 multiply_bitcast_fusion.4
  91.2 8.2 %copy.148 = f32[25,512,128]{2,1,0:T(8,128)} copy(f32[25,512,128]{1,2,0:T(8,128)} %multiply_bitcast_fusion.4) | data formatting | bytes 13107200 | tf_op jit(solution)/shard_map/mul | solution.py:99
  110.3 6.9 %collective-permute-start = (f32[1,1296,128]{2,1,0:T(8,128)}, f32[1,1296,128]{2,1,0:T(8,128)}, u32[]{:S(2)}, u32[]{:S(2)}) collective-permute-start(f32[1,1296,128]{2,1,0:T(8,128)} %bitcast.470), channel_id=1, source_target_pairs={{0,8},{8,16},{16,24},{24,32},{32,40},{40,48},{48,56},{56,64},{64,7... | collective-permute-start | bytes 1990664 | tf_op jit(solution)/shard_map/ppermute | solution.py:21
  136.9 53.6 %gather_fusion.1 = f32[10368]{0:T(1024)S(1)} fusion(f32[10368]{0:T(1024)S(1)} %copy-done.2, s32[11264]{0:T(1024)S(1)} %pad_clamp_fusion), kind=kCustom, calls=%fused_computation.1 | custom fusion | bytes 124416 | tf_op jit(solution)/shard_map/gather | solution.py:86
  193.4 9.6 %fusion.18 = bf16[10368,128]{1,0:T(8,128)(2,1)} fusion(bf16[10368,128]{1,0:T(8,128)(2,1)S(1)} %copy-done.3, f32[1296,128]{1,0:T(8,128)S(1)} %bitcast_add_fusion.8, f32[7776,128]{1,0:T(8,128)} %slice.434, f32[1296,128]{1,0:T(8,128)S(1)} %bitcast_add_fusion.9, f32[]{:T(128)} %bitcast.32, f32[]{:T(128)} %bitcast.31, f32[10368]{0:T(1024)S(1)} %gather_fusion.1), kind=kLoop, calls=%fused_computation.44 | loop fusion | flops 11943936 | bytes 10658312 | tf_op jit(solution)/shard_map/convert_element_type | solution.py:43
  203.0 5.1 stack_reshape.16
  216.3 5.4 multiply_bitcast_fusion.3
  221.7 8.2 %copy.157 = f32[25,512,128]{2,1,0:T(8,128)} copy(f32[25,512,128]{1,2,0:T(8,128)} %multiply_bitcast_fusion.3) | data formatting | bytes 13107200 | tf_op jit(solution)/shard_map/mul | solution.py:99
  241.6 5.1 collective-permute-start.2
  268.6 9.8 %fusion.7 = bf16[10368,128]{1,0:T(8,128)(2,1)} fusion(bf16[10368,128]{1,0:T(8,128)(2,1)S(1)} %copy-done.3, bf16[10368,128]{1,0:T(8,128)(2,1)S(1)} %copy-done.5, f32[1296,128]{1,0:T(8,128)S(1)} %bitcast_add_fusion.6, f32[7776,128]{1,0:T(8,128)} %slice.460, f32[1296,128]{1,0:T(8,128)S(1)} %bitcast_add_fusion.7, f32[]{:T(128)} %bitcast.32, f32[]{:T(128)} %bitcast.31, ...), kind=kLoop, calls=%fused_computation.32 | loop fusion | flops 15925248 | bytes 13312520 | tf_op jit(solution)/shard_map/convert_element_type | solution.py:43
  278.3 5.1 stack_reshape.17
  291.7 5.4 multiply_bitcast_fusion.2
  297.0 8.2 %copy.166 = f32[25,512,128]{2,1,0:T(8,128)} copy(f32[25,512,128]{1,2,0:T(8,128)} %multiply_bitcast_fusion.2) | data formatting | bytes 13107200 | tf_op jit(solution)/shard_map/mul | solution.py:99
  342.1 9.9 %fusion.12 = bf16[10368,128]{1,0:T(8,128)(2,1)} fusion(bf16[10368,128]{1,0:T(8,128)(2,1)} %fusion.18, bf16[10368,128]{1,0:T(8,128)(2,1)S(1)} %copy-done.4, f32[1296,128]{1,0:T(8,128)S(1)} %bitcast_add_fusion.4, f32[7776,128]{1,0:T(8,128)} %slice.486, f32[1296,128]{1,0:T(8,128)S(1)} %bitcast_add_fusion.5, f32[]{:T(128)} %bitcast.32, f32[]{:T(128)} %bitcast.31, ...), kind=kLoop, calls=%fused_computation.37 | loop fusion | flops 15925248 | bytes 13312520 | tf_op jit(solution)/shard_map/convert_element_type | solution.py:43
  352.1 5.1 stack_reshape.18
  365.4 5.4 multiply_bitcast_fusion.1
  370.8 8.2 %copy.175 = f32[25,512,128]{2,1,0:T(8,128)} copy(f32[25,512,128]{1,2,0:T(8,128)} %multiply_bitcast_fusion.1) | data formatting | bytes 13107200 | tf_op jit(solution)/shard_map/mul | solution.py:99
  417.4 9.8 %fusion.19 = bf16[10368,128]{1,0:T(8,128)(2,1)} fusion(bf16[10368,128]{1,0:T(8,128)(2,1)S(1)} %copy-done.4, bf16[10368,128]{1,0:T(8,128)(2,1)S(1)} %copy-done.6, f32[1296,128]{1,0:T(8,128)S(1)} %bitcast_add_fusion.2, f32[7776,128]{1,0:T(8,128)} %slice.512, f32[1296,128]{1,0:T(8,128)S(1)} %bitcast_add_fusion.3, f32[]{:T(128)} %bitcast.32, f32[]{:T(128)} %bitcast.31, ...), kind=kLoop, calls=%fused_computation.45 | loop fusion | flops 15925248 | bytes 13312520 | tf_op jit(solution)/shard_map/convert_element_type | solution.py:43
  427.1 5.1 stack_reshape.19
  440.5 5.4 multiply_bitcast_fusion
  445.8 8.2 %copy.185 = f32[25,512,128]{2,1,0:T(8,128)} copy(f32[25,512,128]{1,2,0:T(8,128)} %multiply_bitcast_fusion) | data formatting | bytes 13107200 | tf_op jit(solution)/shard_map/mul | solution.py:99
  490.6 8.7 %fusion.17 = bf16[10368,128]{1,0:T(8,128)(2,1)S(1)} fusion(f32[1296,128]{1,0:T(8,128)S(1)} %bitcast_add_fusion, f32[7776,128]{1,0:T(8,128)} %slice.538, f32[1296,128]{1,0:T(8,128)S(1)} %bitcast_add_fusion.1, bf16[10368,128]{1,0:T(8,128)(2,1)} %fusion.19, f32[10368]{0:T(1024)S(1)} %gather_fusion.1), kind=kLoop, calls=%fused_computation.43 | loop fusion | flops 7962624 | bytes 10658304 | tf_op jit(solution)/shard_map/convert_element_type | solution.py:43
  502.3 9.5 %pad_maximum_fusion = bf16[10368,128]{1,0:T(8,128)(2,1)} fusion(bf16[1296,128]{1,0:T(8,128)(2,1)S(1)} %get-tuple-element.63, bf16[7776,128]{1,0:T(8,128)(2,1)S(1)} %slice-done, bf16[1296,128]{1,0:T(8,128)(2,1)S(1)} %get-tuple-element.62), kind=kLoop, calls=%fused_computation.71 | loop fusion | flops 7962624 | bytes 5308416 | tf_op jit(solution)/shard_map/concatenate | solution.py:134
  511.8 15.6 %all-to-all-done = bf16[8,1296,128]{2,1,0:T(8,128)(2,1)} async-done(((bf16[8,1296,128]{2,1,0:T(8,128)(2,1)}), bf16[8,1296,128]{2,1,0:T(8,128)(2,1)}, u32[]{:S(2)}, u32[]{:S(2)}) %all-to-all-start) | async-done | bytes 2654240 | tf_op jit(solution)/shard_map/all_to_all | solution.py:146
  527.5 36.4 %all_to_all.48 = bf16[8,1296,128]{2,1,0:T(8,128)(2,1)S(1)} all-to-all(bf16[8,1296,128]{2,1,0:T(8,128)(2,1)} %bitcast.461), channel_id=1, replica_groups=mesh['space'=16,'band'=8] {'band'}, dimensions={0} | all-to-all | bytes 5308416 | tf_op jit(solution)/shard_map/all_to_all | solution.py:147
  563.8 5.4 fusion.25
  569.3 28.7 %all_to_all.49 = bf16[8,128,1024]{2,1,0:T(8,128)(2,1)} all-to-all(bf16[8,128,1024]{2,1,0:T(8,128)(2,1)S(1)} %bitcast.467), channel_id=1, replica_groups=mesh['space'=16,'band'=8] {'band'}, dimensions={0} | all-to-all | bytes 4194304 | tf_op jit(solution)/shard_map/all_to_all | solution.py:38
  600.8 11.8 %all-to-all-start.3 = ((bf16[16,128,64]{1,2,0:T(8,128)(2,1)}), bf16[16,128,64]{1,2,0:T(8,128)(2,1)S(1)}, u32[]{:S(2)}, u32[]{:S(2)}) async-start(bf16[16,128,64]{1,2,0:T(8,128)(2,1)} %bitcast.159), calls=%async_computation.3 | async-start | bytes 524288 | tf_op jit(solution)/shard_map/all_to_all | solution.py:38
  612.6 40.9 %scatter_custom_fusion.1 = bf16[10368,128]{1,0:T(8,128)(2,1)} fusion(s32[10368]{0:T(1024)} %copy-done.30, bf16[10368,128]{1,0:T(8,128)(2,1)} %fusion.19, bf16[]{:T(256)} %constant.48.clone.1), kind=kCustom, calls=%fused_computation.73 | custom fusion | bytes 2654720 | tf_op jit(solution)/shard_map/scatter | solution.py:154
  (219 shorter events, 227.1 us)
Async XLA Ops:
  0.6 50.0 %copy-start = (bf16[10368,128]{1,0:T(8,128)(2,1)S(1)}, bf16[10368,128]{1,0:T(8,128)(2,1)}, u32[]{:S(2)}) copy-start(bf16[10368,128]{1,0:T(8,128)(2,1)} %param.7) | copy-start | bytes 7962628
  105.3 2.4 copy-start.14
  110.3 80.2 %collective-permute-start = (f32[1,1296,128]{2,1,0:T(8,128)}, f32[1,1296,128]{2,1,0:T(8,128)}, u32[]{:S(2)}, u32[]{:S(2)}) collective-permute-start(f32[1,1296,128]{2,1,0:T(8,128)} %bitcast.470), channel_id=1, source_target_pairs={{0,8},{8,16},{16,24},{24,32},{32,40},{40,48},{48,56},{56,64},{64,7... | collective-permute-start | bytes 1990664 | tf_op jit(solution)/shard_map/ppermute | solution.py:21
  119.7 72.3 %collective-permute-start.1 = (f32[1,1296,128]{2,1,0:T(8,128)}, f32[1,1296,128]{2,1,0:T(8,128)}, u32[]{:S(2)}, u32[]{:S(2)}) collective-permute-start(f32[1,1296,128]{2,1,0:T(8,128)} %bitcast.469), channel_id=1, source_target_pairs={{8,0},{16,8},{24,16},{32,24},{40,32},{48,40},{56,48},{64,56},{72,6... | collective-permute-start | bytes 1990664 | tf_op jit(solution)/shard_map/ppermute | solution.py:23
  132.1 4.8 copy-start.2
  190.5 2.9 copy-start.3
  235.7 2.0 copy-start.16
  235.7 2.4 copy-start.17
  235.7 2.8 copy-start.18
  235.8 3.2 copy-start.19
  241.6 23.3 %collective-permute-start.2 = (f32[1,1296,128]{2,1,0:T(8,128)}, f32[1,1296,128]{2,1,0:T(8,128)}, u32[]{:S(2)}, u32[]{:S(2)}) collective-permute-start(f32[1,1296,128]{2,1,0:T(8,128)} %bitcast.472), channel_id=1, source_target_pairs={{0,8},{8,16},{16,24},{24,32},{32,40},{40,48},{48,56},{56,64},{64,7... | collective-permute-start | bytes 1990664 | tf_op jit(solution)/shard_map/ppermute | solution.py:21
  253.4 13.8 %collective-permute-start.3 = (f32[1,1296,128]{2,1,0:T(8,128)}, f32[1,1296,128]{2,1,0:T(8,128)}, u32[]{:S(2)}, u32[]{:S(2)}) collective-permute-start(f32[1,1296,128]{2,1,0:T(8,128)} %bitcast.473), channel_id=1, source_target_pairs={{8,0},{16,8},{24,16},{32,24},{40,32},{48,40},{56,48},{64,56},{72,6... | collective-permute-start | bytes 1990664 | tf_op jit(solution)/shard_map/ppermute | solution.py:23
  264.8 3.7 copy-start.5
  311.1 2.4 copy-start.22
  316.0 22.5 %collective-permute-start.4 = (f32[1,1296,128]{2,1,0:T(8,128)}, f32[1,1296,128]{2,1,0:T(8,128)}, u32[]{:S(2)}, u32[]{:S(2)}) collective-permute-start(f32[1,1296,128]{2,1,0:T(8,128)} %bitcast.474), channel_id=1, source_target_pairs={{0,8},{8,16},{16,24},{24,32},{32,40},{40,48},{48,56},{56,64},{64,7... | collective-permute-start | bytes 1990664 | tf_op jit(solution)/shard_map/ppermute | solution.py:21
  327.0 13.8 %collective-permute-start.5 = (f32[1,1296,128]{2,1,0:T(8,128)}, f32[1,1296,128]{2,1,0:T(8,128)}, u32[]{:S(2)}, u32[]{:S(2)}) collective-permute-start(f32[1,1296,128]{2,1,0:T(8,128)} %bitcast.475), channel_id=1, source_target_pairs={{8,0},{16,8},{24,16},{32,24},{40,32},{48,40},{56,48},{64,56},{72,6... | collective-permute-start | bytes 1990664 | tf_op jit(solution)/shard_map/ppermute | solution.py:23
  338.5 3.6 copy-start.4
  384.8 2.0 copy-start.24
  384.8 2.4 copy-start.25
  384.9 2.8 copy-start.26
  384.9 3.2 copy-start.27
  390.7 22.8 %collective-permute-start.6 = (f32[1,1296,128]{2,1,0:T(8,128)}, f32[1,1296,128]{2,1,0:T(8,128)}, u32[]{:S(2)}, u32[]{:S(2)}) collective-permute-start(f32[1,1296,128]{2,1,0:T(8,128)} %bitcast.476), channel_id=1, source_target_pairs={{0,8},{8,16},{16,24},{24,32},{32,40},{40,48},{48,56},{56,64},{64,7... | collective-permute-start | bytes 1990664 | tf_op jit(solution)/shard_map/ppermute | solution.py:21
  402.2 13.8 %collective-permute-start.7 = (f32[1,1296,128]{2,1,0:T(8,128)}, f32[1,1296,128]{2,1,0:T(8,128)}, u32[]{:S(2)}, u32[]{:S(2)}) collective-permute-start(f32[1,1296,128]{2,1,0:T(8,128)} %bitcast.477), channel_id=1, source_target_pairs={{8,0},{16,8},{24,16},{32,24},{40,32},{48,40},{56,48},{64,56},{72,6... | collective-permute-start | bytes 1990664 | tf_op jit(solution)/shard_map/ppermute | solution.py:23
  413.5 3.9 copy-start.6
  459.9 2.1 copy-start.11
  463.5 25.8 %collective-permute-start.8 = (f32[1,1296,128]{2,1,0:T(8,128)}, f32[1,1296,128]{2,1,0:T(8,128)}, u32[]{:S(2)}, u32[]{:S(2)}) collective-permute-start(f32[1,1296,128]{2,1,0:T(8,128)} %bitcast.468), channel_id=1, source_target_pairs={{0,8},{8,16},{16,24},{24,32},{32,40},{40,48},{48,56},{56,64},{64,7... | collective-permute-start | bytes 1990664 | tf_op jit(solution)/shard_map/ppermute | solution.py:21
  473.3 17.2 %collective-permute-start.9 = (f32[1,1296,128]{2,1,0:T(8,128)}, f32[1,1296,128]{2,1,0:T(8,128)S(1)}, u32[]{:S(2)}, u32[]{:S(2)}) collective-permute-start(f32[1,1296,128]{2,1,0:T(8,128)} %bitcast.471), channel_id=1, source_target_pairs={{8,0},{16,8},{24,16},{32,24},{40,32},{48,40},{56,48},{64,56},{72,6... | collective-permute-start | bytes 1990664 | tf_op jit(solution)/shard_map/ppermute | solution.py:23
  484.7 4.6 copy-start.29
  484.7 5.8 copy-start.28
  484.7 42.8 %all-to-all-start = ((bf16[8,1296,128]{2,1,0:T(8,128)(2,1)}), bf16[8,1296,128]{2,1,0:T(8,128)(2,1)}, u32[]{:S(2)}, u32[]{:S(2)}) async-start(bf16[8,1296,128]{2,1,0:T(8,128)(2,1)} %bitcast.123), calls=%async_computation | async-start | bytes 5308416 | tf_op jit(solution)/shard_map/all_to_all | solution.py:146
  569.2 84.9 %copy-start.1 = (bf16[10368,128]{1,0:T(8,128)(2,1)S(1)}, bf16[10368,128]{1,0:T(8,128)(2,1)}, u32[]{:S(2)}) copy-start(bf16[10368,128]{1,0:T(8,128)(2,1)} %param.7) | copy-start | bytes 7962628
  600.8 52.7 %all-to-all-start.3 = ((bf16[16,128,64]{1,2,0:T(8,128)(2,1)}), bf16[16,128,64]{1,2,0:T(8,128)(2,1)S(1)}, u32[]{:S(2)}, u32[]{:S(2)}) async-start(bf16[16,128,64]{1,2,0:T(8,128)(2,1)} %bitcast.159), calls=%async_computation.3 | async-start | bytes 524288 | tf_op jit(solution)/shard_map/all_to_all | solution.py:38
  (13 other events, 19.0 us)
where the time goes:
time: 667 us; the launch traced here: 654 us
  local copies, waits for them, and re-layouts  373 us (56%)
  other arithmetic  110 us (16%)
  blocking collectives  65.1 us (10%)
  starting transfers between devices  52.2 us (8%)
  matrix products  32.2 us (5%)
  waiting for transfers between devices  18.2 us (3%)
    gather x1, local copies, waits for them, and re-layouts, local(): potential_plane = potential[ordered]  53.6 us
    convert_element_type x5, other arithmetic, settle(): return lax.optimization_barrier(values.astype(jnp.bfloat16))  47.7 us
    scatter x1, local copies, waits for them, and re-layouts, local(): jnp.zeros((node_count,), jnp.int32).at[plain_index()]  47.3 us
    mul x5, local copies, waits for them, and re-layouts, apply_h(): products = products * cell_scale[:, None, None]  40.9 us
    scatter x1, local copies, waits for them, and re-layouts, local(): filtered = jnp.zeros_like(states).at[ordered].set(current)  40.9 us
    unnamed x104, local copies, waits for them, and re-layouts  36.4 us
    all_to_all x1, blocking collectives, local(): lax.all_to_all(weighted, 'band', split_axis=0, concat_axis=1, tiled=True)  36.4 us
    another operation x15, local copies, waits for them, and re-layouts, cut_cells(): return jnp.stack(pieces, axis=axis)  32.8 us
  transfers between devices with their start and end apart: 12, of which 4 were waited for; matrix products, arithmetic and copies ran while one was open for 30% of the time, Pallas kernels for 0%

commit v1 on v0

v1 whole, which is shorter than its diff:
```python
import functools

import jax
import jax.numpy as jnp
from jax import lax
from jax.experimental import pallas as pl
from jax.experimental.pallas import tpu as pltpu
from jax.sharding import PartitionSpec as P

EDGE = 8
SLAB_XY = 5
STEPS = 4
CELLS = SLAB_XY * SLAB_XY
PAIRS = (CELLS + 1) // 2
CELL_NODES = EDGE**3
SIDE = (EDGE - 1) * SLAB_XY + 1
FACE = SIDE * SIDE
NODES = FACE * EDGE
COLS = 128
QUAD = EDGE * EDGE
THIRDS = 3
THIRD = FACE // THIRDS
F32 = jnp.float32
BF16 = jnp.bfloat16
VMEM = pl.BlockSpec(memory_space=pltpu.VMEM)
SMEM = pl.BlockSpec(memory_space=pltpu.SMEM)
BIG = pltpu.CompilerParams(vmem_limit_bytes=24 * 1024 * 1024)


def first_row(cell_y, cell_x, j):
    return (((EDGE - 1) * cell_y + j) * SIDE + (EDGE - 1) * cell_x) * EDGE


def gather_kernel(states_ref, pot_ref, index_ref, matrix_ref, field_ref, pot_out_ref, mat_ref, face_mat_ref,
                  rhs_ref, hot_ref, column_ref):
    for cell_y in range(SLAB_XY):
        five = index_ref[cell_y * SLAB_XY : (cell_y + 1) * SLAB_XY, :].astype(F32)
        five = jnp.concatenate([five, jnp.zeros((EDGE - SLAB_XY, CELL_NODES), F32)], axis=0)
        column_ref[cell_y * CELL_NODES : (cell_y + 1) * CELL_NODES, :EDGE] = jnp.transpose(five)
    pot = jnp.transpose(pot_ref[...])
    high = pot.astype(BF16)
    rest = pot - high.astype(F32)
    mid = rest.astype(BF16)
    low = (rest - mid.astype(F32)).astype(BF16)
    rhs_ref[:, COLS:] = jnp.concatenate(
        [high, mid, low, jnp.zeros((FACE, COLS - 3 * EDGE), BF16)], axis=1)

    new = lax.broadcasted_iota(jnp.int32, (CELL_NODES, CELL_NODES), 0)
    old = lax.broadcasted_iota(jnp.int32, (CELL_NODES, CELL_NODES), 1)
    order = jnp.where(old == (new % EDGE) * QUAD + new // EDGE, 1.0, 0.0).astype(BF16)
    across = (((1,), (1,)), ((), ()))
    turned = lax.dot_general(matrix_ref[...], order, across, preferred_element_type=F32).astype(BF16)
    face_mat_ref[:QUAD, :] = turned[:QUAD, :]
    face_mat_ref[QUAD:, :] = turned[CELL_NODES - QUAD :, :]
    mat_ref[...] = jnp.dot(order, turned, preferred_element_type=F32).astype(BF16)

    def step(i, _):
        plane = i // SLAB_XY
        cell_y = i % SLAB_XY

        @pl.when(cell_y == 0)
        def _():
            rhs_ref[:, :COLS] = states_ref[pl.ds(pl.multiple_of(plane * FACE, 16), FACE), :]

        lanes = lax.broadcasted_iota(jnp.int32, (QUAD, FACE), 1).astype(F32)
        shift = (plane * FACE).astype(F32)
        for cell_x in range(SLAB_XY):
            want = column_ref[pl.ds(pl.multiple_of(cell_y * CELL_NODES + plane * QUAD, 8), QUAD), cell_x : cell_x + 1] - shift
            hot_ref[cell_x * QUAD : (cell_x + 1) * QUAD, :] = jnp.where(want == lanes, 1.0, 0.0).astype(BF16)
        got = jnp.dot(hot_ref[...], rhs_ref[...], preferred_element_type=F32)
        lane = lax.broadcasted_iota(jnp.int32, (EDGE, COLS), 1)
        mine = (lane % EDGE == plane) & (lane < 3 * EDGE)
        for cell_x in range(SLAB_XY):
            for j in range(EDGE):
                at = cell_x * QUAD + j * EDGE
                rows = pl.ds(first_row(cell_y, cell_x, j) + plane, EDGE, stride=EDGE)
                field_ref[rows, :] = got[at : at + EDGE, :COLS]
                value = jnp.sum(jnp.where(mine, got[at : at + EDGE, COLS:], 0.0), axis=1, keepdims=True)
                pot_out_ref[rows, :] = jnp.broadcast_to(value, (EDGE, COLS))
        return 0

    lax.fori_loop(0, EDGE * SLAB_XY, step, 0)


def gather(states, potential, connectivity, matrix):
    return pl.pallas_call(
        gather_kernel,
        name="gather_states",
        out_shape=(
            pltpu.VMEM((NODES, COLS), F32),
            pltpu.VMEM((NODES, COLS), F32),
            pltpu.VMEM((CELL_NODES, CELL_NODES), BF16),
            pltpu.VMEM((2 * QUAD, CELL_NODES), BF16),
        ),
        in_specs=[VMEM] * 4,
        out_specs=(VMEM,) * 4,
        scratch_shapes=[
            pltpu.VMEM((FACE, 2 * COLS), BF16),
            pltpu.VMEM((SLAB_XY * QUAD, FACE), BF16),
            pltpu.VMEM((SLAB_XY * CELL_NODES, COLS), F32),
        ],
        compiler_params=BIG,
    )(states, potential.reshape(EDGE, FACE), connectivity, matrix)


def half_width_of(bounds):
    low, high = bounds
    return jnp.full((1, COLS), (high[0] - low[0]) * 0.5, F32)


def factors(bounds, stage):
    if stage > STEPS:
        return jnp.ones((1, COLS), F32), None
    low, high = bounds
    center = (high[0] + low[0]) * 0.5
    lead = (1.0 if stage == 1 else 2.0) / half_width_of(bounds)
    return lead, lead * center


def pair_cells(pair, scale_ref):
    for half in range(2):
        index = 2 * pair + half
        cell = jnp.minimum(index, CELLS - 1)
        yield half, cell // SLAB_XY, cell % SLAB_XY, jnp.where(index < CELLS, scale_ref[cell], 0.0)


def faces_kernel(stage, settle, emit, spread, *refs):
    refs = list(refs)
    field_ref = refs.pop(0)
    if settle:
        low_in, high_in = refs.pop(0), refs.pop(0)
    bounds = (refs.pop(0), refs.pop(0))
    weight_ref = refs.pop(0)
    if spread:
        face_mat_ref, scale_ref = refs.pop(0), refs.pop(0)
    if settle:
        out_ref = refs.pop(0)
    if emit:
        plain_ref = refs.pop(0)
    if spread:
        low_out, high_out, blocks_ref, sums_ref = refs
    if settle:
        lead, _ = factors(bounds, stage)

        def settle_rows(i, _):
            for side, (face_in, plane) in enumerate(((low_in, 0), (high_in, EDGE - 1))):
                got = face_in[pl.ds(pl.multiple_of(i * 16, 16), 16), :].astype(F32)
                for part in range(2):
                    rows = pl.ds((i * 2 + part) * QUAD + plane, EDGE, stride=EDGE)
                    value = field_ref[rows, :] + lead * got[part * EDGE : (part + 1) * EDGE, :]
                    value = value.astype(BF16).astype(F32)
                    if stage > STEPS:
                        value = value * weight_ref[side]
                    out_ref[rows, :] = value
            return 0

        lax.fori_loop(0, FACE // 16, settle_rows, 0)
        field_ref = out_ref
    if emit:

        def emit_rows(i, _):
            rows = pl.ds(pl.multiple_of(i * 128, 128), 128)
            plain_ref[rows, :] = field_ref[rows, :].astype(BF16)
            return 0

        lax.fori_loop(0, NODES // 128, emit_rows, 0)
    if spread:
        sums_ref[...] = jnp.zeros_like(sums_ref)

        def step(pair, _):
            for half, cell_y, cell_x, scale in pair_cells(pair, scale_ref):
                for j in range(EDGE):
                    rows = pl.ds(pl.multiple_of(first_row(cell_y, cell_x, j), EDGE), QUAD)
                    blocks_ref[pair, j * QUAD : (j + 1) * QUAD, half * COLS : (half + 1) * COLS] = (
                        field_ref[rows, :].astype(BF16))
            product = jnp.dot(face_mat_ref[...], blocks_ref[pair], preferred_element_type=F32)
            for half, cell_y, cell_x, scale in pair_cells(pair, scale_ref):
                for side in range(2):
                    for j in range(EDGE):
                        at = side * QUAD + j * EDGE
                        rows = pl.ds(side * FACE + ((EDGE - 1) * cell_y + j) * SIDE + (EDGE - 1) * cell_x, EDGE)
                        sums_ref[rows, :] += scale * product[at : at + EDGE, half * COLS : (half + 1) * COLS]
            return 0

        lax.fori_loop(0, PAIRS, step, 0)
        low_out[...] = sums_ref[:FACE, :].astype(BF16)
        high_out[...] = sums_ref[FACE:, :].astype(BF16)


def faces(stage, field, got, bounds, weight, face_mat, scale, emit=False, spread=True):
    settle = got is not None
    args, specs, outs = [field], [VMEM], []
    if settle:
        args += list(got)
        specs += [VMEM] * 2
        outs.append(pltpu.VMEM((NODES, COLS), F32))
    args += [*bounds, weight]
    specs += [SMEM] * 3
    if spread:
        args += [face_mat, scale]
        specs += [VMEM, SMEM]
    if emit:
        outs.append(jax.ShapeDtypeStruct((NODES, COLS), BF16))
    if spread:
        outs += [jax.ShapeDtypeStruct((FACE, COLS), BF16)] * 2
        outs.append(pltpu.VMEM((PAIRS, CELL_NODES, 2 * COLS), BF16))
    return pl.pallas_call(
        functools.partial(faces_kernel, stage, settle, emit, spread),
        name="faces",
        out_shape=tuple(outs),
        in_specs=specs,
        out_specs=(VMEM,) * len(outs),
        scratch_shapes=[pltpu.VMEM((2 * FACE, COLS), F32)] if spread else [],
        input_output_aliases={0: 0} if settle else {},
        compiler_params=BIG,
    )(*args)


def cells_kernel(stage, blocks_ref, field_ref, *refs):
    refs = list(refs)
    prev_ref = refs.pop(0) if 1 < stage <= STEPS else None
    pot_ref, mat_ref, low_ref, high_ref, scale_ref, out_ref = refs
    out_ref[...] = jnp.zeros_like(out_ref)

    def step(pair, _):
        product = jnp.dot(mat_ref[...], blocks_ref[pair], preferred_element_type=F32)
        for half, cell_y, cell_x, scale in pair_cells(pair, scale_ref):
            for j in range(EDGE):
                rows = pl.ds(pl.multiple_of(first_row(cell_y, cell_x, j), EDGE), QUAD)
                out_ref[rows, :] += scale * product[j * QUAD : (j + 1) * QUAD, half * COLS : (half + 1) * COLS]
        return 0

    lax.fori_loop(0, PAIRS, step, 0)
    lead, shift = factors((low_ref, high_ref), stage)
    plane = lax.broadcasted_iota(jnp.int32, (QUAD, COLS), 0) % EDGE
    inside = (plane > 0) & (plane < EDGE - 1)

    def finish(i, _):
        rows = pl.ds(pl.multiple_of(i * QUAD, QUAD), QUAD)
        field = field_ref[rows, :]
        value = out_ref[rows, :] + pot_ref[rows, :] * field
        if stage <= STEPS:
            value = lead * value - shift * field
        if prev_ref is not None:
            value = value - prev_ref[rows, :]
        out_ref[rows, :] = jnp.where(inside, value.astype(BF16).astype(F32), value)
        return 0

    lax.fori_loop(0, NODES // QUAD, finish, 0)


def cells(stage, blocks, field, prev, pot, mat, bounds, scale):
    args = [blocks, field] + ([prev] if 1 < stage <= STEPS else []) + [pot, mat]
    specs = [VMEM] * len(args) + [SMEM] * 3
    return pl.pallas_call(
        functools.partial(cells_kernel, stage),
        name="cells",
        out_shape=pltpu.VMEM((NODES, COLS), F32),
        in_specs=specs,
        out_specs=VMEM,
        compiler_params=BIG,
    )(*args, *bounds, scale)


def return_kernel(field_ref, index_ref, out_ref, hot_ref, rhs_ref):
    j = lax.broadcasted_iota(jnp.int32, (EDGE, COLS), 0)

    def step(plane, _):
        for cell in range(CELLS):
            cell_y, cell_x = cell // SLAB_XY, cell % SLAB_XY
            for k in range(EDGE):
                at = cell * QUAD + k * EDGE
                value = field_ref[pl.ds(first_row(cell_y, cell_x, k) + plane, EDGE, stride=EDGE), :]
                if cell_y > 0 and k == 0:
                    value = jnp.zeros_like(value)
                elif cell_x > 0:
                    value = jnp.where(j == 0, 0.0, value)
                rhs_ref[at : at + EDGE, :] = value
        want = index_ref[pl.ds(plane, 1), :].astype(F32) - (plane * FACE).astype(F32)
        rhs = rhs_ref[...].astype(BF16)
        for part in range(THIRDS):
            row = lax.broadcasted_iota(jnp.int32, (THIRD, CELLS * QUAD), 0).astype(F32) + float(part * THIRD)
            hot_ref[...] = jnp.where(want == row, 1.0, 0.0).astype(BF16)
            got = jnp.dot(hot_ref[...], rhs, preferred_element_type=F32)
            start = pl.multiple_of(plane * FACE + part * THIRD, 16)
            out_ref[pl.ds(start, THIRD), :] = got.astype(BF16)
        return 0

    lax.fori_loop(0, EDGE, step, 0)


def hand_back(field, connectivity):
    index = connectivity.reshape(CELLS, EDGE, QUAD).transpose(1, 0, 2).reshape(EDGE, CELLS * QUAD)
    return pl.pallas_call(
        return_kernel,
        name="hand_back",
        out_shape=jax.ShapeDtypeStruct((NODES, COLS), BF16),
        in_specs=[VMEM] * 2,
        out_specs=VMEM,
        scratch_shapes=[
            pltpu.VMEM((THIRD, CELLS * QUAD), BF16),
            pltpu.VMEM((CELLS * QUAD, COLS), F32),
        ],
        compiler_params=BIG,
    )(field, index)


def in_blocks(x, dim, peers):
    dims = x.shape
    blocks = x.reshape(*dims[:dim], peers, dims[dim] // peers, *dims[dim + 1 :])
    return jnp.moveaxis(blocks, dim, 0)


def summed_on_arrival(x, axis, dim):
    blocks = in_blocks(x, dim, lax.axis_size(axis))
    arrived = lax.all_to_all(blocks, axis, split_axis=0, concat_axis=0, tiled=True)
    return arrived.astype(F32).sum(axis=0)


def swap_faces(low, high):
    count = lax.axis_size("space")
    from_below = lax.ppermute(high, "space", [(i, i + 1) for i in range(count - 1)])
    from_above = lax.ppermute(low, "space", [(i + 1, i) for i in range(count - 1)])
    return from_below, from_above


def local(states, potential, cell_matrix, cell_scale, connectivity, lower_bound, upper_bound):
    bounds = (lower_bound, upper_bound)
    position = lax.axis_index("space")
    count = lax.axis_size("space")
    weight = jnp.stack([
        jnp.where(position > 0, 0.5, 1.0).astype(F32),
        jnp.where(position < count - 1, 0.5, 1.0).astype(F32),
    ])
    field, pot, mat, face_mat = gather(states, potential, connectivity, cell_matrix)
    low, high, blocks = faces(0, field, None, bounds, weight, face_mat, cell_scale)
    prev = None
    for stage in range(1, STEPS + 2):
        got = swap_faces(low, high)
        part = cells(stage, blocks, field, prev, pot, mat, bounds, cell_scale)
        prev = field
        if stage < STEPS:
            field, low, high, blocks = faces(stage, part, got, bounds, weight, face_mat, cell_scale)
        elif stage == STEPS:
            field, current, low, high, blocks = faces(
                stage, part, got, bounds, weight, face_mat, cell_scale, emit=True)
        else:
            _, weighted = faces(stage, part, got, bounds, weight, None, None, emit=True, spread=False)
    node_states = lax.all_to_all(current, "band", split_axis=0, concat_axis=1, tiled=True)
    node_images = lax.all_to_all(weighted, "band", split_axis=0, concat_axis=1, tiled=True)
    partial_matrix = lax.dot_general(
        node_states, node_images, (((0,), (0,)), ((), ())), preferred_element_type=F32)
    row_sums = summed_on_arrival(partial_matrix.astype(BF16), "band", 0)
    totals = summed_on_arrival(row_sums.astype(BF16), "space", 1)
    filtered = hand_back(field, connectivity)
    global_count = FACE * ((EDGE - 1) * count + 1)
    return filtered, totals / global_count


def solution(mesh):
    placed = (P("space", "band"), P("space"), P(), P("space"), P("space", None), P(), P())
    return jax.shard_map(
        local,
        mesh=mesh,
        in_specs=placed,
        out_specs=(P("space", "band"), P("band", "space")),
        check_vma=False,
    )
```

time: 667 us -> 277 us (0.42); the launches traced: 654 us -> 276 us
  local copies, waits for them, and re-layouts: 373 us -> 24 us
  Pallas kernels: 0 us -> 110 us
  other arithmetic: 110 us -> 1.1 us
  matrix products: 32.2 us -> 5.41 us
  blocking collectives: 65.1 us -> 58.3 us
    pallas_call x0 -> x13, Pallas kernels: none -> 110 us  [the longest x5 37.9 us: cells(): pl.pallas_call(functools.partial(cells_kernel, stage), name='cells', out_...]
    scatter x2 -> x0, local copies, waits for them, and re-layouts: 88.2 us -> none  [the longest x1 47.3 us: local(): jnp.zeros((node_count,), jnp.int32).at[plain_index()]]
    gather x2 -> x0, local copies, waits for them, and re-layouts: 75.5 us -> none  [the longest x1 53.6 us: local(): potential_plane = potential[ordered]]
    another operation x25 -> x0, local copies, waits for them, and re-layouts: 57.9 us -> none  [the longest x15 32.8 us: cut_cells(): return jnp.stack(pieces, axis=axis)]
    convert_element_type x6 -> x0, other arithmetic: 48.1 us -> none  [the longest x5 47.7 us: settle(): return lax.optimization_barrier(values.astype(jnp.bfloat16))]
    slice x17 -> x0, local copies, waits for them, and re-layouts: 44.4 us -> none  [the longest x5 23.9 us: apply_h(): assembled[face_size:node_count - face_size]]
    add x23 -> x0, other arithmetic: 43 us -> none  [the longest x10 29.9 us: fold_cells(): total = padded if total is None else total + padded]
    mul x5 -> x0, local copies, waits for them, and re-layouts: 40.9 us -> none  [apply_h(): products = products * cell_scale[:, None, None]]
  transfers between devices with their start and end apart: 12 -> 12, of which waited for: 4 -> 5; matrix products, arithmetic and copies ran while one was open for 30% -> 0% of each run, Pallas kernels for 0% -> 20%
where the time goes in v1:
time: 277 us; the launch traced here: 276 us
  Pallas kernels  110 us (40%)
  blocking collectives  58.3 us (21%)
  starting transfers between devices  58 us (21%)
  local copies, waits for them, and re-layouts  24 us (9%)
  waiting for transfers between devices  16.5 us (6%)
  matrix products  5.41 us (2%)
    pallas_call x5, Pallas kernels, cells(): pl.pallas_call(functools.partial(cells_kernel, stage), name='cells', out_...  37.9 us
    pallas_call x6, Pallas kernels, faces(): pl.pallas_call(functools.partial(faces_kernel, stage, settle, emit, sprea...  34.8 us
    all_to_all x1, blocking collectives, local(): lax.all_to_all(weighted, 'band', split_axis=0, concat_axis=1, tiled=True)  32.5 us
    ppermute x5, starting transfers between devices, swap_faces(): lax.ppermute(high, 'space', [(i, i + 1) for i in range(count - 1)])  27.4 us
    all_to_all x1, blocking collectives, summed_on_arrival(): lax.all_to_all(blocks, axis, split_axis=0, concat_axis=0, tiled=True)  25.7 us
    pallas_call x1, Pallas kernels, gather(): pl.pallas_call(gather_kernel, name='gather_states', out_shape=(pltpu.VMEM...  23.3 us
    unnamed x28, local copies, waits for them, and re-layouts  22.1 us
    all_to_all x1, starting transfers between devices, summed_on_arrival(): lax.all_to_all(blocks, axis, split_axis=0, concat_axis=0, tiled=True)  16.6 us
  transfers between devices with their start and end apart: 12, of which 5 were waited for; matrix products, arithmetic and copies ran while one was open for 0% of the time, Pallas kernels for 20%

profile of v1, /device:TPU:1, one launch (start us, length us, event | category | flops | bytes accessed | tf_op | source)
XLA Modules:
  0.0 275.8 jit_solution(6407030353284404073)
XLA Ops:
  6.5 23.3 %gather_states.1 = (f32[10368,128]{1,0:T(8,128)S(1)}, f32[10368,128]{1,0:T(8,128)S(1)}, bf16[512,512]{1,0:T(8,128)(2,1)S(1)}, bf16[128,512]{1,0:T(8,128)(2,1)S(1)}) custom-call(bf16[10368,128]{1,0:T(8,128)(2,1)S(1)} %copy-done.9, f32[8,1296]{1,0:T(8,128)S(1)} %reshape.25.pot_ref, s32[25,512]{1,0:T(8,128)S(1)} %copy-done.11, bf16[512,512]{1,0:T(8,128)(2,1)S(1)} %copy-done.10), custom_call_target="tpu_custom_call" | custom-call | tf_op jit(solution)/shard_map/gather_states/pallas_call | solution.py:86
  29.9 3.8 %faces.6 = (bf16[1296,128]{1,0:T(8,128)(2,1)S(1)}, bf16[1296,128]{1,0:T(8,128)(2,1)S(1)}, bf16[13,512,256]{2,1,0:T(8,128)(2,1)S(1)}) custom-call(f32[10368,128]{1,0:T(8,128)S(1)} %get-tuple-element.27.refs_0_.field_ref, f32[1]{0:T(128)S(6)} %copy.43.refs_1_.refs_2_.refs_3_, f32[1]{0:T(128)S(6)} %copy.44.refs_2_.refs_3_.refs_4_, ...), custom_call_target="tpu_custom_call" | custom-call | tf_op jit(solution)/shard_map/faces/pallas_call | solution.py:207
  33.6 6.9 %collective-permute-start = (bf16[1296,128]{1,0:T(8,128)(2,1)S(1)}, bf16[1296,128]{1,0:T(8,128)(2,1)S(1)}, u32[]{:S(2)}, u32[]{:S(2)}) collective-permute-start(bf16[1296,128]{1,0:T(8,128)(2,1)S(1)} %get-tuple-element.32), channel_id=1, source_target_pairs={{0,8},{8,16},{16,24},{24,32},{32,40},{40,48},{48,56},{56,64},{64,7... | collective-permute-start | bytes 995336 | tf_op jit(solution)/shard_map/ppermute | solution.py:322
  42.4 7.5 %cells.5.refs_0_ = f32[10368,128]{1,0:T(8,128)S(1)} custom-call(bf16[13,512,256]{2,1,0:T(8,128)(2,1)S(1)} %get-tuple-element.29.blocks_ref, f32[10368,128]{1,0:T(8,128)S(1)} %get-tuple-element.27.refs_0_.field_ref, f32[10368,128]{1,0:T(8,128)S(1)} %get-tuple-element.30.refs_0_.refs_1_, bf16[512,512]{1,0:T(8,128)(2,1)S(1)} %get-tuple-element.31.refs_1_.refs_2_, ...), custom_call_target="tpu_custom_call" | custom-call | tf_op jit(solution)/shard_map/cells/pallas_call | solution.py:255
  50.5 6.6 %faces.7 = (f32[10368,128]{1,0:T(8,128)S(1)}, bf16[1296,128]{1,0:T(8,128)(2,1)S(1)}, bf16[1296,128]{1,0:T(8,128)(2,1)S(1)}, bf16[13,512,256]{2,1,0:T(8,128)(2,1)S(1)}) custom-call(f32[10368,128]{1,0:T(8,128)S(1)} %cells.5.refs_0_, bf16[1296,128]{1,0:T(8,128)(2,1)S(1)} %collective-permute-done.refs_1_, ...), custom_call_target="tpu_custom_call", output_to_operand_aliasing={{0}: (0, {})} | custom-call | tf_op jit(solution)/shard_map/faces/pallas_call | solution.py:207
  57.1 4.7 %collective-permute-start.2 = (bf16[1296,128]{1,0:T(8,128)(2,1)S(1)}, bf16[1296,128]{1,0:T(8,128)(2,1)S(1)}, u32[]{:S(2)}, u32[]{:S(2)}) collective-permute-start(bf16[1296,128]{1,0:T(8,128)(2,1)S(1)} %get-tuple-element.36), channel_id=1, source_target_pairs={{0,8},{8,16},{16,24},{24,32},{32,40},{40,48},{48,56},{56,64},{64,7... | collective-permute-start | bytes 995336 | tf_op jit(solution)/shard_map/ppermute | solution.py:322
  63.7 7.7 %cells.6.refs_0_ = f32[10368,128]{1,0:T(8,128)S(1)} custom-call(bf16[13,512,256]{2,1,0:T(8,128)(2,1)S(1)} %get-tuple-element.34.blocks_ref, f32[10368,128]{1,0:T(8,128)S(1)} %get-tuple-element.35.field_ref.refs_0_, f32[10368,128]{1,0:T(8,128)S(1)} %get-tuple-element.27.refs_0_.field_ref, f32[10368,128]{1,0:T(8,128)S(1)} %get-tuple-element.30.refs_0_.refs_1_, ...), custom_call_target="tpu_custom_call" | custom-call | tf_op jit(solution)/shard_map/cells/pallas_call | solution.py:255
  71.7 6.7 %faces.8 = (f32[10368,128]{1,0:T(8,128)S(1)}, bf16[1296,128]{1,0:T(8,128)(2,1)S(1)}, bf16[1296,128]{1,0:T(8,128)(2,1)S(1)}, bf16[13,512,256]{2,1,0:T(8,128)(2,1)S(1)}) custom-call(f32[10368,128]{1,0:T(8,128)S(1)} %cells.6.refs_0_, bf16[1296,128]{1,0:T(8,128)(2,1)S(1)} %collective-permute-done.2.refs_1_, ...), custom_call_target="tpu_custom_call", output_to_operand_aliasing={{0}: (0, {})} | custom-call | tf_op jit(solution)/shard_map/faces/pallas_call | solution.py:207
  78.4 4.9 %collective-permute-start.4 = (bf16[1296,128]{1,0:T(8,128)(2,1)S(1)}, bf16[1296,128]{1,0:T(8,128)(2,1)S(1)}, u32[]{:S(2)}, u32[]{:S(2)}) collective-permute-start(bf16[1296,128]{1,0:T(8,128)(2,1)S(1)} %get-tuple-element.40), channel_id=1, source_target_pairs={{0,8},{8,16},{16,24},{24,32},{32,40},{40,48},{48,56},{56,64},{64,7... | collective-permute-start | bytes 995336 | tf_op jit(solution)/shard_map/ppermute | solution.py:322
  85.2 7.8 %cells.7.refs_0_ = f32[10368,128]{1,0:T(8,128)S(1)} custom-call(bf16[13,512,256]{2,1,0:T(8,128)(2,1)S(1)} %get-tuple-element.38.blocks_ref, f32[10368,128]{1,0:T(8,128)S(1)} %get-tuple-element.39.field_ref.refs_0_, f32[10368,128]{1,0:T(8,128)S(1)} %get-tuple-element.35.field_ref.refs_0_, f32[10368,128]{1,0:T(8,128)S(1)} %get-tuple-element.30.refs_0_.refs_1_, ...), custom_call_target="tpu_custom_call" | custom-call | tf_op jit(solution)/shard_map/cells/pallas_call | solution.py:255
  93.2 6.6 %faces.9 = (f32[10368,128]{1,0:T(8,128)S(1)}, bf16[1296,128]{1,0:T(8,128)(2,1)S(1)}, bf16[1296,128]{1,0:T(8,128)(2,1)S(1)}, bf16[13,512,256]{2,1,0:T(8,128)(2,1)S(1)}) custom-call(f32[10368,128]{1,0:T(8,128)S(1)} %cells.7.refs_0_, bf16[1296,128]{1,0:T(8,128)(2,1)S(1)} %collective-permute-done.4.refs_1_, ...), custom_call_target="tpu_custom_call", output_to_operand_aliasing={{0}: (0, {})} | custom-call | tf_op jit(solution)/shard_map/faces/pallas_call | solution.py:207
  99.9 2.3 copy-done.5
  102.2 4.9 %collective-permute-start.6 = (bf16[1296,128]{1,0:T(8,128)(2,1)S(1)}, bf16[1296,128]{1,0:T(8,128)(2,1)S(1)}, u32[]{:S(2)}, u32[]{:S(2)}) collective-permute-start(bf16[1296,128]{1,0:T(8,128)(2,1)S(1)} %get-tuple-element.44), channel_id=1, source_target_pairs={{0,8},{8,16},{16,24},{24,32},{32,40},{40,48},{48,56},{56,64},{64,7... | collective-permute-start | bytes 995336 | tf_op jit(solution)/shard_map/ppermute | solution.py:322
  109.1 2.5 copy-done.6
  111.6 7.7 %cells.8.refs_0_ = f32[10368,128]{1,0:T(8,128)S(1)} custom-call(bf16[13,512,256]{2,1,0:T(8,128)(2,1)S(1)} %get-tuple-element.42.blocks_ref, f32[10368,128]{1,0:T(8,128)S(1)} %copy-done.6, f32[10368,128]{1,0:T(8,128)S(1)} %get-tuple-element.39.field_ref.refs_0_, f32[10368,128]{1,0:T(8,128)S(1)} %get-tuple-element.30.refs_0_.refs_1_, ...), custom_call_target="tpu_custom_call" | custom-call | tf_op jit(solution)/shard_map/cells/pallas_call | solution.py:255
  119.4 7.7 %faces.10 = (f32[10368,128]{1,0:T(8,128)S(1)}, bf16[10368,128]{1,0:T(8,128)(2,1)}, bf16[1296,128]{1,0:T(8,128)(2,1)S(1)}, bf16[1296,128]{1,0:T(8,128)(2,1)S(1)}, bf16[13,512,256]{2,1,0:T(8,128)(2,1)S(1)}) custom-call(f32[10368,128]{1,0:T(8,128)S(1)} %cells.8.refs_0_, ...), custom_call_target="tpu_custom_call", output_to_operand_aliasing={{0}: (0, {})} | custom-call | tf_op jit(solution)/shard_map/faces/pallas_call | solution.py:207
  127.1 2.3 copy-done.2
  131.3 4.5 %all-to-all-start = ((bf16[8,1296,128]{2,1,0:T(8,128)(2,1)}), bf16[8,1296,128]{2,1,0:T(8,128)(2,1)}, u32[]{:S(2)}, u32[]{:S(2)}) async-start(bf16[8,1296,128]{2,1,0:T(8,128)(2,1)} %bitcast.3), calls=%async_computation | async-start | bytes 5308416 | tf_op jit(solution)/shard_map/all_to_all | solution.py:349
  135.8 6.0 %collective-permute-start.8 = (bf16[1296,128]{1,0:T(8,128)(2,1)S(1)}, bf16[1296,128]{1,0:T(8,128)(2,1)S(1)}, u32[]{:S(2)}, u32[]{:S(2)}) collective-permute-start(bf16[1296,128]{1,0:T(8,128)(2,1)S(1)} %get-tuple-element.49), channel_id=1, source_target_pairs={{0,8},{8,16},{16,24},{24,32},{32,40},{40,48},{48,56},{56,64},{64,7... | collective-permute-start | bytes 995336 | tf_op jit(solution)/shard_map/ppermute | solution.py:322
  143.7 2.5 copy-done.1
  146.2 2.5 copy-done.3
  148.7 2.0 copy-done.8
  150.7 7.1 %cells.9.refs_0_ = f32[10368,128]{1,0:T(8,128)S(1)} custom-call(bf16[13,512,256]{2,1,0:T(8,128)(2,1)S(1)} %copy-done.8, f32[10368,128]{1,0:T(8,128)S(1)} %copy-done.3, f32[10368,128]{1,0:T(8,128)S(1)} %copy-done.1, bf16[512,512]{1,0:T(8,128)(2,1)S(1)} %get-tuple-element.31.refs_1_.refs_2_, f32[1]{0:T(128)S(6)} %copy.43.refs_1_.refs_2_.refs_3_, ...), custom_call_target="tpu_custom_call" | custom-call | tf_op jit(solution)/shard_map/cells/pallas_call | solution.py:255
  157.8 11.5 %collective-permute-done.8.refs_1_ = bf16[1296,128]{1,0:T(8,128)(2,1)S(1)} collective-permute-done((bf16[1296,128]{1,0:T(8,128)(2,1)S(1)}, bf16[1296,128]{1,0:T(8,128)(2,1)S(1)}, u32[]{:S(2)}, u32[]{:S(2)}) %collective-permute-start.8) | collective-permute-done | bytes 331808 | tf_op jit(solution)/shard_map/ppermute | solution.py:322
  169.4 3.9 %collective-permute-done.9.refs_2_ = bf16[1296,128]{1,0:T(8,128)(2,1)S(1)} collective-permute-done((bf16[1296,128]{1,0:T(8,128)(2,1)S(1)}, bf16[1296,128]{1,0:T(8,128)(2,1)S(1)}, u32[]{:S(2)}, u32[]{:S(2)}) %collective-permute-start.9) | collective-permute-done | bytes 331808 | tf_op jit(solution)/shard_map/ppermute | solution.py:323
  173.3 3.3 %faces.11 = (f32[10368,128]{1,0:T(8,128)S(1)}, bf16[10368,128]{1,0:T(8,128)(2,1)S(1)}) custom-call(f32[10368,128]{1,0:T(8,128)S(1)} %cells.9.refs_0_, bf16[1296,128]{1,0:T(8,128)(2,1)S(1)} %collective-permute-done.8.refs_1_, bf16[1296,128]{1,0:T(8,128)(2,1)S(1)} %collective-permute-done.9.refs_2_, ...), custom_call_target="tpu_custom_call", output_to_operand_aliasing={{0}: (0, {})} | custom-call | tf_op jit(solution)/shard_map/faces/pallas_call | solution.py:207
  176.7 32.5 %all_to_all.48 = bf16[8,1296,128]{2,1,0:T(8,128)(2,1)S(1)} all-to-all(bf16[8,1296,128]{2,1,0:T(8,128)(2,1)S(1)} %bitcast.31), channel_id=1, replica_groups=mesh['space'=16,'band'=8] {'band'}, dimensions={0} | all-to-all | bytes 5308416 | tf_op jit(solution)/shard_map/all_to_all | solution.py:350
  209.2 5.4 %fusion.5 = bf16[1024,1024]{1,0:T(8,128)(2,1)S(1)} fusion(bf16[8,1296,128]{2,1,0:T(8,128)(2,1)S(1)} %all_to_all.48, bf16[8,1296,128]{2,1,0:T(8,128)(2,1)} %all-to-all-done), kind=kOutput, calls=%fused_computation.5 | convolution fusion | flops 2718957568 | bytes 7405568 | tf_op jit(solution)/shard_map/dot_general | solution.py:351
  214.6 25.7 %all_to_all.49 = bf16[8,128,1024]{2,1,0:T(8,128)(2,1)S(1)} all-to-all(bf16[8,128,1024]{2,1,0:T(8,128)(2,1)S(1)} %bitcast.32), channel_id=1, replica_groups=mesh['space'=16,'band'=8] {'band'}, dimensions={0} | all-to-all | bytes 4194304 | tf_op jit(solution)/shard_map/all_to_all | solution.py:316
  241.6 16.6 %all-to-all-start.3 = ((bf16[16,128,64]{1,2,0:T(8,128)(2,1)}), bf16[16,128,64]{1,2,0:T(8,128)(2,1)S(1)}, u32[]{:S(2)}, u32[]{:S(2)}) async-start(bf16[16,128,64]{1,2,0:T(8,128)(2,1)} %bitcast.9), calls=%async_computation.3 | async-start | bytes 524288 | tf_op jit(solution)/shard_map/all_to_all | solution.py:316
  258.4 2.5 copy-done.4
  260.9 14.2 %hand_back.1 = bf16[10368,128]{1,0:T(8,128)(2,1)} custom-call(f32[10368,128]{1,0:T(8,128)S(1)} %copy-done.4, s32[8,1600]{1,0:T(8,128)S(1)} %reshape.27.index_ref), custom_call_target="tpu_custom_call" | custom-call | tf_op jit(solution)/shard_map/hand_back/pallas_call | solution.py:294
  (45 shorter events, 19.1 us)
Async XLA Ops:
  0.6 29.2 %copy-start.13 = (f32[25]{0:T(128)S(1)}, f32[25]{0:T(128)}, u32[]{:S(2)}) copy-start(f32[25]{0:T(128)} %refs_4_.11) | copy-start | bytes 304
  2.9 1.8 copy-start.9
  4.7 1.0 copy-start.10
  5.7 0.8 copy-start.11
  29.8 79.2 %copy-start = (f32[10368,128]{1,0:T(8,128)}, f32[10368,128]{1,0:T(8,128)S(1)}, u32[]{:S(2)}) copy-start(f32[10368,128]{1,0:T(8,128)S(1)} %get-tuple-element.30.refs_0_.refs_1_) | copy-start | bytes 15925252
  33.6 16.3 %collective-permute-start = (bf16[1296,128]{1,0:T(8,128)(2,1)S(1)}, bf16[1296,128]{1,0:T(8,128)(2,1)S(1)}, u32[]{:S(2)}, u32[]{:S(2)}) collective-permute-start(bf16[1296,128]{1,0:T(8,128)(2,1)S(1)} %get-tuple-element.32), channel_id=1, source_target_pairs={{0,8},{8,16},{16,24},{24,32},{32,40},{40,48},{48,56},{56,64},{64,7... | collective-permute-start | bytes 995336 | tf_op jit(solution)/shard_map/ppermute | solution.py:322
  40.5 9.9 %collective-permute-start.1 = (bf16[1296,128]{1,0:T(8,128)(2,1)S(1)}, bf16[1296,128]{1,0:T(8,128)(2,1)S(1)}, u32[]{:S(2)}, u32[]{:S(2)}) collective-permute-start(bf16[1296,128]{1,0:T(8,128)(2,1)S(1)} %get-tuple-element.33), channel_id=1, source_target_pairs={{8,0},{16,8},{24,16},{32,24},{40,32},{48,40},{56,48},{64,56},{72,6... | collective-permute-start | bytes 995336 | tf_op jit(solution)/shard_map/ppermute | solution.py:323
  57.1 14.4 %collective-permute-start.2 = (bf16[1296,128]{1,0:T(8,128)(2,1)S(1)}, bf16[1296,128]{1,0:T(8,128)(2,1)S(1)}, u32[]{:S(2)}, u32[]{:S(2)}) collective-permute-start(bf16[1296,128]{1,0:T(8,128)(2,1)S(1)} %get-tuple-element.36), channel_id=1, source_target_pairs={{0,8},{8,16},{16,24},{24,32},{32,40},{40,48},{48,56},{56,64},{64,7... | collective-permute-start | bytes 995336 | tf_op jit(solution)/shard_map/ppermute | solution.py:322
  61.8 9.9 %collective-permute-start.3 = (bf16[1296,128]{1,0:T(8,128)(2,1)S(1)}, bf16[1296,128]{1,0:T(8,128)(2,1)S(1)}, u32[]{:S(2)}, u32[]{:S(2)}) collective-permute-start(bf16[1296,128]{1,0:T(8,128)(2,1)S(1)} %get-tuple-element.37), channel_id=1, source_target_pairs={{8,0},{16,8},{24,16},{32,24},{40,32},{48,40},{56,48},{64,56},{72,6... | collective-permute-start | bytes 995336 | tf_op jit(solution)/shard_map/ppermute | solution.py:323
  78.4 14.6 %collective-permute-start.4 = (bf16[1296,128]{1,0:T(8,128)(2,1)S(1)}, bf16[1296,128]{1,0:T(8,128)(2,1)S(1)}, u32[]{:S(2)}, u32[]{:S(2)}) collective-permute-start(bf16[1296,128]{1,0:T(8,128)(2,1)S(1)} %get-tuple-element.40), channel_id=1, source_target_pairs={{0,8},{8,16},{16,24},{24,32},{32,40},{40,48},{48,56},{56,64},{64,7... | collective-permute-start | bytes 995336 | tf_op jit(solution)/shard_map/ppermute | solution.py:322
  83.3 9.9 %collective-permute-start.5 = (bf16[1296,128]{1,0:T(8,128)(2,1)S(1)}, bf16[1296,128]{1,0:T(8,128)(2,1)S(1)}, u32[]{:S(2)}, u32[]{:S(2)}) collective-permute-start(bf16[1296,128]{1,0:T(8,128)(2,1)S(1)} %get-tuple-element.41), channel_id=1, source_target_pairs={{8,0},{16,8},{24,16},{32,24},{40,32},{48,40},{56,48},{64,56},{72,6... | collective-permute-start | bytes 995336 | tf_op jit(solution)/shard_map/ppermute | solution.py:323
  99.9 2.4 copy-start.5
  102.2 17.1 %collective-permute-start.6 = (bf16[1296,128]{1,0:T(8,128)(2,1)S(1)}, bf16[1296,128]{1,0:T(8,128)(2,1)S(1)}, u32[]{:S(2)}, u32[]{:S(2)}) collective-permute-start(bf16[1296,128]{1,0:T(8,128)(2,1)S(1)} %get-tuple-element.44), channel_id=1, source_target_pairs={{0,8},{8,16},{16,24},{24,32},{32,40},{40,48},{48,56},{56,64},{64,7... | collective-permute-start | bytes 995336 | tf_op jit(solution)/shard_map/ppermute | solution.py:322
  107.2 12.2 %collective-permute-start.7 = (bf16[1296,128]{1,0:T(8,128)(2,1)S(1)}, bf16[1296,128]{1,0:T(8,128)(2,1)S(1)}, u32[]{:S(2)}, u32[]{:S(2)}) collective-permute-start(bf16[1296,128]{1,0:T(8,128)(2,1)S(1)} %get-tuple-element.45), channel_id=1, source_target_pairs={{8,0},{16,8},{24,16},{32,24},{40,32},{48,40},{56,48},{64,56},{72,6... | collective-permute-start | bytes 995336 | tf_op jit(solution)/shard_map/ppermute | solution.py:323
  109.1 2.5 copy-start.6
  127.1 2.3 copy-start.2
  129.5 1.8 copy-start.7
  131.3 45.4 %all-to-all-start = ((bf16[8,1296,128]{2,1,0:T(8,128)(2,1)}), bf16[8,1296,128]{2,1,0:T(8,128)(2,1)}, u32[]{:S(2)}, u32[]{:S(2)}) async-start(bf16[8,1296,128]{2,1,0:T(8,128)(2,1)} %bitcast.3), calls=%async_computation | async-start | bytes 5308416 | tf_op jit(solution)/shard_map/all_to_all | solution.py:349
  135.8 33.6 %collective-permute-start.8 = (bf16[1296,128]{1,0:T(8,128)(2,1)S(1)}, bf16[1296,128]{1,0:T(8,128)(2,1)S(1)}, u32[]{:S(2)}, u32[]{:S(2)}) collective-permute-start(bf16[1296,128]{1,0:T(8,128)(2,1)S(1)} %get-tuple-element.49), channel_id=1, source_target_pairs={{0,8},{8,16},{16,24},{24,32},{32,40},{40,48},{48,56},{56,64},{64,7... | collective-permute-start | bytes 995336 | tf_op jit(solution)/shard_map/ppermute | solution.py:322
  141.8 31.5 %collective-permute-start.9 = (bf16[1296,128]{1,0:T(8,128)(2,1)S(1)}, bf16[1296,128]{1,0:T(8,128)(2,1)S(1)}, u32[]{:S(2)}, u32[]{:S(2)}) collective-permute-start(bf16[1296,128]{1,0:T(8,128)(2,1)S(1)} %get-tuple-element.50), channel_id=1, source_target_pairs={{8,0},{16,8},{24,16},{32,24},{40,32},{48,40},{56,48},{64,56},{72,6... | collective-permute-start | bytes 995336 | tf_op jit(solution)/shard_map/ppermute | solution.py:323
  143.7 2.5 copy-start.1
  146.2 2.5 copy-start.3
  148.7 2.0 copy-start.8
  240.4 17.8 %copy-start.12 = (s32[25,512]{1,0:T(8,128)S(1)}, s32[25,512]{1,0:T(8,128)}, u32[]{:S(2)}) copy-start(s32[25,512]{1,0:T(8,128)} %index_ref.1) | copy-start | bytes 153604
  241.6 33.5 %all-to-all-start.3 = ((bf16[16,128,64]{1,2,0:T(8,128)(2,1)}), bf16[16,128,64]{1,2,0:T(8,128)(2,1)S(1)}, u32[]{:S(2)}, u32[]{:S(2)}) async-start(bf16[16,128,64]{1,2,0:T(8,128)(2,1)} %bitcast.9), calls=%async_computation.3 | async-start | bytes 524288 | tf_op jit(solution)/shard_map/all_to_all | solution.py:316
  258.4 2.5 copy-start.4

commit v2 on v1

--- a/solution.py
+++ b/solution.py
@@ -17,6 +17,9 @@
 FACE = SIDE * SIDE
 NODES = FACE * EDGE
 COLS = 128
+SLABS = 16
+GROUP = 144
+GATHER_PARTS = ((0, CELLS),)
 QUAD = EDGE * EDGE
 THIRDS = 3
 THIRD = FACE // THIRDS
@@ -25,14 +28,15 @@
 VMEM = pl.BlockSpec(memory_space=pltpu.VMEM)
 SMEM = pl.BlockSpec(memory_space=pltpu.SMEM)
 BIG = pltpu.CompilerParams(vmem_limit_bytes=24 * 1024 * 1024)
+SMALL = pltpu.CompilerParams(vmem_limit_bytes=8 * 1024 * 1024)
 
 
 def first_row(cell_y, cell_x, j):
     return (((EDGE - 1) * cell_y + j) * SIDE + (EDGE - 1) * cell_x) * EDGE
 
 
-def gather_kernel(states_ref, pot_ref, index_ref, matrix_ref, field_ref, pot_out_ref, mat_ref, face_mat_ref,
-                  rhs_ref, hot_ref, column_ref):
+def gather_kernel(states_ref, pot_ref, index_ref, matrix_ref, low_ref, high_ref, field_ref, pot_out_ref, mat_ref,
+                  face_mat_ref, rhs_ref, hot_ref, column_ref):
     for cell_y in range(SLAB_XY):
         five = index_ref[cell_y * SLAB_XY : (cell_y + 1) * SLAB_XY, :].astype(F32)
         five = jnp.concatenate([five, jnp.zeros((EDGE - SLAB_XY, CELL_NODES), F32)], axis=0)
@@ -53,36 +57,38 @@
     face_mat_ref[:QUAD, :] = turned[:QUAD, :]
     face_mat_ref[QUAD:, :] = turned[CELL_NODES - QUAD :, :]
     mat_ref[...] = jnp.dot(order, turned, preferred_element_type=F32).astype(BF16)
-
-    def step(i, _):
-        plane = i // SLAB_XY
-        cell_y = i % SLAB_XY
-
-        @pl.when(cell_y == 0)
-        def _():
-            rhs_ref[:, :COLS] = states_ref[pl.ds(pl.multiple_of(plane * FACE, 16), FACE), :]
-
-        lanes = lax.broadcasted_iota(jnp.int32, (QUAD, FACE), 1).astype(F32)
-        shift = (plane * FACE).astype(F32)
-        for cell_x in range(SLAB_XY):
-            want = column_ref[pl.ds(pl.multiple_of(cell_y * CELL_NODES + plane * QUAD, 8), QUAD), cell_x : cell_x + 1] - shift
-            hot_ref[cell_x * QUAD : (cell_x + 1) * QUAD, :] = jnp.where(want == lanes, 1.0, 0.0).astype(BF16)
-        got = jnp.dot(hot_ref[...], rhs_ref[...], preferred_element_type=F32)
+    lead, shift = factors((low_ref, high_ref), 2)
+
+    def step(plane, _):
+        rhs_ref[:, :COLS] = states_ref[pl.ds(pl.multiple_of(plane * FACE, 16), FACE), :]
+        start = (plane * FACE).astype(F32)
         lane = lax.broadcasted_iota(jnp.int32, (EDGE, COLS), 1)
         mine = (lane % EDGE == plane) & (lane < 3 * EDGE)
-        for cell_x in range(SLAB_XY):
-            for j in range(EDGE):
-                at = cell_x * QUAD + j * EDGE
-                rows = pl.ds(first_row(cell_y, cell_x, j) + plane, EDGE, stride=EDGE)
-                field_ref[rows, :] = got[at : at + EDGE, :COLS]
-                value = jnp.sum(jnp.where(mine, got[at : at + EDGE, COLS:], 0.0), axis=1, keepdims=True)
-                pot_out_ref[rows, :] = jnp.broadcast_to(value, (EDGE, COLS))
+        for first, last in GATHER_PARTS:
+            at = 0
+            for cell in range(first, last):
+                cell_y, cell_x = cell // SLAB_XY, cell % SLAB_XY
+                rows = QUAD if cell_y == SLAB_XY - 1 else QUAD - EDGE
+                lanes = lax.broadcasted_iota(jnp.int32, (rows, FACE), 1).astype(F32)
+                want = column_ref[pl.ds(pl.multiple_of(cell_y * CELL_NODES + plane * QUAD, 8), rows), cell_x : cell_x + 1] - start
+                hot_ref[at : at + rows, :] = jnp.where(want == lanes, 1.0, 0.0).astype(BF16)
+                at += rows
+            got = jnp.dot(hot_ref[:at, :], rhs_ref[...], preferred_element_type=F32)
+            at = 0
+            for cell in range(first, last):
+                cell_y, cell_x = cell // SLAB_XY, cell % SLAB_XY
+                for j in range(EDGE if cell_y == SLAB_XY - 1 else EDGE - 1):
+                    rows = pl.ds(first_row(cell_y, cell_x, j) + plane, EDGE, stride=EDGE)
+                    field_ref[rows, :] = got[at : at + EDGE, :COLS]
+                    value = jnp.sum(jnp.where(mine, got[at : at + EDGE, COLS:], 0.0), axis=1, keepdims=True)
+                    pot_out_ref[rows, :] = lead * value - shift
+                    at += EDGE
         return 0
 
-    lax.fori_loop(0, EDGE * SLAB_XY, step, 0)
-
-
-def gather(states, potential, connectivity, matrix):
+    lax.fori_loop(0, EDGE, step, 0)
+
+
+def gather(states, potential, connectivity, matrix, bounds):
     return pl.pallas_call(
         gather_kernel,
         name="gather_states",
@@ -92,15 +98,15 @@
             pltpu.VMEM((CELL_NODES, CELL_NODES), BF16),
             pltpu.VMEM((2 * QUAD, CELL_NODES), BF16),
         ),
-        in_specs=[VMEM] * 4,
+        in_specs=[VMEM] * 4 + [SMEM] * 2,
         out_specs=(VMEM,) * 4,
         scratch_shapes=[
             pltpu.VMEM((FACE, 2 * COLS), BF16),
-            pltpu.VMEM((SLAB_XY * QUAD, FACE), BF16),
+            pltpu.VMEM((CELLS * QUAD, FACE), BF16),
             pltpu.VMEM((SLAB_XY * CELL_NODES, COLS), F32),
         ],
         compiler_params=BIG,
-    )(states, potential.reshape(EDGE, FACE), connectivity, matrix)
+    )(states, potential.reshape(EDGE, FACE), connectivity, matrix, *bounds)
 
 
 def half_width_of(bounds):
@@ -128,9 +134,10 @@
     refs = list(refs)
     field_ref = refs.pop(0)
     if settle:
-        low_in, high_in = refs.pop(0), refs.pop(0)
+        near_in, far_in = refs.pop(0), refs.pop(0)
     bounds = (refs.pop(0), refs.pop(0))
-    weight_ref = refs.pop(0)
+    position_ref = refs.pop(0)
+    odd = position_ref[0] % 2
     if spread:
         face_mat_ref, scale_ref = refs.pop(0), refs.pop(0)
     if settle:
@@ -138,23 +145,28 @@
     if emit:
         plain_ref = refs.pop(0)
     if spread:
-        low_out, high_out, blocks_ref, sums_ref = refs
+        near_out, far_out, blocks_ref, sums_ref = refs
     if settle:
         lead, _ = factors(bounds, stage)
+        ends = (position_ref[0] == 0) | (position_ref[0] == SLABS - 1)
+        far_weight = jnp.where(ends, 1.0, 0.5)
 
         def settle_rows(i, _):
-            for side, (face_in, plane) in enumerate(((low_in, 0), (high_in, EDGE - 1))):
-                got = face_in[pl.ds(pl.multiple_of(i * 16, 16), 16), :].astype(F32)
-                for part in range(2):
-                    rows = pl.ds((i * 2 + part) * QUAD + plane, EDGE, stride=EDGE)
+            for face_in, plane, weight in (
+                (near_in, (EDGE - 1) * (1 - odd), 0.5),
+                (far_in, (EDGE - 1) * odd, far_weight),
+            ):
+                got = face_in[pl.ds(pl.multiple_of(i * GROUP, 16), GROUP), :].astype(F32)
+                for part in range(GROUP // EDGE):
+                    rows = pl.ds((i * (GROUP // EDGE) + part) * QUAD + plane, EDGE, stride=EDGE)
                     value = field_ref[rows, :] + lead * got[part * EDGE : (part + 1) * EDGE, :]
                     value = value.astype(BF16).astype(F32)
                     if stage > STEPS:
-                        value = value * weight_ref[side]
+                        value = value * weight
                     out_ref[rows, :] = value
             return 0
 
-        lax.fori_loop(0, FACE // 16, settle_rows, 0)
+        lax.fori_loop(0, FACE // GROUP, settle_rows, 0)
         field_ref = out_ref
     if emit:
 
@@ -183,18 +195,18 @@
             return 0
 
         lax.fori_loop(0, PAIRS, step, 0)
-        low_out[...] = sums_ref[:FACE, :].astype(BF16)
-        high_out[...] = sums_ref[FACE:, :].astype(BF16)
-
-
-def faces(stage, field, got, bounds, weight, face_mat, scale, emit=False, spread=True):
+        near_out[...] = sums_ref[pl.ds(pl.multiple_of((1 - odd) * FACE, 16), FACE), :].astype(BF16)
+        far_out[...] = sums_ref[pl.ds(pl.multiple_of(odd * FACE, 16), FACE), :].astype(BF16)
+
+
+def faces(stage, field, got, bounds, position, face_mat, scale, emit=False, spread=True):
     settle = got is not None
     args, specs, outs = [field], [VMEM], []
     if settle:
         args += list(got)
         specs += [VMEM] * 2
         outs.append(pltpu.VMEM((NODES, COLS), F32))
-    args += [*bounds, weight]
+    args += [*bounds, position]
     specs += [SMEM] * 3
     if spread:
         args += [face_mat, scale]
@@ -212,7 +224,7 @@
         out_specs=(VMEM,) * len(outs),
         scratch_shapes=[pltpu.VMEM((2 * FACE, COLS), F32)] if spread else [],
         input_output_aliases={0: 0} if settle else {},
-        compiler_params=BIG,
+        compiler_params=SMALL,
     )(*args)
 
 
@@ -220,33 +232,40 @@
     refs = list(refs)
     prev_ref = refs.pop(0) if 1 < stage <= STEPS else None
     pot_ref, mat_ref, low_ref, high_ref, scale_ref, out_ref = refs
+    bounds = (low_ref, high_ref)
     out_ref[...] = jnp.zeros_like(out_ref)
+    lead, _ = factors(bounds, stage)
 
     def step(pair, _):
         product = jnp.dot(mat_ref[...], blocks_ref[pair], preferred_element_type=F32)
         for half, cell_y, cell_x, scale in pair_cells(pair, scale_ref):
+            factor = lead * scale
             for j in range(EDGE):
                 rows = pl.ds(pl.multiple_of(first_row(cell_y, cell_x, j), EDGE), QUAD)
-                out_ref[rows, :] += scale * product[j * QUAD : (j + 1) * QUAD, half * COLS : (half + 1) * COLS]
+                out_ref[rows, :] += factor * product[j * QUAD : (j + 1) * QUAD, half * COLS : (half + 1) * COLS]
         return 0
 
     lax.fori_loop(0, PAIRS, step, 0)
-    lead, shift = factors((low_ref, high_ref), stage)
-    plane = lax.broadcasted_iota(jnp.int32, (QUAD, COLS), 0) % EDGE
+    plane = lax.broadcasted_iota(jnp.int32, (EDGE, COLS), 0)
     inside = (plane > 0) & (plane < EDGE - 1)
+    half_width = half_width_of(bounds) * 0.5
+    center = jnp.full((1, COLS), (high_ref[0] + low_ref[0]) * 0.5, F32)
 
     def finish(i, _):
-        rows = pl.ds(pl.multiple_of(i * QUAD, QUAD), QUAD)
-        field = field_ref[rows, :]
-        value = out_ref[rows, :] + pot_ref[rows, :] * field
-        if stage <= STEPS:
-            value = lead * value - shift * field
-        if prev_ref is not None:
-            value = value - prev_ref[rows, :]
-        out_ref[rows, :] = jnp.where(inside, value.astype(BF16).astype(F32), value)
+        for part in range(GROUP // EDGE):
+            rows = pl.ds(pl.multiple_of(i * GROUP + part * EDGE, EDGE), EDGE)
+            shifted = pot_ref[rows, :]
+            if stage == 1:
+                shifted = shifted * 0.5
+            elif stage > STEPS:
+                shifted = shifted * half_width + center
+            value = out_ref[rows, :] + shifted * field_ref[rows, :]
+            if prev_ref is not None:
+                value = value - prev_ref[rows, :]
+            out_ref[rows, :] = jnp.where(inside, value.astype(BF16).astype(F32), value)
         return 0
 
-    lax.fori_loop(0, NODES // QUAD, finish, 0)
+    lax.fori_loop(0, NODES // GROUP, finish, 0)
 
 
 def cells(stage, blocks, field, prev, pot, mat, bounds, scale):
@@ -258,11 +277,12 @@
         out_shape=pltpu.VMEM((NODES, COLS), F32),
         in_specs=specs,
         out_specs=VMEM,
-        compiler_params=BIG,
+        compiler_params=SMALL,
     )(*args, *bounds, scale)
 
 
-def return_kernel(field_ref, index_ref, out_ref, hot_ref, rhs_ref):
+def return_kernel(plain_ref, index_ref, out_ref, hot_ref, rhs_ref, field_ref):
+    field_ref[...] = plain_ref[...].astype(F32)
     j = lax.broadcasted_iota(jnp.int32, (EDGE, COLS), 0)
 
     def step(plane, _):
@@ -300,59 +320,63 @@
         scratch_shapes=[
             pltpu.VMEM((THIRD, CELLS * QUAD), BF16),
             pltpu.VMEM((CELLS * QUAD, COLS), F32),
+            pltpu.VMEM((NODES, COLS), F32),
         ],
         compiler_params=BIG,
     )(field, index)
 
 
-def in_blocks(x, dim, peers):
-    dims = x.shape
-    blocks = x.reshape(*dims[:dim], peers, dims[dim] // peers, *dims[dim + 1 :])
-    return jnp.moveaxis(blocks, dim, 0)
-
-
-def summed_on_arrival(x, axis, dim):
-    blocks = in_blocks(x, dim, lax.axis_size(axis))
-    arrived = lax.all_to_all(blocks, axis, split_axis=0, concat_axis=0, tiled=True)
-    return arrived.astype(F32).sum(axis=0)
-
-
-def swap_faces(low, high):
+def project(states, images):
+    count, bands = lax.axis_size("space"), lax.axis_size("band")
+    odd = lax.axis_index("space") % 2
+    halves = count // 2
+    product = lax.dot_general(images, states, (((0,), (0,)), ((), ())), preferred_element_type=F32).astype(BF16)
+    width = product.shape[0] // count
+    product = product.reshape(halves, 2, width, bands, COLS)
+    kept = lax.dynamic_index_in_dim(product, odd, axis=1, keepdims=False)
+    sent = lax.dynamic_index_in_dim(product, 1 - odd, axis=1, keepdims=False)
+    got = lax.ppermute(sent, "space", [(i, i ^ 1) for i in range(count)])
+    both = (kept.astype(F32) + got.astype(F32)).astype(BF16)
+    both = both.transpose(0, 2, 1, 3).reshape(halves * bands, width, COLS)
+    groups = [[(2 * half + part) * bands + band for half in range(halves) for band in range(bands)] for part in range(2)]
+    arrived = lax.all_to_all(both, ("space", "band"), split_axis=0, concat_axis=0, tiled=True, axis_index_groups=groups)
+    return arrived.astype(F32).sum(axis=0).T
+
+
+def swap_faces(near, far):
     count = lax.axis_size("space")
-    from_below = lax.ppermute(high, "space", [(i, i + 1) for i in range(count - 1)])
-    from_above = lax.ppermute(low, "space", [(i + 1, i) for i in range(count - 1)])
-    return from_below, from_above
+    apart = [(i, i + 1) for i in range(1, count - 1, 2)]
+    beside = [(i, i + 1) for i in range(0, count, 2)]
+    both_ways = lambda pairs: pairs + [(j, i) for i, j in pairs]
+    near, far = lax.optimization_barrier((near, far))
+    from_near = lax.ppermute(near, "space", both_ways(beside))
+    from_far = lax.ppermute(far, "space", both_ways(apart))
+    return from_near, from_far
 
 
 def local(states, potential, cell_matrix, cell_scale, connectivity, lower_bound, upper_bound):
     bounds = (lower_bound, upper_bound)
-    position = lax.axis_index("space")
+    position = lax.axis_index("space").astype(jnp.int32).reshape(1)
     count = lax.axis_size("space")
-    weight = jnp.stack([
-        jnp.where(position > 0, 0.5, 1.0).astype(F32),
-        jnp.where(position < count - 1, 0.5, 1.0).astype(F32),
-    ])
-    field, pot, mat, face_mat = gather(states, potential, connectivity, cell_matrix)
-    low, high, blocks = faces(0, field, None, bounds, weight, face_mat, cell_scale)
+    field, pot, mat, face_mat = gather(states, potential, connectivity, cell_matrix, bounds)
+    near, far, blocks = faces(0, field, None, bounds, position, face_mat, cell_scale)
     prev = None
     for stage in range(1, STEPS + 2):
-        got = swap_faces(low, high)
+        got = swap_faces(near, far)
         part = cells(stage, blocks, field, prev, pot, mat, bounds, cell_scale)
         prev = field
         if stage < STEPS:
-            field, low, high, blocks = faces(stage, part, got, bounds, weight, face_mat, cell_scale)
+            field, near, far, blocks = faces(stage, part, got, bounds, position, face_mat, cell_scale)
         elif stage == STEPS:
-            field, current, low, high, blocks = faces(
-                stage, part, got, bounds, weight, face_mat, cell_scale, emit=True)
+            field, current, near, far, blocks = faces(
+                stage, part, got, bounds, position, face_mat, cell_scale, emit=True)
         else:
-            _, weighted = faces(stage, part, got, bounds, weight, None, None, emit=True, spread=False)
+            _, weighted = faces(stage, part, got, bounds, position, None, None, emit=True, spread=False)
     node_states = lax.all_to_all(current, "band", split_axis=0, concat_axis=1, tiled=True)
+    weighted, current = lax.optimization_barrier((weighted, current))
+    filtered = hand_back(current, connectivity)
     node_images = lax.all_to_all(weighted, "band", split_axis=0, concat_axis=1, tiled=True)
-    partial_matrix = lax.dot_general(
-        node_states, node_images, (((0,), (0,)), ((), ())), preferred_element_type=F32)
-    row_sums = summed_on_arrival(partial_matrix.astype(BF16), "band", 0)
-    totals = summed_on_arrival(row_sums.astype(BF16), "space", 1)
-    filtered = hand_back(field, connectivity)
+    totals = project(node_states, node_images)
     global_count = FACE * ((EDGE - 1) * count + 1)
     return filtered, totals / global_count
 

time: 277 us -> 233 us (0.84)
  blocking collectives: 58.3 us -> 0 us
  waiting for transfers between devices: 16.5 us -> 50.3 us
  Pallas kernels: 110 us -> 96.7 us
  local copies, waits for them, and re-layouts: 24 us -> 17 us
    all_to_all x2 -> x0, blocking collectives: 58.3 us -> none  [the longest x1 32.5 us: local(): lax.all_to_all(weighted, 'band', split_axis=0, concat_axis=1, tiled=True)]
    all_to_all x1 -> x2, waiting for transfers between devices: 0.01 us -> 29.5 us  [the longest x1 28.1 us: local(): lax.all_to_all(weighted, 'band', split_axis=0, concat_axis=1, tiled=True)]
    pallas_call x1, Pallas kernels: 23.3 us -> 13.4 us  [gather(): pl.pallas_call(gather_kernel, name='gather_states', out_shape=(pltpu.VMEM...]
    unnamed x28 -> x23, local copies, waits for them, and re-layouts: 22.1 us -> 15.4 us
    ppermute x10 -> x11, starting transfers between devices: 37 us -> 32 us  [the longest x5 29.9 us: swap_faces(): from_far = lax.ppermute(far, 'space', both_ways(apart))]
    all_to_all x1 -> x2, starting transfers between devices: 16.6 us -> 21.5 us  [the longest x1 17 us: project(): lax.all_to_all(both, ('space', 'band'), split_axis=0, concat_axis=0, tile...]
    ppermute x10 -> x11, waiting for transfers between devices: 16.5 us -> 20.7 us  [the longest x5 18.1 us: swap_faces(): from_far = lax.ppermute(far, 'space', both_ways(apart))]
    pallas_call x5, Pallas kernels: 37.9 us -> 33.7 us  [cells(): pl.pallas_call(functools.partial(cells_kernel, stage), name='cells', out_...]
  transfers between devices with their start and end apart: 12 -> 14, of which waited for: 5 -> 8; matrix products, arithmetic and copies ran while one was open for 0% -> 0% of each run, Pallas kernels for 20% -> 24%
where the time goes in v2:
time: 233 us; the launch traced here: 232 us
  Pallas kernels  96.7 us (42%)
  starting transfers between devices  57.9 us (25%)
  waiting for transfers between devices  50.3 us (22%)
  local copies, waits for them, and re-layouts  17 us (7%)
  matrix products  5.4 us (2%)
    pallas_call x5, Pallas kernels, cells(): pl.pallas_call(functools.partial(cells_kernel, stage), name='cells', out_...  33.7 us
    pallas_call x6, Pallas kernels, faces(): pl.pallas_call(functools.partial(faces_kernel, stage, settle, emit, sprea...  33.2 us
    ppermute x5, starting transfers between devices, swap_faces(): from_far = lax.ppermute(far, 'space', both_ways(apart))  29.9 us
    all_to_all x1, waiting for transfers between devices, local(): lax.all_to_all(weighted, 'band', split_axis=0, concat_axis=1, tiled=True)  28.1 us
    ppermute x5, waiting for transfers between devices, swap_faces(): from_far = lax.ppermute(far, 'space', both_ways(apart))  18.1 us
    all_to_all x1, starting transfers between devices, project(): lax.all_to_all(both, ('space', 'band'), split_axis=0, concat_axis=0, tile...  17 us
    pallas_call x1, Pallas kernels, hand_back(): pl.pallas_call(return_kernel, name='hand_back', out_shape=jax.ShapeDtypeS...  16.3 us
    unnamed x23, local copies, waits for them, and re-layouts  15.4 us
  transfers between devices with their start and end apart: 14, of which 8 were waited for; matrix products, arithmetic and copies ran while one was open for 0% of the time, Pallas kernels for 24%

profile of v2, /device:TPU:1, one launch (start us, length us, event | category | flops | bytes accessed | tf_op | source)
XLA Modules:
  0.0 231.6 jit_solution(17510729977847386107)
XLA Ops:
  2.8 1.7 copy-done.6
  6.5 13.4 %gather_states.1 = (f32[10368,128]{1,0:T(8,128)S(1)}, f32[10368,128]{1,0:T(8,128)S(1)}, bf16[512,512]{1,0:T(8,128)(2,1)S(1)}, bf16[128,512]{1,0:T(8,128)(2,1)S(1)}) custom-call(bf16[10368,128]{1,0:T(8,128)(2,1)S(1)} %copy-done.6, f32[8,1296]{1,0:T(8,128)S(1)} %reshape.30.pot_ref, s32[25,512]{1,0:T(8,128)S(1)} %copy-done.8, bf16[512,512]{1,0:T(8,128)(2,1)S(1)} %copy-done.7, ...), custom_call_target="tpu_custom_call" | custom-call | tf_op jit(solution)/shard_map/gather_states/pallas_call | solution.py:92
  19.9 3.8 %faces.6 = (bf16[1296,128]{1,0:T(8,128)(2,1)S(1)}, bf16[1296,128]{1,0:T(8,128)(2,1)S(1)}, bf16[13,512,256]{2,1,0:T(8,128)(2,1)S(1)}) custom-call(f32[10368,128]{1,0:T(8,128)S(1)} %get-tuple-element.39.refs_0_.field_ref, f32[1]{0:T(128)S(6)} %copy.53.low_ref.refs_1_.refs_2_.refs_3_, f32[1]{0:T(128)S(6)} %copy.54.high_ref.refs_2_.refs_3_.refs_4_, ...), custom_call_target="tpu_custom_call" | custom-call | tf_op jit(solution)/shard_map/faces/pallas_call | solution.py:219
  23.7 1.5 collective-permute-start
  25.1 5.5 %collective-permute-start.1 = (bf16[1296,128]{1,0:T(8,128)(2,1)S(1)}, bf16[1296,128]{1,0:T(8,128)(2,1)S(1)}, u32[]{:S(2)}, u32[]{:S(2)}) collective-permute-start(bf16[1296,128]{1,0:T(8,128)(2,1)S(1)} %get-tuple-element.47), channel_id=1, source_target_pairs={{8,16},{24,32},{40,48},{56,64},{72,80},{88,96},{104,112},{16,8},{3... | collective-permute-start | bytes 995336 | tf_op jit(solution)/shard_map/ppermute | solution.py:353
  30.6 6.6 %cells.5.refs_0_ = f32[10368,128]{1,0:T(8,128)S(1)} custom-call(bf16[13,512,256]{2,1,0:T(8,128)(2,1)S(1)} %get-tuple-element.41.blocks_ref, f32[10368,128]{1,0:T(8,128)S(1)} %get-tuple-element.39.refs_0_.field_ref, f32[10368,128]{1,0:T(8,128)S(1)} %get-tuple-element.42.refs_0_.refs_1_, bf16[512,512]{1,0:T(8,128)(2,1)S(1)} %get-tuple-element.43.refs_1_.refs_2_, ...), custom_call_target="tpu_custom_call" | custom-call | tf_op jit(solution)/shard_map/cells/pallas_call | solution.py:274
  38.2 5.7 %faces.7 = (f32[10368,128]{1,0:T(8,128)S(1)}, bf16[1296,128]{1,0:T(8,128)(2,1)S(1)}, bf16[1296,128]{1,0:T(8,128)(2,1)S(1)}, bf16[13,512,256]{2,1,0:T(8,128)(2,1)S(1)}) custom-call(f32[10368,128]{1,0:T(8,128)S(1)} %cells.5.refs_0_, bf16[1296,128]{1,0:T(8,128)(2,1)S(1)} %collective-permute-done.refs_1_, ...), custom_call_target="tpu_custom_call", output_to_operand_aliasing={{0}: (0, {})} | custom-call | tf_op jit(solution)/shard_map/faces/pallas_call | solution.py:219
  44.1 5.9 %collective-permute-start.3 = (bf16[1296,128]{1,0:T(8,128)(2,1)S(1)}, bf16[1296,128]{1,0:T(8,128)(2,1)S(1)}, u32[]{:S(2)}, u32[]{:S(2)}) collective-permute-start(bf16[1296,128]{1,0:T(8,128)(2,1)S(1)} %get-tuple-element.53), channel_id=1, source_target_pairs={{8,16},{24,32},{40,48},{56,64},{72,80},{88,96},{104,112},{16,8},{3... | collective-permute-start | bytes 995336 | tf_op jit(solution)/shard_map/ppermute | solution.py:353
  50.0 6.7 %cells.6.refs_0_ = f32[10368,128]{1,0:T(8,128)S(1)} custom-call(bf16[13,512,256]{2,1,0:T(8,128)(2,1)S(1)} %get-tuple-element.48.blocks_ref, f32[10368,128]{1,0:T(8,128)S(1)} %get-tuple-element.49.field_ref.refs_0_, f32[10368,128]{1,0:T(8,128)S(1)} %get-tuple-element.39.refs_0_.field_ref, f32[10368,128]{1,0:T(8,128)S(1)} %get-tuple-element.42.refs_0_.refs_1_, ...), custom_call_target="tpu_custom_call" | custom-call | tf_op jit(solution)/shard_map/cells/pallas_call | solution.py:274
  57.6 5.8 %faces.8 = (f32[10368,128]{1,0:T(8,128)S(1)}, bf16[1296,128]{1,0:T(8,128)(2,1)S(1)}, bf16[1296,128]{1,0:T(8,128)(2,1)S(1)}, bf16[13,512,256]{2,1,0:T(8,128)(2,1)S(1)}) custom-call(f32[10368,128]{1,0:T(8,128)S(1)} %cells.6.refs_0_, bf16[1296,128]{1,0:T(8,128)(2,1)S(1)} %collective-permute-done.2.refs_1_, ...), custom_call_target="tpu_custom_call", output_to_operand_aliasing={{0}: (0, {})} | custom-call | tf_op jit(solution)/shard_map/faces/pallas_call | solution.py:219
  63.4 5.9 %collective-permute-start.5 = (bf16[1296,128]{1,0:T(8,128)(2,1)S(1)}, bf16[1296,128]{1,0:T(8,128)(2,1)S(1)}, u32[]{:S(2)}, u32[]{:S(2)}) collective-permute-start(bf16[1296,128]{1,0:T(8,128)(2,1)S(1)} %get-tuple-element.59), channel_id=1, source_target_pairs={{8,16},{24,32},{40,48},{56,64},{72,80},{88,96},{104,112},{16,8},{3... | collective-permute-start | bytes 995336 | tf_op jit(solution)/shard_map/ppermute | solution.py:353
  69.3 6.7 %cells.7.refs_0_ = f32[10368,128]{1,0:T(8,128)S(1)} custom-call(bf16[13,512,256]{2,1,0:T(8,128)(2,1)S(1)} %get-tuple-element.54.blocks_ref, f32[10368,128]{1,0:T(8,128)S(1)} %get-tuple-element.55.field_ref.refs_0_, f32[10368,128]{1,0:T(8,128)S(1)} %get-tuple-element.49.field_ref.refs_0_, f32[10368,128]{1,0:T(8,128)S(1)} %get-tuple-element.42.refs_0_.refs_1_, ...), custom_call_target="tpu_custom_call" | custom-call | tf_op jit(solution)/shard_map/cells/pallas_call | solution.py:274
  76.9 5.7 %faces.9 = (f32[10368,128]{1,0:T(8,128)S(1)}, bf16[1296,128]{1,0:T(8,128)(2,1)S(1)}, bf16[1296,128]{1,0:T(8,128)(2,1)S(1)}, bf16[13,512,256]{2,1,0:T(8,128)(2,1)S(1)}) custom-call(f32[10368,128]{1,0:T(8,128)S(1)} %cells.7.refs_0_, bf16[1296,128]{1,0:T(8,128)(2,1)S(1)} %collective-permute-done.4.refs_1_, ...), custom_call_target="tpu_custom_call", output_to_operand_aliasing={{0}: (0, {})} | custom-call | tf_op jit(solution)/shard_map/faces/pallas_call | solution.py:219
  82.8 5.9 %collective-permute-start.7 = (bf16[1296,128]{1,0:T(8,128)(2,1)S(1)}, bf16[1296,128]{1,0:T(8,128)(2,1)S(1)}, u32[]{:S(2)}, u32[]{:S(2)}) collective-permute-start(bf16[1296,128]{1,0:T(8,128)(2,1)S(1)} %get-tuple-element.65), channel_id=1, source_target_pairs={{8,16},{24,32},{40,48},{56,64},{72,80},{88,96},{104,112},{16,8},{3... | collective-permute-start | bytes 995336 | tf_op jit(solution)/shard_map/ppermute | solution.py:353
  88.7 6.8 %cells.8.refs_0_ = f32[10368,128]{1,0:T(8,128)S(1)} custom-call(bf16[13,512,256]{2,1,0:T(8,128)(2,1)S(1)} %get-tuple-element.60.blocks_ref, f32[10368,128]{1,0:T(8,128)S(1)} %get-tuple-element.61.field_ref, f32[10368,128]{1,0:T(8,128)S(1)} %get-tuple-element.55.field_ref.refs_0_, f32[10368,128]{1,0:T(8,128)S(1)} %get-tuple-element.42.refs_0_.refs_1_, ...), custom_call_target="tpu_custom_call" | custom-call | tf_op jit(solution)/shard_map/cells/pallas_call | solution.py:274
  96.3 7.8 %faces.10 = (f32[10368,128]{1,0:T(8,128)S(1)}, bf16[10368,128]{1,0:T(8,128)(2,1)}, bf16[1296,128]{1,0:T(8,128)(2,1)S(1)}, bf16[1296,128]{1,0:T(8,128)(2,1)S(1)}, bf16[13,512,256]{2,1,0:T(8,128)(2,1)S(1)}) custom-call(f32[10368,128]{1,0:T(8,128)S(1)} %cells.8.refs_0_, ...), custom_call_target="tpu_custom_call", output_to_operand_aliasing={{0}: (0, {})} | custom-call | tf_op jit(solution)/shard_map/faces/pallas_call | solution.py:219
  104.1 2.4 %copy-done.2 = f32[10368,128]{1,0:T(8,128)} copy-done((f32[10368,128]{1,0:T(8,128)}, f32[10368,128]{1,0:T(8,128)S(1)}, u32[]{:S(2)}) %copy-start.2) | copy-done | bytes 5308440
  106.5 1.8 copy-done.4
  108.3 4.5 %all-to-all-start.1 = ((bf16[8,1296,128]{2,1,0:T(8,128)(2,1)}), bf16[8,1296,128]{2,1,0:T(8,128)(2,1)}, u32[]{:S(2)}, u32[]{:S(2)}) async-start(bf16[8,1296,128]{2,1,0:T(8,128)(2,1)} %bitcast.4), calls=%async_computation.1 | async-start | bytes 5308416 | tf_op jit(solution)/shard_map/all_to_all | solution.py:375
  112.9 6.7 %collective-permute-start.9 = (bf16[1296,128]{1,0:T(8,128)(2,1)S(1)}, bf16[1296,128]{1,0:T(8,128)(2,1)S(1)}, u32[]{:S(2)}, u32[]{:S(2)}) collective-permute-start(bf16[1296,128]{1,0:T(8,128)(2,1)S(1)} %get-tuple-element.71), channel_id=1, source_target_pairs={{8,16},{24,32},{40,48},{56,64},{72,80},{88,96},{104,112},{16,8},{3... | collective-permute-start | bytes 995336 | tf_op jit(solution)/shard_map/ppermute | solution.py:353
  119.6 2.5 %copy-done.1 = f32[10368,128]{1,0:T(8,128)S(1)} copy-done((f32[10368,128]{1,0:T(8,128)S(1)}, f32[10368,128]{1,0:T(8,128)}, u32[]{:S(2)}) %copy-start.1) | copy-done | bytes 5308440
  122.1 2.5 %copy-done.3 = f32[10368,128]{1,0:T(8,128)S(1)} copy-done((f32[10368,128]{1,0:T(8,128)S(1)}, f32[10368,128]{1,0:T(8,128)}, u32[]{:S(2)}) %copy-start.3) | copy-done | bytes 5308440
  124.6 2.0 copy-done.5
  126.6 6.9 %cells.9.refs_0_ = f32[10368,128]{1,0:T(8,128)S(1)} custom-call(bf16[13,512,256]{2,1,0:T(8,128)(2,1)S(1)} %copy-done.5, f32[10368,128]{1,0:T(8,128)S(1)} %copy-done.3, f32[10368,128]{1,0:T(8,128)S(1)} %copy-done.1, bf16[512,512]{1,0:T(8,128)(2,1)S(1)} %get-tuple-element.43.refs_1_.refs_2_, f32[1]{0:T(128)S(6)} %copy.53.low_ref.refs_1_.refs_2_.refs_3_, ...), custom_call_target="tpu_custom_call" | custom-call | tf_op jit(solution)/shard_map/cells/pallas_call | solution.py:274
  133.5 14.6 %collective-permute-done.9.refs_2_ = bf16[1296,128]{1,0:T(8,128)(2,1)S(1)} collective-permute-done((bf16[1296,128]{1,0:T(8,128)(2,1)S(1)}, bf16[1296,128]{1,0:T(8,128)(2,1)S(1)}, u32[]{:S(2)}, u32[]{:S(2)}) %collective-permute-start.9) | collective-permute-done | bytes 331808 | tf_op jit(solution)/shard_map/ppermute | solution.py:353
  148.1 4.4 %faces.11 = (f32[10368,128]{1,0:T(8,128)S(1)}, bf16[10368,128]{1,0:T(8,128)(2,1)}) custom-call(f32[10368,128]{1,0:T(8,128)S(1)} %cells.9.refs_0_, bf16[1296,128]{1,0:T(8,128)(2,1)S(1)} %collective-permute-done.8.refs_1_, bf16[1296,128]{1,0:T(8,128)(2,1)S(1)} %collective-permute-done.9.refs_2_, ...), custom_call_target="tpu_custom_call", output_to_operand_aliasing={{0}: (0, {})} | custom-call | tf_op jit(solution)/shard_map/faces/pallas_call | solution.py:219
  152.5 4.5 %all-to-all-start = ((bf16[8,1296,128]{2,1,0:T(8,128)(2,1)}), bf16[8,1296,128]{2,1,0:T(8,128)(2,1)S(1)}, u32[]{:S(2)}, u32[]{:S(2)}) async-start(bf16[8,1296,128]{2,1,0:T(8,128)(2,1)} %bitcast.2), calls=%async_computation | async-start | bytes 5308416 | tf_op jit(solution)/shard_map/all_to_all | solution.py:378
  157.0 28.1 %all-to-all-done = bf16[8,1296,128]{2,1,0:T(8,128)(2,1)S(1)} async-done(((bf16[8,1296,128]{2,1,0:T(8,128)(2,1)}), bf16[8,1296,128]{2,1,0:T(8,128)(2,1)S(1)}, u32[]{:S(2)}, u32[]{:S(2)}) %all-to-all-start) | async-done | bytes 2654240 | tf_op jit(solution)/shard_map/all_to_all | solution.py:378
  185.1 5.4 %convert_bitcast_fusion = bf16[128,8,8,128]{3,1,2,0:T(8,128)(2,1)S(1)} fusion(bf16[8,1296,128]{2,1,0:T(8,128)(2,1)} %all-to-all-done.1, bf16[8,1296,128]{2,1,0:T(8,128)(2,1)S(1)} %all-to-all-done), kind=kOutput, calls=%fused_computation.8 | convolution fusion | flops 2718957568 | bytes 7405568 | tf_op jit(solution)/shard_map/dot_general | solution.py:333
  191.9 2.6 %collective-permute-done.10 = bf16[8,64,8,128]{3,1,2,0:T(8,128)(2,1)S(1)} collective-permute-done((bf16[8,64,8,128]{3,1,2,0:T(8,128)(2,1)S(1)}, bf16[8,64,8,128]{3,1,2,0:T(8,128)(2,1)S(1)}, u32[]{:S(2)}, u32[]{:S(2)}) %collective-permute-start.10) | collective-permute-done | bytes 1048608 | tf_op jit(solution)/shard_map/ppermute | solution.py:338
  195.8 17.0 %all-to-all-start.2 = ((bf16[64,64,128]{2,1,0:T(8,128)(2,1)}), bf16[64,64,128]{2,1,0:T(8,128)(2,1)S(1)}, u32[]{:S(2)}, u32[]{:S(2)}) async-start(bf16[64,64,128]{2,1,0:T(8,128)(2,1)} %bitcast.9), calls=%async_computation.2 | async-start | bytes 2097152 | tf_op jit(solution)/shard_map/all_to_all | solution.py:342
  213.1 16.3 %hand_back.1 = bf16[10368,128]{1,0:T(8,128)(2,1)} custom-call(bf16[10368,128]{1,0:T(8,128)(2,1)} %get-tuple-element.74.plain_ref, s32[8,1600]{1,0:T(8,128)S(1)} %reshape.33.index_ref), custom_call_target="tpu_custom_call" | custom-call | tf_op jit(solution)/shard_map/hand_back/pallas_call | solution.py:314
  (42 shorter events, 11.6 us)
Async XLA Ops:
  0.6 19.2 %copy-start.10 = (f32[25]{0:T(128)S(1)}, f32[25]{0:T(128)}, u32[]{:S(2)}) copy-start(f32[25]{0:T(128)} %refs_4_.11) | copy-start | bytes 304
  2.8 1.8 copy-start.6
  4.6 1.0 copy-start.7
  5.6 0.8 copy-start.8
  19.9 68.8 %copy-start = (f32[10368,128]{1,0:T(8,128)}, f32[10368,128]{1,0:T(8,128)S(1)}, u32[]{:S(2)}) copy-start(f32[10368,128]{1,0:T(8,128)S(1)} %get-tuple-element.42.refs_0_.refs_1_) | copy-start | bytes 15925252
  23.7 13.6 %collective-permute-start = (bf16[1296,128]{1,0:T(8,128)(2,1)S(1)}, bf16[1296,128]{1,0:T(8,128)(2,1)S(1)}, u32[]{:S(2)}, u32[]{:S(2)}) collective-permute-start(bf16[1296,128]{1,0:T(8,128)(2,1)S(1)} %get-tuple-element.46), channel_id=1, source_target_pairs={{0,8},{16,24},{32,40},{48,56},{64,72},{80,88},{96,104},{112,120},{... | collective-permute-start | bytes 995336 | tf_op jit(solution)/shard_map/ppermute | solution.py:352
  25.1 13.1 %collective-permute-start.1 = (bf16[1296,128]{1,0:T(8,128)(2,1)S(1)}, bf16[1296,128]{1,0:T(8,128)(2,1)S(1)}, u32[]{:S(2)}, u32[]{:S(2)}) collective-permute-start(bf16[1296,128]{1,0:T(8,128)(2,1)S(1)} %get-tuple-element.47), channel_id=1, source_target_pairs={{8,16},{24,32},{40,48},{56,64},{72,80},{88,96},{104,112},{16,8},{3... | collective-permute-start | bytes 995336 | tf_op jit(solution)/shard_map/ppermute | solution.py:353
  44.0 12.7 %collective-permute-start.2 = (bf16[1296,128]{1,0:T(8,128)(2,1)S(1)}, bf16[1296,128]{1,0:T(8,128)(2,1)S(1)}, u32[]{:S(2)}, u32[]{:S(2)}) collective-permute-start(bf16[1296,128]{1,0:T(8,128)(2,1)S(1)} %get-tuple-element.52), channel_id=1, source_target_pairs={{0,8},{16,24},{32,40},{48,56},{64,72},{80,88},{96,104},{112,120},{... | collective-permute-start | bytes 995336 | tf_op jit(solution)/shard_map/ppermute | solution.py:352
  44.1 13.5 %collective-permute-start.3 = (bf16[1296,128]{1,0:T(8,128)(2,1)S(1)}, bf16[1296,128]{1,0:T(8,128)(2,1)S(1)}, u32[]{:S(2)}, u32[]{:S(2)}) collective-permute-start(bf16[1296,128]{1,0:T(8,128)(2,1)S(1)} %get-tuple-element.53), channel_id=1, source_target_pairs={{8,16},{24,32},{40,48},{56,64},{72,80},{88,96},{104,112},{16,8},{3... | collective-permute-start | bytes 995336 | tf_op jit(solution)/shard_map/ppermute | solution.py:353
  63.3 12.7 %collective-permute-start.4 = (bf16[1296,128]{1,0:T(8,128)(2,1)S(1)}, bf16[1296,128]{1,0:T(8,128)(2,1)S(1)}, u32[]{:S(2)}, u32[]{:S(2)}) collective-permute-start(bf16[1296,128]{1,0:T(8,128)(2,1)S(1)} %get-tuple-element.58), channel_id=1, source_target_pairs={{0,8},{16,24},{32,40},{48,56},{64,72},{80,88},{96,104},{112,120},{... | collective-permute-start | bytes 995336 | tf_op jit(solution)/shard_map/ppermute | solution.py:352
  63.4 13.5 %collective-permute-start.5 = (bf16[1296,128]{1,0:T(8,128)(2,1)S(1)}, bf16[1296,128]{1,0:T(8,128)(2,1)S(1)}, u32[]{:S(2)}, u32[]{:S(2)}) collective-permute-start(bf16[1296,128]{1,0:T(8,128)(2,1)S(1)} %get-tuple-element.59), channel_id=1, source_target_pairs={{8,16},{24,32},{40,48},{56,64},{72,80},{88,96},{104,112},{16,8},{3... | collective-permute-start | bytes 995336 | tf_op jit(solution)/shard_map/ppermute | solution.py:353
  82.7 12.8 %collective-permute-start.6 = (bf16[1296,128]{1,0:T(8,128)(2,1)S(1)}, bf16[1296,128]{1,0:T(8,128)(2,1)S(1)}, u32[]{:S(2)}, u32[]{:S(2)}) collective-permute-start(bf16[1296,128]{1,0:T(8,128)(2,1)S(1)} %get-tuple-element.64), channel_id=1, source_target_pairs={{0,8},{16,24},{32,40},{48,56},{64,72},{80,88},{96,104},{112,120},{... | collective-permute-start | bytes 995336 | tf_op jit(solution)/shard_map/ppermute | solution.py:352
  82.8 13.5 %collective-permute-start.7 = (bf16[1296,128]{1,0:T(8,128)(2,1)S(1)}, bf16[1296,128]{1,0:T(8,128)(2,1)S(1)}, u32[]{:S(2)}, u32[]{:S(2)}) collective-permute-start(bf16[1296,128]{1,0:T(8,128)(2,1)S(1)} %get-tuple-element.65), channel_id=1, source_target_pairs={{8,16},{24,32},{40,48},{56,64},{72,80},{88,96},{104,112},{16,8},{3... | collective-permute-start | bytes 995336 | tf_op jit(solution)/shard_map/ppermute | solution.py:353
  104.1 2.4 %copy-start.2 = (f32[10368,128]{1,0:T(8,128)}, f32[10368,128]{1,0:T(8,128)S(1)}, u32[]{:S(2)}) copy-start(f32[10368,128]{1,0:T(8,128)S(1)} %get-tuple-element.67.field_ref) | copy-start | bytes 15925252
  106.5 1.8 copy-start.4
  108.3 44.1 %all-to-all-start.1 = ((bf16[8,1296,128]{2,1,0:T(8,128)(2,1)}), bf16[8,1296,128]{2,1,0:T(8,128)(2,1)}, u32[]{:S(2)}, u32[]{:S(2)}) async-start(bf16[8,1296,128]{2,1,0:T(8,128)(2,1)} %bitcast.4), calls=%async_computation.1 | async-start | bytes 5308416 | tf_op jit(solution)/shard_map/all_to_all | solution.py:375
  112.8 20.7 %collective-permute-start.8 = (bf16[1296,128]{1,0:T(8,128)(2,1)S(1)}, bf16[1296,128]{1,0:T(8,128)(2,1)S(1)}, u32[]{:S(2)}, u32[]{:S(2)}) collective-permute-start(bf16[1296,128]{1,0:T(8,128)(2,1)S(1)} %get-tuple-element.70), channel_id=1, source_target_pairs={{0,8},{16,24},{32,40},{48,56},{64,72},{80,88},{96,104},{112,120},{... | collective-permute-start | bytes 995336 | tf_op jit(solution)/shard_map/ppermute | solution.py:352
  112.9 35.2 %collective-permute-start.9 = (bf16[1296,128]{1,0:T(8,128)(2,1)S(1)}, bf16[1296,128]{1,0:T(8,128)(2,1)S(1)}, u32[]{:S(2)}, u32[]{:S(2)}) collective-permute-start(bf16[1296,128]{1,0:T(8,128)(2,1)S(1)} %get-tuple-element.71), channel_id=1, source_target_pairs={{8,16},{24,32},{40,48},{56,64},{72,80},{88,96},{104,112},{16,8},{3... | collective-permute-start | bytes 995336 | tf_op jit(solution)/shard_map/ppermute | solution.py:353
  119.6 2.5 %copy-start.1 = (f32[10368,128]{1,0:T(8,128)S(1)}, f32[10368,128]{1,0:T(8,128)}, u32[]{:S(2)}) copy-start(f32[10368,128]{1,0:T(8,128)} %copy-done) | copy-start | bytes 15925252
  122.1 2.5 %copy-start.3 = (f32[10368,128]{1,0:T(8,128)S(1)}, f32[10368,128]{1,0:T(8,128)}, u32[]{:S(2)}) copy-start(f32[10368,128]{1,0:T(8,128)} %copy-done.2) | copy-start | bytes 15925252
  124.6 2.0 copy-start.5
  152.5 32.7 %all-to-all-start = ((bf16[8,1296,128]{2,1,0:T(8,128)(2,1)}), bf16[8,1296,128]{2,1,0:T(8,128)(2,1)S(1)}, u32[]{:S(2)}, u32[]{:S(2)}) async-start(bf16[8,1296,128]{2,1,0:T(8,128)(2,1)} %bitcast.2), calls=%async_computation | async-start | bytes 5308416 | tf_op jit(solution)/shard_map/all_to_all | solution.py:378
  191.6 21.2 %copy-start.9 = (s32[25,512]{1,0:T(8,128)S(1)}, s32[25,512]{1,0:T(8,128)}, u32[]{:S(2)}) copy-start(s32[25,512]{1,0:T(8,128)} %index_ref.1) | copy-start | bytes 153604
  191.6 2.9 %collective-permute-start.10 = (bf16[8,64,8,128]{3,1,2,0:T(8,128)(2,1)S(1)}, bf16[8,64,8,128]{3,1,2,0:T(8,128)(2,1)S(1)}, u32[]{:S(2)}, u32[]{:S(2)}) collective-permute-start(bf16[8,64,8,128]{3,1,2,0:T(8,128)(2,1)S(1)} %bitcast.44), channel_id=1, source_target_pairs={{0,8},{8,0},{16,24},{24,16},{32,40},{40,32},{48,56},{56,48},{64,72... | collective-permute-start | bytes 3145736 | tf_op jit(solution)/shard_map/ppermute | solution.py:338
  195.8 34.9 %all-to-all-start.2 = ((bf16[64,64,128]{2,1,0:T(8,128)(2,1)}), bf16[64,64,128]{2,1,0:T(8,128)(2,1)S(1)}, u32[]{:S(2)}, u32[]{:S(2)}) async-start(bf16[64,64,128]{2,1,0:T(8,128)(2,1)} %bitcast.9), calls=%async_computation.2 | async-start | bytes 2097152 | tf_op jit(solution)/shard_map/all_to_all | solution.py:342

commit v3 on v2

v3 whole, which is shorter than its diff:
```python
import functools

import jax
import jax.numpy as jnp
from jax import lax
from jax.experimental import pallas as pl
from jax.experimental.pallas import tpu as pltpu
from jax.sharding import PartitionSpec as P

EDGE = 8
SLAB_XY = 5
STEPS = 4
CELLS = SLAB_XY * SLAB_XY
PAIRS = (CELLS + 1) // 2
CELL_NODES = EDGE**3
SIDE = (EDGE - 1) * SLAB_XY + 1
FACE = SIDE * SIDE
NODES = FACE * EDGE
COLS = 128
SLABS = 16
GROUP = 144
BANDS = 8
INNER = (EDGE - 2) * FACE
INNER_BLOCK = 976
OUTER = FACE + FACE // 2
OUTER_BLOCK = 256
BLOCK = INNER_BLOCK + 2 * OUTER_BLOCK
GATHER_PARTS = ((0, CELLS),)
QUAD = EDGE * EDGE
THIRDS = 3
THIRD = FACE // THIRDS
F32 = jnp.float32
BF16 = jnp.bfloat16
VMEM = pl.BlockSpec(memory_space=pltpu.VMEM)
SMEM = pl.BlockSpec(memory_space=pltpu.SMEM)
HBM = pl.BlockSpec(memory_space=pltpu.HBM)
BIG = pltpu.CompilerParams(vmem_limit_bytes=24 * 1024 * 1024)
SMALL = pltpu.CompilerParams(vmem_limit_bytes=8 * 1024 * 1024)


def first_row(cell_y, cell_x, j):
    return (((EDGE - 1) * cell_y + j) * SIDE + (EDGE - 1) * cell_x) * EDGE


def gather_kernel(states_hbm, pot_ref, index_hbm, matrix_hbm, low_ref, high_ref, field_ref, pot_out_ref, mat_ref,
                  full_ref, inner_ref, outer_ref, rhs_ref, hot_ref, column_ref, states_ref, index_ref, matrix_ref, sems):
    index_copy = pltpu.make_async_copy(index_hbm, index_ref, sems.at[0])
    matrix_copy = pltpu.make_async_copy(matrix_hbm, matrix_ref, sems.at[1])
    states_copy = pltpu.make_async_copy(states_hbm, states_ref, sems.at[2])
    index_copy.start()
    matrix_copy.start()
    states_copy.start()
    index_copy.wait()
    for cell_y in range(SLAB_XY):
        five = index_ref[cell_y * SLAB_XY : (cell_y + 1) * SLAB_XY, :].astype(F32)
        five = jnp.concatenate([five, jnp.zeros((EDGE - SLAB_XY, CELL_NODES), F32)], axis=0)
        column_ref[cell_y * CELL_NODES : (cell_y + 1) * CELL_NODES, :EDGE] = jnp.transpose(five)
    pot = jnp.transpose(pot_ref[...])
    high = pot.astype(BF16)
    rest = pot - high.astype(F32)
    mid = rest.astype(BF16)
    low = (rest - mid.astype(F32)).astype(BF16)
    rhs_ref[:, COLS:] = jnp.concatenate(
        [high, mid, low, jnp.zeros((FACE, COLS - 3 * EDGE), BF16)], axis=1)

    matrix_copy.wait()
    new = lax.broadcasted_iota(jnp.int32, (CELL_NODES, CELL_NODES), 0)
    old = lax.broadcasted_iota(jnp.int32, (CELL_NODES, CELL_NODES), 1)
    order = jnp.where(old == (new % EDGE) * QUAD + new // EDGE, 1.0, 0.0).astype(BF16)
    across = (((1,), (1,)), ((), ()))
    turned = lax.dot_general(matrix_ref[...], order, across, preferred_element_type=F32).astype(BF16)
    mat_ref[...] = jnp.dot(order, turned, preferred_element_type=F32).astype(BF16)
    for side, first in enumerate((0, CELL_NODES - QUAD)):
        rows = pl.ds(side * QUAD, QUAD)
        face_rows = turned[first : first + QUAD, :].astype(F32)
        z = lax.broadcasted_iota(jnp.int32, (QUAD, CELL_NODES), 1) % EDGE
        full_ref[rows, :] = face_rows.astype(BF16)
        inner_ref[rows, :] = jnp.where((z > 0) & (z < EDGE - 1), face_rows, 0.0).astype(BF16)
        outer_ref[rows, :QUAD] = matrix_ref[first : first + QUAD, :QUAD]
        outer_ref[rows, QUAD:] = matrix_ref[first : first + QUAD, CELL_NODES - QUAD :]
    lead, shift = factors((low_ref, high_ref), 2)
    states_copy.wait()

    def step(plane, _):
        rhs_ref[:, :COLS] = states_ref[pl.ds(pl.multiple_of(plane * FACE, 16), FACE), :]
        start = (plane * FACE).astype(F32)
        lane = lax.broadcasted_iota(jnp.int32, (EDGE, COLS), 1)
        mine = (lane % EDGE == plane) & (lane < 3 * EDGE)
        for first, last in GATHER_PARTS:
            at = 0
            for cell in range(first, last):
                cell_y, cell_x = cell // SLAB_XY, cell % SLAB_XY
                rows = QUAD if cell_y == SLAB_XY - 1 else QUAD - EDGE
                lanes = lax.broadcasted_iota(jnp.int32, (rows, FACE), 1).astype(F32)
                want = column_ref[pl.ds(pl.multiple_of(cell_y * CELL_NODES + plane * QUAD, 8), rows), cell_x : cell_x + 1] - start
                hot_ref[at : at + rows, :] = jnp.where(want == lanes, 1.0, 0.0).astype(BF16)
                at += rows
            got = jnp.dot(hot_ref[:at, :], rhs_ref[...], preferred_element_type=F32)
            at = 0
            for cell in range(first, last):
                cell_y, cell_x = cell // SLAB_XY, cell % SLAB_XY
                for j in range(EDGE if cell_y == SLAB_XY - 1 else EDGE - 1):
                    rows = pl.ds(first_row(cell_y, cell_x, j) + plane, EDGE, stride=EDGE)
                    field_ref[rows, :] = got[at : at + EDGE, :COLS]
                    value = jnp.sum(jnp.where(mine, got[at : at + EDGE, COLS:], 0.0), axis=1, keepdims=True)
                    pot_out_ref[rows, :] = lead * value - shift
                    at += EDGE
        return 0

    lax.fori_loop(0, EDGE, step, 0)


def gather(states, potential, connectivity, matrix, bounds):
    return pl.pallas_call(
        gather_kernel,
        name="gather_states",
        out_shape=(
            pltpu.VMEM((NODES, COLS), F32),
            pltpu.VMEM((NODES, COLS), F32),
            pltpu.VMEM((CELL_NODES, CELL_NODES), BF16),
            pltpu.VMEM((2 * QUAD, CELL_NODES), BF16),
            pltpu.VMEM((2 * QUAD, CELL_NODES), BF16),
            pltpu.VMEM((2 * QUAD, 2 * QUAD), BF16),
        ),
        in_specs=[HBM, VMEM, HBM, HBM] + [SMEM] * 2,
        out_specs=(VMEM,) * 6,
        scratch_shapes=[
            pltpu.VMEM((FACE, 2 * COLS), BF16),
            pltpu.VMEM((CELLS * QUAD, FACE), BF16),
            pltpu.VMEM((SLAB_XY * CELL_NODES, COLS), F32),
            pltpu.VMEM((NODES, COLS), BF16),
            pltpu.VMEM((CELLS, CELL_NODES), jnp.int32),
            pltpu.VMEM((CELL_NODES, CELL_NODES), BF16),
            pltpu.SemaphoreType.DMA((3,)),
        ],
        compiler_params=BIG,
    )(states, potential.reshape(EDGE, FACE), connectivity, matrix, *bounds)


def half_width_of(bounds):
    low, high = bounds
    return jnp.full((1, COLS), (high[0] - low[0]) * 0.5, F32)


def factors(bounds, stage):
    if stage > STEPS:
        return jnp.ones((1, COLS), F32), None
    low, high = bounds
    center = (high[0] + low[0]) * 0.5
    lead = (1.0 if stage == 1 else 2.0) / half_width_of(bounds)
    return lead, lead * center


def pair_cells(pair, scale_ref):
    for half in range(2):
        index = 2 * pair + half
        cell = jnp.minimum(index, CELLS - 1)
        yield half, cell // SLAB_XY, cell % SLAB_XY, jnp.where(index < CELLS, scale_ref[cell], 0.0)


def cell_blocks(field_ref, pair, scale_ref):
    columns = []
    for half, cell_y, cell_x, _ in pair_cells(pair, scale_ref):
        pieces = []
        for j in range(EDGE):
            rows = pl.ds(pl.multiple_of(first_row(cell_y, cell_x, j), EDGE), QUAD)
            pieces.append(field_ref[rows, :].astype(BF16))
        columns.append(jnp.concatenate(pieces, axis=0))
    return jnp.concatenate(columns, axis=1)


def add_faces(sums_ref, product, pair, scale_ref):
    for half, cell_y, cell_x, scale in pair_cells(pair, scale_ref):
        for side in range(2):
            for j in range(EDGE):
                at = side * QUAD + j * EDGE
                rows = pl.ds(side * FACE + ((EDGE - 1) * cell_y + j) * SIDE + (EDGE - 1) * cell_x, EDGE)
                sums_ref[rows, :] += scale * product[at : at + EDGE, half * COLS : (half + 1) * COLS]


def spread_faces(field_ref, matrix_ref, scale_ref, sums_ref):
    sums_ref[...] = jnp.zeros_like(sums_ref)

    def step(pair, _):
        blocks = cell_blocks(field_ref, pair, scale_ref)
        product = jnp.dot(matrix_ref[...], blocks, preferred_element_type=F32)
        add_faces(sums_ref, product, pair, scale_ref)
        return 0

    lax.fori_loop(0, PAIRS, step, 0)


def hand_out(sums_ref, odd, near_out, far_out):
    near_out[...] = sums_ref[pl.ds(pl.multiple_of((1 - odd) * FACE, 16), FACE), :].astype(BF16)
    far_out[...] = sums_ref[pl.ds(pl.multiple_of(odd * FACE, 16), FACE), :].astype(BF16)


def first_faces_kernel(field_ref, full_ref, scale_ref, position_ref, near_out, far_out, sums_ref):
    spread_faces(field_ref, full_ref, scale_ref, sums_ref)
    hand_out(sums_ref, position_ref[0] % 2, near_out, far_out)


def first_faces(field, full, scale, position):
    return pl.pallas_call(
        first_faces_kernel,
        name="first_faces",
        out_shape=(jax.ShapeDtypeStruct((FACE, COLS), BF16),) * 2,
        in_specs=[VMEM] * 2 + [SMEM] * 2,
        out_specs=(VMEM,) * 2,
        scratch_shapes=[pltpu.VMEM((2 * FACE, COLS), F32)],
        compiler_params=SMALL,
    )(field, full, scale, position)


def put_inner(field_ref, store):
    def planes(i, _):
        for z in range(1, EDGE - 1):
            for part in range(3):
                node = i * 48 + part * 16
                halves = [field_ref[pl.ds((node + k) * EDGE + z, EDGE, stride=EDGE), :] for k in (0, EDGE)]
                store((z - 1) * FACE + node, jnp.concatenate(halves, axis=0).astype(BF16))
        return 0

    lax.fori_loop(0, FACE // 48, planes, 0)
    for row in range(INNER, BANDS * INNER_BLOCK, 16):
        store(row, jnp.zeros((16, COLS), BF16))


def put_outer(face_ref, odd, far_weight, store):
    def rows(i, _):
        for part in range(4):
            row = (i * 4 + part) * 16
            far = row < FACE
            near_at = (1 - odd) * FACE + odd * (FACE // 2) + row - FACE
            at = jnp.where(far, odd * FACE + row, jnp.minimum(near_at, 2 * FACE))
            value = face_ref[pl.ds(pl.multiple_of(at, EDGE), 16), :]
            if far_weight is not None:
                value = value * jnp.where(far, far_weight, 1.0)
            index = lax.broadcasted_iota(jnp.int32, (16, COLS), 0) + row
            store(row, jnp.where(index < OUTER, value, 0.0).astype(BF16))
        return 0

    lax.fori_loop(0, BANDS * OUTER_BLOCK // 64, rows, 0)


def faces_kernel(stage, *refs):
    emit, spread = stage >= STEPS, stage <= STEPS
    refs = list(refs)
    field_ref, near_in, far_in, low_ref, high_ref, position_ref = refs[:6]
    refs = refs[6:]
    if spread:
        outer_ref, scale_ref, _ = refs[:3]
        refs = refs[3:]
        out_ref = refs.pop(0)
        if emit:
            plain_ref, edge_ref = refs.pop(0), refs.pop(0)
        sums_ref, near_out, far_out, face_ref = refs
    else:
        _, block_ref, face_ref = refs
    odd = position_ref[0] % 2
    lead, _ = factors((low_ref, high_ref), stage)
    ends = (position_ref[0] == 0) | (position_ref[0] == SLABS - 1)
    far_weight = jnp.where(ends, 1.0, 0.5)

    def settle_rows(i, _):
        for face_in, plane, side in ((near_in, (EDGE - 1) * (1 - odd), 1 - odd), (far_in, (EDGE - 1) * odd, odd)):
            got = face_in[pl.ds(pl.multiple_of(i * GROUP, 16), GROUP), :].astype(F32)
            for part in range(GROUP // EDGE):
                rows = pl.ds((i * (GROUP // EDGE) + part) * QUAD + plane, EDGE, stride=EDGE)
                value = field_ref[rows, :] + lead * got[part * EDGE : (part + 1) * EDGE, :]
                value = value.astype(BF16).astype(F32)
                if spread:
                    out_ref[rows, :] = value
                face_ref[pl.ds(pl.multiple_of(side * FACE + i * GROUP + part * EDGE, EDGE), EDGE), :] = value
        return 0

    lax.fori_loop(0, FACE // GROUP, settle_rows, 0)
    if not spread:

        def put(row, value):
            at = (row // OUTER_BLOCK) * BLOCK + OUTER_BLOCK + INNER_BLOCK + row % OUTER_BLOCK
            block_ref[pl.ds(pl.multiple_of(at, 16), 16), :] = value

        put_outer(face_ref, odd, far_weight, put)
        return
    if spread:

        def step(pair, _):
            columns = []
            for half, cell_y, cell_x, _ in pair_cells(pair, scale_ref):
                pieces = []
                for side in range(2):
                    for j in range(EDGE):
                        rows = pl.ds(side * FACE + ((EDGE - 1) * cell_y + j) * SIDE + (EDGE - 1) * cell_x, EDGE)
                        pieces.append(face_ref[rows, :])
                columns.append(jnp.concatenate(pieces, axis=0).astype(BF16))
            product = jnp.dot(outer_ref[...], jnp.concatenate(columns, axis=1), preferred_element_type=F32)
            add_faces(sums_ref, product, pair, scale_ref)
            return 0

        lax.fori_loop(0, PAIRS, step, 0)
        hand_out(sums_ref, odd, near_out, far_out)
    if emit:

        def emit_rows(i, _):
            rows = pl.ds(pl.multiple_of(i * 2 * GROUP, 2 * GROUP), 2 * GROUP)
            plain_ref[rows, :] = out_ref[rows, :].astype(BF16)
            return 0

        def put_edge(row, value):
            edge_ref[pl.ds(pl.multiple_of(row, 16), 16), :] = value

        lax.fori_loop(0, NODES // (2 * GROUP), emit_rows, 0)
        put_outer(face_ref, odd, None, put_edge)


def faces(stage, part, got, bounds, position, outer=None, scale=None, sums=None, blocks=None):
    emit, spread = stage >= STEPS, stage <= STEPS
    args = [part, *got, *bounds, position]
    specs = [VMEM] * 3 + [SMEM] * 3
    outs = []
    if spread:
        args += [outer, scale, sums]
        specs += [VMEM, SMEM, VMEM]
        outs.append(pltpu.VMEM((NODES, COLS), F32))
        if emit:
            outs.append(jax.ShapeDtypeStruct((NODES, COLS), BF16))
            outs.append(jax.ShapeDtypeStruct((BANDS * OUTER_BLOCK, COLS), BF16))
        aliases = {0: 0, 8: len(outs)}
        outs.append(pltpu.VMEM((2 * FACE, COLS), F32))
        outs += [jax.ShapeDtypeStruct((FACE, COLS), BF16)] * 2
    else:
        args.append(blocks)
        specs.append(VMEM)
        outs.append(pltpu.VMEM((BANDS * BLOCK, COLS), BF16))
        aliases = {6: 0}
    return pl.pallas_call(
        functools.partial(faces_kernel, stage),
        name="faces",
        out_shape=tuple(outs),
        in_specs=specs,
        out_specs=(VMEM,) * len(outs),
        scratch_shapes=[pltpu.VMEM((2 * FACE + 16, COLS), F32)],
        input_output_aliases=aliases,
        compiler_params=SMALL,
    )(*args)


def cells_kernel(stage, field_ref, *refs):
    refs = list(refs)
    in_place = 1 < stage <= STEPS
    if in_place:
        refs.pop(0)
    pot_ref, mat_ref = refs.pop(0), refs.pop(0)
    inner_ref = refs.pop(0) if stage <= STEPS else None
    if stage > STEPS:
        edge_ref = refs.pop(0)
    low_ref, high_ref, scale_ref, out_ref = refs[:4]
    bounds = (low_ref, high_ref)
    if stage > STEPS:
        plain_ref, field_ref, block_ref = field_ref, refs[5], refs[4]
        for band in range(BANDS):
            block_ref[band * BLOCK : band * BLOCK + OUTER_BLOCK, :] = (
                edge_ref[band * OUTER_BLOCK : (band + 1) * OUTER_BLOCK, :])

        def widen(i, _):
            rows = pl.ds(pl.multiple_of(i * 2 * GROUP, 2 * GROUP), 2 * GROUP)
            field_ref[rows, :] = plain_ref[rows, :].astype(F32)
            return 0

        lax.fori_loop(0, NODES // (2 * GROUP), widen, 0)
    lead, _ = factors(bounds, stage)
    if in_place:
        lead = -lead
    else:
        out_ref[...] = jnp.zeros_like(out_ref)

    def step(pair, _):
        product = jnp.dot(mat_ref[...], cell_blocks(field_ref, pair, scale_ref), preferred_element_type=F32)
        for half, cell_y, cell_x, scale in pair_cells(pair, scale_ref):
            factor = lead * scale
            for j in range(EDGE):
                rows = pl.ds(pl.multiple_of(first_row(cell_y, cell_x, j), EDGE), QUAD)
                out_ref[rows, :] += factor * product[j * QUAD : (j + 1) * QUAD, half * COLS : (half + 1) * COLS]
        return 0

    lax.fori_loop(0, PAIRS, step, 0)
    plane = lax.broadcasted_iota(jnp.int32, (EDGE, COLS), 0)
    inside = (plane > 0) & (plane < EDGE - 1)
    half_width = half_width_of(bounds) * 0.5
    center = jnp.full((1, COLS), (high_ref[0] + low_ref[0]) * 0.5, F32)

    def finish(i, _):
        for part in range(GROUP // EDGE):
            rows = pl.ds(pl.multiple_of(i * GROUP + part * EDGE, EDGE), EDGE)
            shifted = pot_ref[rows, :]
            if stage == 1:
                shifted = shifted * 0.5
            elif stage > STEPS:
                shifted = shifted * half_width + center
            value = shifted * field_ref[rows, :]
            value = value - out_ref[rows, :] if in_place else value + out_ref[rows, :]
            out_ref[rows, :] = jnp.where(inside, value.astype(BF16).astype(F32), value)
        return 0

    lax.fori_loop(0, NODES // GROUP, finish, 0)

    def put(row, value):
        if stage == STEPS:
            refs[5][pl.ds(pl.multiple_of(row, 16), 16), :] = value
        else:
            at = (row // INNER_BLOCK) * BLOCK + OUTER_BLOCK + row % INNER_BLOCK
            block_ref[pl.ds(pl.multiple_of(at, 16), 16), :] = value

    if stage >= STEPS:
        put_inner(out_ref, put)
    if stage <= STEPS:
        spread_faces(out_ref, inner_ref, scale_ref, refs[4])


def cells(stage, field, prev, pot, mat, inner, bounds, scale, edge=None):
    args = [field] + ([prev] if 1 < stage <= STEPS else []) + [pot, mat, inner if stage <= STEPS else edge]
    specs = [VMEM] * len(args) + [SMEM] * 3
    outs = [pltpu.VMEM((NODES, COLS), F32)]
    if stage <= STEPS:
        outs.append(pltpu.VMEM((2 * FACE, COLS), F32))
    if stage == STEPS:
        outs.append(jax.ShapeDtypeStruct((BANDS * INNER_BLOCK, COLS), BF16))
    if stage > STEPS:
        outs.append(pltpu.VMEM((BANDS * BLOCK, COLS), BF16))
    return pl.pallas_call(
        functools.partial(cells_kernel, stage),
        name="cells",
        out_shape=tuple(outs),
        in_specs=specs,
        out_specs=(VMEM,) * len(outs),
        scratch_shapes=[] if stage <= STEPS else [pltpu.VMEM((NODES, COLS), F32)],
        input_output_aliases={1: 0} if 1 < stage <= STEPS else {},
        compiler_params=SMALL if stage <= STEPS else BIG,
    )(*args, *bounds, scale)


def return_kernel(plain_ref, index_ref, out_ref, hot_ref, rhs_ref, field_ref):
    field_ref[...] = plain_ref[...].astype(F32)
    j = lax.broadcasted_iota(jnp.int32, (EDGE, COLS), 0)

    def step(plane, _):
        for cell in range(CELLS):
            cell_y, cell_x = cell // SLAB_XY, cell % SLAB_XY
            for k in range(EDGE):
                at = cell * QUAD + k * EDGE
                value = field_ref[pl.ds(first_row(cell_y, cell_x, k) + plane, EDGE, stride=EDGE), :]
                if cell_y > 0 and k == 0:
                    value = jnp.zeros_like(value)
                elif cell_x > 0:
                    value = jnp.where(j == 0, 0.0, value)
                rhs_ref[at : at + EDGE, :] = value
        want = index_ref[pl.ds(plane, 1), :].astype(F32) - (plane * FACE).astype(F32)
        rhs = rhs_ref[...].astype(BF16)
        for part in range(THIRDS):
            row = lax.broadcasted_iota(jnp.int32, (THIRD, CELLS * QUAD), 0).astype(F32) + float(part * THIRD)
            hot_ref[...] = jnp.where(want == row, 1.0, 0.0).astype(BF16)
            got = jnp.dot(hot_ref[...], rhs, preferred_element_type=F32)
            start = pl.multiple_of(plane * FACE + part * THIRD, 16)
            out_ref[pl.ds(start, THIRD), :] = got.astype(BF16)
        return 0

    lax.fori_loop(0, EDGE, step, 0)


def hand_back(field, connectivity):
    index = connectivity.reshape(CELLS, EDGE, QUAD).transpose(1, 0, 2).reshape(EDGE, CELLS * QUAD)
    return pl.pallas_call(
        return_kernel,
        name="hand_back",
        out_shape=jax.ShapeDtypeStruct((NODES, COLS), BF16),
        in_specs=[VMEM] * 2,
        out_specs=VMEM,
        scratch_shapes=[
            pltpu.VMEM((THIRD, CELLS * QUAD), BF16),
            pltpu.VMEM((CELLS * QUAD, COLS), F32),
            pltpu.VMEM((NODES, COLS), F32),
        ],
        compiler_params=BIG,
    )(field, index)


def product_kernel(states_ref, mixed_ref, position_ref, kept_ref, sent_ref, inner_ref, outer_ref):
    odd = position_ref[0] % 2 == 1
    for band in range(BANDS):
        rows = slice(band * COLS, (band + 1) * COLS)
        inner_ref[rows, :] = jnp.transpose(mixed_ref[band, OUTER_BLOCK : OUTER_BLOCK + INNER_BLOCK, :])
        outer_ref[rows, :] = jnp.transpose(mixed_ref[band, OUTER_BLOCK + INNER_BLOCK :, :])

    def step(i, _):
        inner = jnp.concatenate([states_ref[2 * i], states_ref[2 * i + 1]], axis=1)
        outer = jnp.concatenate([mixed_ref[2 * i, :OUTER_BLOCK, :], mixed_ref[2 * i + 1, :OUTER_BLOCK, :]], axis=1)
        product = jnp.dot(inner_ref[...], inner, preferred_element_type=F32)
        product += jnp.dot(outer_ref[...], outer, preferred_element_type=F32)
        half = COLS // 2
        for band in range(BANDS):
            for part in range(2):
                columns = slice(part * COLS, (part + 1) * COLS)
                first = product[band * COLS : band * COLS + half, columns]
                second = product[band * COLS + half : (band + 1) * COLS, columns]
                kept_ref[band, 2 * i + part] = jnp.where(odd, second, first).astype(BF16)
                sent_ref[band, 2 * i + part] = jnp.where(odd, first, second).astype(BF16)
        return 0

    lax.fori_loop(0, BANDS // 2, step, 0)


def project(states, mixed, position):
    count = lax.axis_size("space")
    halves = count // 2
    shape = jax.ShapeDtypeStruct((halves, BANDS, COLS // 2, COLS), BF16)
    kept, sent = pl.pallas_call(
        product_kernel,
        name="products",
        out_shape=(shape, shape),
        in_specs=[VMEM] * 2 + [SMEM],
        out_specs=(VMEM,) * 2,
        scratch_shapes=[
            pltpu.VMEM((BANDS * COLS, INNER_BLOCK), BF16),
            pltpu.VMEM((BANDS * COLS, OUTER_BLOCK), BF16),
        ],
        compiler_params=BIG,
    )(states, mixed, position)
    got = lax.ppermute(sent, "space", [(i, i ^ 1) for i in range(count)])
    both = (kept.astype(F32) + got.astype(F32)).astype(BF16).reshape(halves * BANDS, COLS // 2, COLS)
    groups = [[(2 * half + part) * BANDS + band for half in range(halves) for band in range(BANDS)] for part in range(2)]
    arrived = lax.all_to_all(both, ("space", "band"), split_axis=0, concat_axis=0, tiled=True, axis_index_groups=groups)
    return arrived.astype(F32).sum(axis=0).T


def swap_faces(near, far):
    count = lax.axis_size("space")
    apart = [(i, i + 1) for i in range(1, count - 1, 2)]
    beside = [(i, i + 1) for i in range(0, count, 2)]
    both_ways = lambda pairs: pairs + [(j, i) for i, j in pairs]
    near, far = lax.optimization_barrier((near, far))
    from_near = lax.ppermute(near, "space", both_ways(beside))
    from_far = lax.ppermute(far, "space", both_ways(apart))
    return from_near, from_far


def local(states, potential, cell_matrix, cell_scale, connectivity, lower_bound, upper_bound):
    bounds = (lower_bound, upper_bound)
    position = lax.axis_index("space").astype(jnp.int32).reshape(1)
    count = lax.axis_size("space")
    field, pot, mat, full, inner, outer = gather(states, potential, connectivity, cell_matrix, bounds)
    near, far = first_faces(field, full, cell_scale, position)
    prev = None
    for stage in range(1, STEPS + 1):
        got = swap_faces(near, far)
        part, sums, *early = cells(stage, field, prev, pot, mat, inner, bounds, cell_scale)
        prev = field
        if early:
            got, early = lax.optimization_barrier((got, early))
        field, *plain, _, near, far = faces(stage, part, got, bounds, position, outer, cell_scale, sums)
    node_states = lax.all_to_all(
        early[0].reshape(BANDS, INNER_BLOCK, COLS), "band", split_axis=0, concat_axis=0, tiled=True)
    current, edge = plain
    got = swap_faces(near, far)
    part, blocks = cells(STEPS + 1, current, None, pot, mat, None, bounds, cell_scale, edge)
    blocks, = faces(STEPS + 1, part, got, bounds, position, blocks=blocks)
    blocks, current = lax.optimization_barrier((blocks, current))
    filtered = hand_back(current, connectivity)
    mixed = lax.all_to_all(blocks.reshape(BANDS, BLOCK, COLS), "band", split_axis=0, concat_axis=0, tiled=True)
    totals = project(node_states, mixed, position)
    global_count = FACE * ((EDGE - 1) * count + 1)
    return filtered, totals / global_count


def solution(mesh):
    placed = (P("space", "band"), P("space"), P(), P("space"), P("space", None), P(), P())
    return jax.shard_map(
        local,
        mesh=mesh,
        in_specs=placed,
        out_specs=(P("space", "band"), P("band", "space")),
        check_vma=False,
    )
```

time: 233 us -> 221 us (0.948)
  waiting for transfers between devices: 50.3 us -> 6.89 us
  blocking collectives: 0 us -> 38.3 us
  starting transfers between devices: 57.9 us -> 41.8 us
  Pallas kernels: 96.7 us -> 112 us
  matrix products: 5.4 us -> 0 us
    all_to_all x0 -> x1, blocking collectives: none -> 38.3 us  [local(): lax.all_to_all(blocks.reshape(BANDS, BLOCK, COLS), 'band', split_axis=0,...]
    all_to_all x2 -> x1, waiting for transfers between devices: 28.1 us -> 0.01 us  [local(): lax.all_to_all(early[0].reshape(BANDS, INNER_BLOCK, COLS), 'band', split_...]
    pallas_call x5, Pallas kernels: 33.7 us -> 51.2 us  [cells(): pl.pallas_call(functools.partial(cells_kernel, stage), name='cells', out_...]
    ppermute x5, waiting for transfers between devices: 18.1 us -> 1.23 us  [swap_faces(): from_far = lax.ppermute(far, 'space', both_ways(apart))]
    ppermute x5, starting transfers between devices: 29.9 us -> 23.3 us  [swap_faces(): from_far = lax.ppermute(far, 'space', both_ways(apart))]
    dot_general x1 -> x0, matrix products: 5.4 us -> none  [project(): lax.dot_general(images, states, (((0,), (0,)), ((), ())), preferred_eleme...]
    all_to_all x1, starting transfers between devices: 17 us -> 11.9 us  [project(): lax.all_to_all(both, ('space', 'band'), split_axis=0, concat_axis=0, tile...]
    all_to_all x2 -> x1, starting transfers between devices: 9 us -> 4.47 us  [local(): lax.all_to_all(early[0].reshape(BANDS, INNER_BLOCK, COLS), 'band', split_...]
  transfers between devices with their start and end apart: 14 -> 13, of which waited for: 8 -> 3; matrix products, arithmetic and copies ran while one was open for 0% -> 0% of each run, Pallas kernels for 24% -> 33%
where the time goes in v3:
time: 221 us; the launch traced here: 220 us
  Pallas kernels  112 us (51%)
  starting transfers between devices  41.8 us (19%)
  blocking collectives  38.3 us (17%)
  local copies, waits for them, and re-layouts  15.3 us (7%)
  waiting for transfers between devices  6.89 us (3%)
  other arithmetic  3.4 us (2%)
  between operations  2.28 us (1%)
    pallas_call x5, Pallas kernels, cells(): pl.pallas_call(functools.partial(cells_kernel, stage), name='cells', out_...  51.2 us
    all_to_all x1, blocking collectives, local(): lax.all_to_all(blocks.reshape(BANDS, BLOCK, COLS), 'band', split_axis=0,...  38.3 us
    ppermute x5, starting transfers between devices, swap_faces(): from_far = lax.ppermute(far, 'space', both_ways(apart))  23.3 us
    pallas_call x5, Pallas kernels, faces(): pl.pallas_call(functools.partial(faces_kernel, stage), name='faces', out_...  22.5 us
    pallas_call x1, Pallas kernels, hand_back(): pl.pallas_call(return_kernel, name='hand_back', out_shape=jax.ShapeDtypeS...  14.6 us
    pallas_call x1, Pallas kernels, gather(): pl.pallas_call(gather_kernel, name='gather_states', out_shape=(pltpu.VMEM...  14.5 us
    unnamed x28, local copies, waits for them, and re-layouts  14.2 us
    all_to_all x1, starting transfers between devices, project(): lax.all_to_all(both, ('space', 'band'), split_axis=0, concat_axis=0, tile...  11.9 us
  transfers between devices with their start and end apart: 13, of which 3 were waited for; matrix products, arithmetic and copies ran while one was open for 0% of the time, Pallas kernels for 33%

profile of v3, /device:TPU:1, one launch (start us, length us, event | category | flops | bytes accessed | tf_op | source)
XLA Modules:
  0.0 219.9 jit_solution(2705113305751955562)
XLA Ops:
  2.8 1.7 copy-done.5
  6.5 14.5 %gather_states.1 = (f32[10368,128]{1,0:T(8,128)S(1)}, f32[10368,128]{1,0:T(8,128)S(1)}, bf16[512,512]{1,0:T(8,128)(2,1)S(1)}, bf16[128,512]{1,0:T(8,128)(2,1)S(1...) custom-call(bf16[10368,128]{1,0:T(8,128)(2,1)S(1)} %copy-done.5, f32[8,1296]{1,0:T(8,128)S(1)} %reshape.25.pot_ref, ...), custom_call_target="tpu_custom_call" | custom-call | tf_op jit(solution)/shard_map/gather_states/pallas_call | solution.py:114
  21.0 3.6 %first_faces.1 = (bf16[1296,128]{1,0:T(8,128)(2,1)S(1)}, bf16[1296,128]{1,0:T(8,128)(2,1)S(1)}) custom-call(f32[10368,128]{1,0:T(8,128)S(1)} %get-tuple-element.49.field_ref.refs_0_, bf16[128,512]{1,0:T(8,128)(2,1)S(1)} %get-tuple-element.54.full_ref, f32[25]{0:T(128)S(1)} %copy-done.13, s32[1]{0:T(128)} %bitcast.position_ref.refs_5_), custom_call_target="tpu_custom_call" | custom-call | tf_op jit(solution)/shard_map/first_faces/pallas_call | solution.py:204
  24.6 1.5 collective-permute-start
  26.0 5.5 %collective-permute-start.1 = (bf16[1296,128]{1,0:T(8,128)(2,1)S(1)}, bf16[1296,128]{1,0:T(8,128)(2,1)S(1)}, u32[]{:S(2)}, u32[]{:S(2)}) collective-permute-start(bf16[1296,128]{1,0:T(8,128)(2,1)S(1)} %get-tuple-element.56), channel_id=1, source_target_pairs={{8,16},{24,32},{40,48},{56,64},{72,80},{88,96},{104,112},{16,8},{3... | collective-permute-start | bytes 995336 | tf_op jit(solution)/shard_map/ppermute | solution.py:543
  31.6 9.9 %cells.5 = (f32[10368,128]{1,0:T(8,128)S(1)}, f32[2592,128]{1,0:T(8,128)S(1)}) custom-call(f32[10368,128]{1,0:T(8,128)S(1)} %get-tuple-element.49.field_ref.refs_0_, f32[10368,128]{1,0:T(8,128)S(1)} %get-tuple-element.50.refs_0_.refs_1_, bf16[512,512]{1,0:T(8,128)(2,1)S(1)} %get-tuple-element.51.refs_1_.refs_2_, ...), custom_call_target="tpu_custom_call" | custom-call | tf_op jit(solution)/shard_map/cells/pallas_call | solution.py:431
  41.4 5.0 %faces.5 = (f32[10368,128]{1,0:T(8,128)S(1)}, f32[2592,128]{1,0:T(8,128)S(1)}, bf16[1296,128]{1,0:T(8,128)(2,1)S(1)}, bf16[1296,128]{1,0:T(8,128)(2,1)S(1)}) custom-call(f32[10368,128]{1,0:T(8,128)S(1)} %get-tuple-element.53.refs_0_, bf16[1296,128]{1,0:T(8,128)(2,1)S(1)} %collective-permute-done.refs_1_, ...), custom_call_target="tpu_custom_call", output_to_operand_aliasing={{0}: (0, {}), {1}: (8, {})} | custom-call | tf_op jit(solution)/shard_map/faces/pallas_call | solution.py:337
  46.5 3.6 %collective-permute-start.3 = (bf16[1296,128]{1,0:T(8,128)(2,1)S(1)}, bf16[1296,128]{1,0:T(8,128)(2,1)S(1)}, u32[]{:S(2)}, u32[]{:S(2)}) collective-permute-start(bf16[1296,128]{1,0:T(8,128)(2,1)S(1)} %get-tuple-element.64), channel_id=1, source_target_pairs={{8,16},{24,32},{40,48},{56,64},{72,80},{88,96},{104,112},{16,8},{3... | collective-permute-start | bytes 995336 | tf_op jit(solution)/shard_map/ppermute | solution.py:543
  50.1 9.3 %cells.6 = (f32[10368,128]{1,0:T(8,128)S(1)}, f32[2592,128]{1,0:T(8,128)S(1)}) custom-call(f32[10368,128]{1,0:T(8,128)S(1)} %get-tuple-element.59.field_ref.refs_0_, f32[10368,128]{1,0:T(8,128)S(1)} %get-tuple-element.49.field_ref.refs_0_, f32[10368,128]{1,0:T(8,128)S(1)} %get-tuple-element.50.refs_0_.refs_1_, ...), custom_call_target="tpu_custom_call", output_to_operand_aliasing={{0}: (1, {})} | custom-call | tf_op jit(solution)/shard_map/cells/pallas_call | solution.py:431
  59.5 5.0 %faces.6 = (f32[10368,128]{1,0:T(8,128)S(1)}, f32[2592,128]{1,0:T(8,128)S(1)}, bf16[1296,128]{1,0:T(8,128)(2,1)S(1)}, bf16[1296,128]{1,0:T(8,128)(2,1)S(1)}) custom-call(f32[10368,128]{1,0:T(8,128)S(1)} %get-tuple-element.60.refs_0_, bf16[1296,128]{1,0:T(8,128)(2,1)S(1)} %collective-permute-done.2.refs_1_, ...), custom_call_target="tpu_custom_call", output_to_operand_aliasing={{0}: (0, {}), {1}: (8, {})} | custom-call | tf_op jit(solution)/shard_map/faces/pallas_call | solution.py:337
  64.5 4.9 %collective-permute-start.5 = (bf16[1296,128]{1,0:T(8,128)(2,1)S(1)}, bf16[1296,128]{1,0:T(8,128)(2,1)S(1)}, u32[]{:S(2)}, u32[]{:S(2)}) collective-permute-start(bf16[1296,128]{1,0:T(8,128)(2,1)S(1)} %get-tuple-element.71), channel_id=1, source_target_pairs={{8,16},{24,32},{40,48},{56,64},{72,80},{88,96},{104,112},{16,8},{3... | collective-permute-start | bytes 995336 | tf_op jit(solution)/shard_map/ppermute | solution.py:543
  69.5 9.3 %cells.7 = (f32[10368,128]{1,0:T(8,128)S(1)}, f32[2592,128]{1,0:T(8,128)S(1)}) custom-call(f32[10368,128]{1,0:T(8,128)S(1)} %get-tuple-element.66.field_ref.refs_0_, f32[10368,128]{1,0:T(8,128)S(1)} %get-tuple-element.59.field_ref.refs_0_, f32[10368,128]{1,0:T(8,128)S(1)} %get-tuple-element.50.refs_0_.refs_1_, ...), custom_call_target="tpu_custom_call", output_to_operand_aliasing={{0}: (1, {})} | custom-call | tf_op jit(solution)/shard_map/cells/pallas_call | solution.py:431
  78.8 5.0 %faces.7 = (f32[10368,128]{1,0:T(8,128)S(1)}, f32[2592,128]{1,0:T(8,128)S(1)}, bf16[1296,128]{1,0:T(8,128)(2,1)S(1)}, bf16[1296,128]{1,0:T(8,128)(2,1)S(1)}) custom-call(f32[10368,128]{1,0:T(8,128)S(1)} %get-tuple-element.67.refs_0_, bf16[1296,128]{1,0:T(8,128)(2,1)S(1)} %collective-permute-done.4.refs_1_, ...), custom_call_target="tpu_custom_call", output_to_operand_aliasing={{0}: (0, {}), {1}: (8, {})} | custom-call | tf_op jit(solution)/shard_map/faces/pallas_call | solution.py:337
  83.9 4.5 %collective-permute-start.7 = (bf16[1296,128]{1,0:T(8,128)(2,1)S(1)}, bf16[1296,128]{1,0:T(8,128)(2,1)S(1)}, u32[]{:S(2)}, u32[]{:S(2)}) collective-permute-start(bf16[1296,128]{1,0:T(8,128)(2,1)S(1)} %get-tuple-element.78), channel_id=1, source_target_pairs={{8,16},{24,32},{40,48},{56,64},{72,80},{88,96},{104,112},{16,8},{3... | collective-permute-start | bytes 995336 | tf_op jit(solution)/shard_map/ppermute | solution.py:543
  88.4 11.3 %cells.8 = (f32[10368,128]{1,0:T(8,128)S(1)}, f32[2592,128]{1,0:T(8,128)S(1)}, bf16[7808,128]{1,0:T(8,128)(2,1)}) custom-call(f32[10368,128]{1,0:T(8,128)S(1)} %get-tuple-element.73.field_ref, f32[10368,128]{1,0:T(8,128)S(1)} %get-tuple-element.66.field_ref.refs_0_, ...), custom_call_target="tpu_custom_call", output_to_operand_aliasing={{0}: (1, {})} | custom-call | tf_op jit(solution)/shard_map/cells/pallas_call | solution.py:431
  99.7 2.4 %copy-done = f32[10368,128]{1,0:T(8,128)} copy-done((f32[10368,128]{1,0:T(8,128)}, f32[10368,128]{1,0:T(8,128)S(1)}, u32[]{:S(2)}) %copy-start) | copy-done | bytes 5308440
  103.9 4.5 %all-to-all-start = ((bf16[8,976,128]{2,1,0:T(8,128)(2,1)}), bf16[8,976,128]{2,1,0:T(8,128)(2,1)}, u32[]{:S(2)}, u32[]{:S(2)}) async-start(bf16[8,976,128]{2,1,0:T(8,128)(2,1)} %bitcast.2), calls=%async_computation | async-start | bytes 3997696 | tf_op jit(solution)/shard_map/all_to_all | solution.py:561
  108.4 2.5 %copy-done.1 = f32[10368,128]{1,0:T(8,128)S(1)} copy-done((f32[10368,128]{1,0:T(8,128)S(1)}, f32[10368,128]{1,0:T(8,128)}, u32[]{:S(2)}) %copy-start.1) | copy-done | bytes 5308440
  110.9 1.3 copy-done.7
  113.2 5.8 %faces.8 = (f32[10368,128]{1,0:T(8,128)S(1)}, bf16[10368,128]{1,0:T(8,128)(2,1)S(1)}, bf16[2048,128]{1,0:T(8,128)(2,1)S(1)}, f32[2592,128]{1,0:T(8,128)S(1)}, bf...) custom-call(f32[10368,128]{1,0:T(8,128)S(1)} %copy-done.1, ...), custom_call_target="tpu_custom_call", output_to_operand_aliasing={{0}: (0, {}), {3}: (8, {})} | custom-call | tf_op jit(solution)/shard_map/faces/pallas_call | solution.py:337
  119.1 4.7 %collective-permute-start.9 = (bf16[1296,128]{1,0:T(8,128)(2,1)S(1)}, bf16[1296,128]{1,0:T(8,128)(2,1)S(1)}, u32[]{:S(2)}, u32[]{:S(2)}) collective-permute-start(bf16[1296,128]{1,0:T(8,128)(2,1)S(1)} %get-tuple-element.89), channel_id=1, source_target_pairs={{8,16},{24,32},{40,48},{56,64},{72,80},{88,96},{104,112},{16,8},{3... | collective-permute-start | bytes 995336 | tf_op jit(solution)/shard_map/ppermute | solution.py:543
  123.8 11.3 %cells.9 = (f32[10368,128]{1,0:T(8,128)S(1)}, bf16[11904,128]{1,0:T(8,128)(2,1)S(1)}) custom-call(bf16[10368,128]{1,0:T(8,128)(2,1)S(1)} %get-tuple-element.91.field_ref.plain_ref, f32[10368,128]{1,0:T(8,128)S(1)} %copy-done.3, bf16[512,512]{1,0:T(8,128)(2,1)S(1)} %get-tuple-element.51.refs_1_.refs_2_, bf16[2048,128]{1,0:T(8,128)(2,1)S(1)} %get-tuple-element.84.refs_2_, ...), custom_call_target="tpu_custom_call" | custom-call | tf_op jit(solution)/shard_map/cells/pallas_call | solution.py:431
  136.4 1.8 faces.9
  138.2 1.6 copy-done.4
  139.8 38.3 %all_to_all.15.mixed_ref = bf16[8,1488,128]{2,1,0:T(8,128)(2,1)S(1)} all-to-all(bf16[8,1488,128]{2,1,0:T(8,128)(2,1)} %bitcast.9), channel_id=1, replica_groups=mesh['space'=16,'band'=8] {'band'}, dimensions={0} | all-to-all | bytes 6094848 | tf_op jit(solution)/shard_map/all_to_all | solution.py:569
  178.1 5.7 %products.1 = (bf16[8,8,64,128]{3,2,1,0:T(8,128)(2,1)S(1)}, bf16[8,8,64,128]{3,2,1,0:T(8,128)(2,1)S(1)}) custom-call(bf16[8,976,128]{2,1,0:T(8,128)(2,1)} %all-to-all-done.states_ref, bf16[8,1488,128]{2,1,0:T(8,128)(2,1)S(1)} %all_to_all.15.mixed_ref, s32[1]{0:T(128)} %bitcast.position_ref.refs_5_), custom_call_target="tpu_custom_call" | custom-call | tf_op jit(solution)/shard_map/products/pallas_call | solution.py:517
  184.1 2.6 %collective-permute-done.10 = bf16[8,8,64,128]{3,2,1,0:T(8,128)(2,1)S(1)} collective-permute-done((bf16[8,8,64,128]{3,2,1,0:T(8,128)(2,1)S(1)}, bf16[8,8,64,128]{3,2,1,0:T(8,128)(2,1)S(1)}, u32[]{:S(2)}, u32[]{:S(2)}) %collective-permute-start.10) | collective-permute-done | bytes 1048608 | tf_op jit(solution)/shard_map/ppermute | solution.py:529
  186.7 1.4 add_convert_fusion
  188.1 11.9 %all-to-all-start.2 = ((bf16[64,64,128]{2,1,0:T(8,128)(2,1)}), bf16[64,64,128]{2,1,0:T(8,128)(2,1)}, u32[]{:S(2)}, u32[]{:S(2)}) async-start(bf16[64,64,128]{2,1,0:T(8,128)(2,1)} %bitcast.10), calls=%async_computation.2 | async-start | bytes 2097152 | tf_op jit(solution)/shard_map/all_to_all | solution.py:532
  200.3 14.6 %hand_back.1 = bf16[10368,128]{1,0:T(8,128)(2,1)} custom-call(bf16[10368,128]{1,0:T(8,128)(2,1)S(1)} %get-tuple-element.91.field_ref.plain_ref, s32[8,1600]{1,0:T(8,128)S(1)} %reshape.28.index_ref), custom_call_target="tpu_custom_call" | custom-call | tf_op jit(solution)/shard_map/hand_back/pallas_call | solution.py:473
  214.8 3.0 %all-to-all-done.2 = bf16[64,64,128]{2,1,0:T(8,128)(2,1)} async-done(((bf16[64,64,128]{2,1,0:T(8,128)(2,1)}), bf16[64,64,128]{2,1,0:T(8,128)(2,1)}, u32[]{:S(2)}, u32[]{:S(2)}) %all-to-all-start.2) | async-done | bytes 1048608 | tf_op jit(solution)/shard_map/all_to_all | solution.py:532
  217.8 1.4 convert_reduce_fusion
  (44 shorter events, 8.2 us)
Async XLA Ops:
  0.6 20.3 %copy-start.13 = (f32[25]{0:T(128)S(1)}, f32[25]{0:T(128)}, u32[]{:S(2)}) copy-start(f32[25]{0:T(128)} %refs_5_.6) | copy-start | bytes 304
  2.8 1.8 copy-start.5
  4.6 1.0 copy-start.8
  5.6 0.8 copy-start.11
  21.0 67.4 %copy-start.2 = (f32[10368,128]{1,0:T(8,128)}, f32[10368,128]{1,0:T(8,128)S(1)}, u32[]{:S(2)}) copy-start(f32[10368,128]{1,0:T(8,128)S(1)} %get-tuple-element.50.refs_0_.refs_1_) | copy-start | bytes 15925252
  24.6 16.9 %collective-permute-start = (bf16[1296,128]{1,0:T(8,128)(2,1)S(1)}, bf16[1296,128]{1,0:T(8,128)(2,1)S(1)}, u32[]{:S(2)}, u32[]{:S(2)}) collective-permute-start(bf16[1296,128]{1,0:T(8,128)(2,1)S(1)} %get-tuple-element.55), channel_id=1, source_target_pairs={{0,8},{16,24},{32,40},{48,56},{64,72},{80,88},{96,104},{112,120},{... | collective-permute-start | bytes 995336 | tf_op jit(solution)/shard_map/ppermute | solution.py:542
  26.0 15.4 %collective-permute-start.1 = (bf16[1296,128]{1,0:T(8,128)(2,1)S(1)}, bf16[1296,128]{1,0:T(8,128)(2,1)S(1)}, u32[]{:S(2)}, u32[]{:S(2)}) collective-permute-start(bf16[1296,128]{1,0:T(8,128)(2,1)S(1)} %get-tuple-element.56), channel_id=1, source_target_pairs={{8,16},{24,32},{40,48},{56,64},{72,80},{88,96},{104,112},{16,8},{3... | collective-permute-start | bytes 995336 | tf_op jit(solution)/shard_map/ppermute | solution.py:543
  46.4 13.0 %collective-permute-start.2 = (bf16[1296,128]{1,0:T(8,128)(2,1)S(1)}, bf16[1296,128]{1,0:T(8,128)(2,1)S(1)}, u32[]{:S(2)}, u32[]{:S(2)}) collective-permute-start(bf16[1296,128]{1,0:T(8,128)(2,1)S(1)} %get-tuple-element.63), channel_id=1, source_target_pairs={{0,8},{16,24},{32,40},{48,56},{64,72},{80,88},{96,104},{112,120},{... | collective-permute-start | bytes 995336 | tf_op jit(solution)/shard_map/ppermute | solution.py:542
  46.5 13.0 %collective-permute-start.3 = (bf16[1296,128]{1,0:T(8,128)(2,1)S(1)}, bf16[1296,128]{1,0:T(8,128)(2,1)S(1)}, u32[]{:S(2)}, u32[]{:S(2)}) collective-permute-start(bf16[1296,128]{1,0:T(8,128)(2,1)S(1)} %get-tuple-element.64), channel_id=1, source_target_pairs={{8,16},{24,32},{40,48},{56,64},{72,80},{88,96},{104,112},{16,8},{3... | collective-permute-start | bytes 995336 | tf_op jit(solution)/shard_map/ppermute | solution.py:543
  64.4 14.4 %collective-permute-start.4 = (bf16[1296,128]{1,0:T(8,128)(2,1)S(1)}, bf16[1296,128]{1,0:T(8,128)(2,1)S(1)}, u32[]{:S(2)}, u32[]{:S(2)}) collective-permute-start(bf16[1296,128]{1,0:T(8,128)(2,1)S(1)} %get-tuple-element.70), channel_id=1, source_target_pairs={{0,8},{16,24},{32,40},{48,56},{64,72},{80,88},{96,104},{112,120},{... | collective-permute-start | bytes 995336 | tf_op jit(solution)/shard_map/ppermute | solution.py:542
  64.5 14.3 %collective-permute-start.5 = (bf16[1296,128]{1,0:T(8,128)(2,1)S(1)}, bf16[1296,128]{1,0:T(8,128)(2,1)S(1)}, u32[]{:S(2)}, u32[]{:S(2)}) collective-permute-start(bf16[1296,128]{1,0:T(8,128)(2,1)S(1)} %get-tuple-element.71), channel_id=1, source_target_pairs={{8,16},{24,32},{40,48},{56,64},{72,80},{88,96},{104,112},{16,8},{3... | collective-permute-start | bytes 995336 | tf_op jit(solution)/shard_map/ppermute | solution.py:543
  83.8 19.4 %collective-permute-start.6 = (bf16[1296,128]{1,0:T(8,128)(2,1)S(1)}, bf16[1296,128]{1,0:T(8,128)(2,1)S(1)}, u32[]{:S(2)}, u32[]{:S(2)}) collective-permute-start(bf16[1296,128]{1,0:T(8,128)(2,1)S(1)} %get-tuple-element.77), channel_id=1, source_target_pairs={{0,8},{16,24},{32,40},{48,56},{64,72},{80,88},{96,104},{112,120},{... | collective-permute-start | bytes 995336 | tf_op jit(solution)/shard_map/ppermute | solution.py:542
  83.9 19.3 %collective-permute-start.7 = (bf16[1296,128]{1,0:T(8,128)(2,1)S(1)}, bf16[1296,128]{1,0:T(8,128)(2,1)S(1)}, u32[]{:S(2)}, u32[]{:S(2)}) collective-permute-start(bf16[1296,128]{1,0:T(8,128)(2,1)S(1)} %get-tuple-element.78), channel_id=1, source_target_pairs={{8,16},{24,32},{40,48},{56,64},{72,80},{88,96},{104,112},{16,8},{3... | collective-permute-start | bytes 995336 | tf_op jit(solution)/shard_map/ppermute | solution.py:543
  99.7 2.4 %copy-start = (f32[10368,128]{1,0:T(8,128)}, f32[10368,128]{1,0:T(8,128)S(1)}, u32[]{:S(2)}) copy-start(f32[10368,128]{1,0:T(8,128)S(1)} %get-tuple-element.74.refs_0_) | copy-start | bytes 15925252
  102.1 1.1 copy-start.6
  103.2 0.7 copy-start.9
  103.9 35.9 %all-to-all-start = ((bf16[8,976,128]{2,1,0:T(8,128)(2,1)}), bf16[8,976,128]{2,1,0:T(8,128)(2,1)}, u32[]{:S(2)}, u32[]{:S(2)}) async-start(bf16[8,976,128]{2,1,0:T(8,128)(2,1)} %bitcast.2), calls=%async_computation | async-start | bytes 3997696 | tf_op jit(solution)/shard_map/all_to_all | solution.py:561
  108.4 2.5 %copy-start.1 = (f32[10368,128]{1,0:T(8,128)S(1)}, f32[10368,128]{1,0:T(8,128)}, u32[]{:S(2)}) copy-start(f32[10368,128]{1,0:T(8,128)} %copy-done) | copy-start | bytes 15925252
  110.9 1.3 copy-start.7
  112.2 1.0 copy-start.10
  113.2 10.6 %copy-start.3 = (f32[10368,128]{1,0:T(8,128)S(1)}, f32[10368,128]{1,0:T(8,128)}, u32[]{:S(2)}) copy-start(f32[10368,128]{1,0:T(8,128)} %copy-done.2) | copy-start | bytes 15925252
  119.0 16.2 %collective-permute-start.8 = (bf16[1296,128]{1,0:T(8,128)(2,1)S(1)}, bf16[1296,128]{1,0:T(8,128)(2,1)S(1)}, u32[]{:S(2)}, u32[]{:S(2)}) collective-permute-start(bf16[1296,128]{1,0:T(8,128)(2,1)S(1)} %get-tuple-element.88), channel_id=1, source_target_pairs={{0,8},{16,24},{32,40},{48,56},{64,72},{80,88},{96,104},{112,120},{... | collective-permute-start | bytes 995336 | tf_op jit(solution)/shard_map/ppermute | solution.py:542
  119.1 17.3 %collective-permute-start.9 = (bf16[1296,128]{1,0:T(8,128)(2,1)S(1)}, bf16[1296,128]{1,0:T(8,128)(2,1)S(1)}, u32[]{:S(2)}, u32[]{:S(2)}) collective-permute-start(bf16[1296,128]{1,0:T(8,128)(2,1)S(1)} %get-tuple-element.89), channel_id=1, source_target_pairs={{8,16},{24,32},{40,48},{56,64},{72,80},{88,96},{104,112},{16,8},{3... | collective-permute-start | bytes 995336 | tf_op jit(solution)/shard_map/ppermute | solution.py:543
  138.2 1.6 copy-start.4
  183.8 16.3 %copy-start.12 = (s32[25,512]{1,0:T(8,128)S(1)}, s32[25,512]{1,0:T(8,128)}, u32[]{:S(2)}) copy-start(s32[25,512]{1,0:T(8,128)} %index_hbm.1) | copy-start | bytes 153604
  183.8 2.9 %collective-permute-start.10 = (bf16[8,8,64,128]{3,2,1,0:T(8,128)(2,1)S(1)}, bf16[8,8,64,128]{3,2,1,0:T(8,128)(2,1)S(1)}, u32[]{:S(2)}, u32[]{:S(2)}) collective-permute-start(bf16[8,8,64,128]{3,2,1,0:T(8,128)(2,1)S(1)} %get-tuple-element.95), channel_id=1, source_target_pairs={{0,8},{8,0},{16,24},{24,16},{32,40},{40,32},{48,56},{56,48},{64,72... | collective-permute-start | bytes 3145736 | tf_op jit(solution)/shard_map/ppermute | solution.py:529
  188.1 29.7 %all-to-all-start.2 = ((bf16[64,64,128]{2,1,0:T(8,128)(2,1)}), bf16[64,64,128]{2,1,0:T(8,128)(2,1)}, u32[]{:S(2)}, u32[]{:S(2)}) async-start(bf16[64,64,128]{2,1,0:T(8,128)(2,1)} %bitcast.10), calls=%async_computation.2 | async-start | bytes 2097152 | tf_op jit(solution)/shard_map/all_to_all | solution.py:532

commit v4 on v3

--- a/solution.py
+++ b/solution.py
@@ -110,6 +110,10 @@
     lax.fori_loop(0, EDGE, step, 0)
 
 
+def in_hbm(x):
+    return pltpu.with_memory_space_constraint(x, pltpu.HBM)
+
+
 def gather(states, potential, connectivity, matrix, bounds):
     return pl.pallas_call(
         gather_kernel,
@@ -134,7 +138,7 @@
             pltpu.SemaphoreType.DMA((3,)),
         ],
         compiler_params=BIG,
-    )(states, potential.reshape(EDGE, FACE), connectivity, matrix, *bounds)
+    )(in_hbm(states), potential.reshape(EDGE, FACE), in_hbm(connectivity), in_hbm(matrix), *bounds)
 
 
 def half_width_of(bounds):
@@ -156,6 +160,16 @@
         index = 2 * pair + half
         cell = jnp.minimum(index, CELLS - 1)
         yield half, cell // SLAB_XY, cell % SLAB_XY, jnp.where(index < CELLS, scale_ref[cell], 0.0)
+
+
+def for_pairs(work, group):
+    def step(i, _):
+        work(*[group * i + k for k in range(group)])
+        return 0
+
+    lax.fori_loop(0, PAIRS // group, step, 0)
+    if PAIRS % group:
+        work(*[jnp.int32(pair) for pair in range(PAIRS - PAIRS % group, PAIRS)])
 
 
 def cell_blocks(field_ref, pair, scale_ref):
@@ -181,13 +195,13 @@
 def spread_faces(field_ref, matrix_ref, scale_ref, sums_ref):
     sums_ref[...] = jnp.zeros_like(sums_ref)
 
-    def step(pair, _):
-        blocks = cell_blocks(field_ref, pair, scale_ref)
-        product = jnp.dot(matrix_ref[...], blocks, preferred_element_type=F32)
-        add_faces(sums_ref, product, pair, scale_ref)
-        return 0
-
-    lax.fori_loop(0, PAIRS, step, 0)
+    def spread(*pairs):
+        blocks = [cell_blocks(field_ref, pair, scale_ref) for pair in pairs]
+        products = [jnp.dot(matrix_ref[...], block, preferred_element_type=F32) for block in blocks]
+        for pair, product in zip(pairs, products):
+            add_faces(sums_ref, product, pair, scale_ref)
+
+    for_pairs(spread, 3)
 
 
 def hand_out(sums_ref, odd, near_out, far_out):
@@ -232,7 +246,7 @@
             row = (i * 4 + part) * 16
             far = row < FACE
             near_at = (1 - odd) * FACE + odd * (FACE // 2) + row - FACE
-            at = jnp.where(far, odd * FACE + row, jnp.minimum(near_at, 2 * FACE))
+            at = jnp.where(far, odd * FACE + row, jnp.minimum(near_at, 2 * FACE - 16))
             value = face_ref[pl.ds(pl.multiple_of(at, EDGE), 16), :]
             if far_weight is not None:
                 value = value * jnp.where(far, far_weight, 1.0)
@@ -244,48 +258,39 @@
 
 
 def faces_kernel(stage, *refs):
-    emit, spread = stage >= STEPS, stage <= STEPS
+    late, spread = stage >= STEPS, stage <= STEPS
     refs = list(refs)
     field_ref, near_in, far_in, low_ref, high_ref, position_ref = refs[:6]
     refs = refs[6:]
     if spread:
         outer_ref, scale_ref, _ = refs[:3]
         refs = refs[3:]
-        out_ref = refs.pop(0)
-        if emit:
-            plain_ref, edge_ref = refs.pop(0), refs.pop(0)
-        sums_ref, near_out, far_out, face_ref = refs
+        if late:
+            face_ref, edge_ref, sums_ref, near_out, far_out = refs
+        else:
+            out_ref, sums_ref, near_out, far_out, face_ref = refs
     else:
-        _, block_ref, face_ref = refs
+        _, block_ref, face_ref, edge_ref, sems = refs
     odd = position_ref[0] % 2
     lead, _ = factors((low_ref, high_ref), stage)
-    ends = (position_ref[0] == 0) | (position_ref[0] == SLABS - 1)
-    far_weight = jnp.where(ends, 1.0, 0.5)
 
     def settle_rows(i, _):
         for face_in, plane, side in ((near_in, (EDGE - 1) * (1 - odd), 1 - odd), (far_in, (EDGE - 1) * odd, odd)):
             got = face_in[pl.ds(pl.multiple_of(i * GROUP, 16), GROUP), :].astype(F32)
             for part in range(GROUP // EDGE):
-                rows = pl.ds((i * (GROUP // EDGE) + part) * QUAD + plane, EDGE, stride=EDGE)
+                here = pl.ds(pl.multiple_of(side * FACE + i * GROUP + part * EDGE, EDGE), EDGE)
+                rows = here if late else pl.ds((i * (GROUP // EDGE) + part) * QUAD + plane, EDGE, stride=EDGE)
                 value = field_ref[rows, :] + lead * got[part * EDGE : (part + 1) * EDGE, :]
                 value = value.astype(BF16).astype(F32)
-                if spread:
+                if not late:
                     out_ref[rows, :] = value
-                face_ref[pl.ds(pl.multiple_of(side * FACE + i * GROUP + part * EDGE, EDGE), EDGE), :] = value
+                face_ref[here, :] = value
         return 0
 
     lax.fori_loop(0, FACE // GROUP, settle_rows, 0)
-    if not spread:
-
-        def put(row, value):
-            at = (row // OUTER_BLOCK) * BLOCK + OUTER_BLOCK + INNER_BLOCK + row % OUTER_BLOCK
-            block_ref[pl.ds(pl.multiple_of(at, 16), 16), :] = value
-
-        put_outer(face_ref, odd, far_weight, put)
-        return
     if spread:
 
-        def step(pair, _):
+        def face_blocks(pair):
             columns = []
             for half, cell_y, cell_x, _ in pair_cells(pair, scale_ref):
                 pieces = []
@@ -294,97 +299,138 @@
                         rows = pl.ds(side * FACE + ((EDGE - 1) * cell_y + j) * SIDE + (EDGE - 1) * cell_x, EDGE)
                         pieces.append(face_ref[rows, :])
                 columns.append(jnp.concatenate(pieces, axis=0).astype(BF16))
-            product = jnp.dot(outer_ref[...], jnp.concatenate(columns, axis=1), preferred_element_type=F32)
-            add_faces(sums_ref, product, pair, scale_ref)
-            return 0
-
-        lax.fori_loop(0, PAIRS, step, 0)
+            return jnp.concatenate(columns, axis=1)
+
+        def spread_outer(*pairs):
+            blocks = [face_blocks(pair) for pair in pairs]
+            products = [jnp.dot(outer_ref[...], block, preferred_element_type=F32) for block in blocks]
+            for pair, product in zip(pairs, products):
+                add_faces(sums_ref, product, pair, scale_ref)
+
+        for_pairs(spread_outer, 3)
         hand_out(sums_ref, odd, near_out, far_out)
-    if emit:
-
-        def emit_rows(i, _):
-            rows = pl.ds(pl.multiple_of(i * 2 * GROUP, 2 * GROUP), 2 * GROUP)
-            plain_ref[rows, :] = out_ref[rows, :].astype(BF16)
-            return 0
+    if late:
+        ends = (position_ref[0] == 0) | (position_ref[0] == SLABS - 1)
+        far_weight = jnp.where(ends, 1.0, 0.5)
 
         def put_edge(row, value):
             edge_ref[pl.ds(pl.multiple_of(row, 16), 16), :] = value
 
-        lax.fori_loop(0, NODES // (2 * GROUP), emit_rows, 0)
-        put_outer(face_ref, odd, None, put_edge)
+        put_outer(face_ref, odd, None if spread else far_weight, put_edge)
+    if not spread:
+        copies = [
+            pltpu.make_async_copy(
+                edge_ref.at[pl.ds(band * OUTER_BLOCK, OUTER_BLOCK), :],
+                block_ref.at[pl.ds(band * BLOCK + OUTER_BLOCK + INNER_BLOCK, OUTER_BLOCK), :],
+                sems.at[band],
+            )
+            for band in range(BANDS)
+        ]
+        for copy in copies:
+            copy.start()
+        for copy in copies:
+            copy.wait()
 
 
 def faces(stage, part, got, bounds, position, outer=None, scale=None, sums=None, blocks=None):
-    emit, spread = stage >= STEPS, stage <= STEPS
     args = [part, *got, *bounds, position]
     specs = [VMEM] * 3 + [SMEM] * 3
-    outs = []
-    if spread:
+    faces_shape = (2 * FACE, COLS)
+    scratch = []
+    if stage < STEPS:
+        outs = [pltpu.VMEM((NODES, COLS), F32), pltpu.VMEM(faces_shape, F32)]
+        aliases = {0: 0, 8: 1}
+        scratch = [pltpu.VMEM(faces_shape, F32)]
+    elif stage == STEPS:
+        outs = [
+            jax.ShapeDtypeStruct(faces_shape, F32),
+            jax.ShapeDtypeStruct((BANDS * OUTER_BLOCK, COLS), BF16),
+            jax.ShapeDtypeStruct(faces_shape, F32),
+        ]
+        aliases = {8: 2}
+    else:
+        args.append(in_hbm(blocks))
+        outs = [pltpu.HBM((BANDS * BLOCK, COLS), BF16)]
+        aliases = {6: 0}
+        scratch = [
+            pltpu.VMEM(faces_shape, F32),
+            pltpu.VMEM((BANDS * OUTER_BLOCK, COLS), BF16),
+            pltpu.SemaphoreType.DMA((BANDS,)),
+        ]
+    if stage <= STEPS:
         args += [outer, scale, sums]
         specs += [VMEM, SMEM, VMEM]
-        outs.append(pltpu.VMEM((NODES, COLS), F32))
-        if emit:
-            outs.append(jax.ShapeDtypeStruct((NODES, COLS), BF16))
-            outs.append(jax.ShapeDtypeStruct((BANDS * OUTER_BLOCK, COLS), BF16))
-        aliases = {0: 0, 8: len(outs)}
-        outs.append(pltpu.VMEM((2 * FACE, COLS), F32))
         outs += [jax.ShapeDtypeStruct((FACE, COLS), BF16)] * 2
     else:
-        args.append(blocks)
-        specs.append(VMEM)
-        outs.append(pltpu.VMEM((BANDS * BLOCK, COLS), BF16))
-        aliases = {6: 0}
+        specs.append(HBM)
     return pl.pallas_call(
         functools.partial(faces_kernel, stage),
         name="faces",
         out_shape=tuple(outs),
         in_specs=specs,
-        out_specs=(VMEM,) * len(outs),
-        scratch_shapes=[pltpu.VMEM((2 * FACE + 16, COLS), F32)],
+        out_specs=((VMEM,) * len(outs)) if stage <= STEPS else (HBM,),
+        scratch_shapes=scratch,
         input_output_aliases=aliases,
-        compiler_params=SMALL,
+        compiler_params=SMALL if stage < STEPS else BIG,
     )(*args)
 
 
-def cells_kernel(stage, field_ref, *refs):
+def rebuild(inner_ref, settled_ref, field_ref):
+    def nodes(i, _):
+        for part in range(3):
+            node = i * 48 + part * 16
+            for z in range(EDGE):
+                for k in (0, EDGE):
+                    if z in (0, EDGE - 1):
+                        at = pl.ds(pl.multiple_of((z // (EDGE - 1)) * FACE + node + k, EDGE), EDGE)
+                        value = settled_ref[at, :]
+                    elif k == 0:
+                        both = inner_ref[pl.ds(pl.multiple_of((z - 1) * FACE + node, 16), 16), :].astype(F32)
+                        value = both[:EDGE]
+                    else:
+                        value = both[EDGE:]
+                    field_ref[pl.ds((node + k) * EDGE + z, EDGE, stride=EDGE), :] = value
+        return 0
+
+    lax.fori_loop(0, FACE // 48, nodes, 0)
+
+
+def cells_kernel(stage, *refs):
     refs = list(refs)
-    in_place = 1 < stage <= STEPS
-    if in_place:
-        refs.pop(0)
-    pot_ref, mat_ref = refs.pop(0), refs.pop(0)
-    inner_ref = refs.pop(0) if stage <= STEPS else None
-    if stage > STEPS:
-        edge_ref = refs.pop(0)
-    low_ref, high_ref, scale_ref, out_ref = refs[:4]
-    bounds = (low_ref, high_ref)
-    if stage > STEPS:
-        plain_ref, field_ref, block_ref = field_ref, refs[5], refs[4]
+    last = stage > STEPS
+    if last:
+        (early_ref, settled_ref, edge_ref, pot_ref, mat_ref, low_ref, high_ref, scale_ref,
+         rim_ref, plain_ref, block_ref, field_ref, out_ref) = refs
         for band in range(BANDS):
             block_ref[band * BLOCK : band * BLOCK + OUTER_BLOCK, :] = (
                 edge_ref[band * OUTER_BLOCK : (band + 1) * OUTER_BLOCK, :])
-
-        def widen(i, _):
-            rows = pl.ds(pl.multiple_of(i * 2 * GROUP, 2 * GROUP), 2 * GROUP)
-            field_ref[rows, :] = plain_ref[rows, :].astype(F32)
-            return 0
-
-        lax.fori_loop(0, NODES // (2 * GROUP), widen, 0)
+        rebuild(early_ref, settled_ref, field_ref)
+    else:
+        field_ref = refs.pop(0)
+        if stage > 1:
+            refs.pop(0)
+        pot_ref, mat_ref, inner_ref, low_ref, high_ref, scale_ref, out_ref, sums_ref, *more = refs
+        if more:
+            early_ref, rim_ref = more
+    in_place = 1 < stage <= STEPS
+    bounds = (low_ref, high_ref)
     lead, _ = factors(bounds, stage)
     if in_place:
         lead = -lead
     else:
         out_ref[...] = jnp.zeros_like(out_ref)
 
-    def step(pair, _):
-        product = jnp.dot(mat_ref[...], cell_blocks(field_ref, pair, scale_ref), preferred_element_type=F32)
-        for half, cell_y, cell_x, scale in pair_cells(pair, scale_ref):
-            factor = lead * scale
-            for j in range(EDGE):
-                rows = pl.ds(pl.multiple_of(first_row(cell_y, cell_x, j), EDGE), QUAD)
-                out_ref[rows, :] += factor * product[j * QUAD : (j + 1) * QUAD, half * COLS : (half + 1) * COLS]
-        return 0
-
-    lax.fori_loop(0, PAIRS, step, 0)
+    def multiply(*pairs):
+        blocks = [cell_blocks(field_ref, pair, scale_ref) for pair in pairs]
+        products = [jnp.dot(mat_ref[...], block, preferred_element_type=F32) for block in blocks]
+        for pair, product in zip(pairs, products):
+            for half, cell_y, cell_x, scale in pair_cells(pair, scale_ref):
+                factor = lead * scale
+                for j in range(EDGE):
+                    rows = pl.ds(pl.multiple_of(first_row(cell_y, cell_x, j), EDGE), QUAD)
+                    out_ref[rows, :] += factor * product[j * QUAD : (j + 1) * QUAD, half * COLS : (half + 1) * COLS]
+
+    for_pairs(multiply, 4)
     plane = lax.broadcasted_iota(jnp.int32, (EDGE, COLS), 0)
     inside = (plane > 0) & (plane < EDGE - 1)
     half_width = half_width_of(bounds) * 0.5
@@ -396,7 +442,7 @@
             shifted = pot_ref[rows, :]
             if stage == 1:
                 shifted = shifted * 0.5
-            elif stage > STEPS:
+            elif last:
                 shifted = shifted * half_width + center
             value = shifted * field_ref[rows, :]
             value = value - out_ref[rows, :] if in_place else value + out_ref[rows, :]
@@ -406,38 +452,72 @@
     lax.fori_loop(0, NODES // GROUP, finish, 0)
 
     def put(row, value):
-        if stage == STEPS:
-            refs[5][pl.ds(pl.multiple_of(row, 16), 16), :] = value
-        else:
+        if last:
             at = (row // INNER_BLOCK) * BLOCK + OUTER_BLOCK + row % INNER_BLOCK
             block_ref[pl.ds(pl.multiple_of(at, 16), 16), :] = value
+        else:
+            early_ref[pl.ds(pl.multiple_of(row, 16), 16), :] = value
+
+    def put_rim(i, _):
+        for side in range(2):
+            for part in range(GROUP // EDGE):
+                node = i * GROUP + part * EDGE
+                rows = pl.ds(node * EDGE + side * (EDGE - 1), EDGE, stride=EDGE)
+                rim_ref[pl.ds(pl.multiple_of(side * FACE + node, EDGE), EDGE), :] = out_ref[rows, :]
+        return 0
 
     if stage >= STEPS:
         put_inner(out_ref, put)
-    if stage <= STEPS:
-        spread_faces(out_ref, inner_ref, scale_ref, refs[4])
-
-
-def cells(stage, field, prev, pot, mat, inner, bounds, scale, edge=None):
-    args = [field] + ([prev] if 1 < stage <= STEPS else []) + [pot, mat, inner if stage <= STEPS else edge]
-    specs = [VMEM] * len(args) + [SMEM] * 3
+        lax.fori_loop(0, FACE // GROUP, put_rim, 0)
+    if last:
+
+        def emit_rows(i, _):
+            rows = pl.ds(pl.multiple_of(i * 2 * GROUP, 2 * GROUP), 2 * GROUP)
+            plain_ref[rows, :] = field_ref[rows, :].astype(BF16)
+            return 0
+
+        lax.fori_loop(0, NODES // (2 * GROUP), emit_rows, 0)
+    else:
+        spread_faces(out_ref, inner_ref, scale_ref, sums_ref)
+
+
+def cells(stage, field, prev, pot, mat, inner, bounds, scale):
+    args = [field] + ([prev] if stage > 1 else []) + [pot, mat, inner]
+    faces_shape = (2 * FACE, COLS)
     outs = [pltpu.VMEM((NODES, COLS), F32)]
-    if stage <= STEPS:
-        outs.append(pltpu.VMEM((2 * FACE, COLS), F32))
-    if stage == STEPS:
-        outs.append(jax.ShapeDtypeStruct((BANDS * INNER_BLOCK, COLS), BF16))
-    if stage > STEPS:
-        outs.append(pltpu.VMEM((BANDS * BLOCK, COLS), BF16))
+    if stage < STEPS:
+        outs.append(pltpu.VMEM(faces_shape, F32))
+    else:
+        outs += [
+            pltpu.HBM(faces_shape, F32),
+            pltpu.HBM((BANDS * INNER_BLOCK, COLS), BF16),
+            pltpu.HBM(faces_shape, F32),
+        ]
     return pl.pallas_call(
         functools.partial(cells_kernel, stage),
         name="cells",
         out_shape=tuple(outs),
-        in_specs=specs,
+        in_specs=[VMEM] * len(args) + [SMEM] * 3,
         out_specs=(VMEM,) * len(outs),
-        scratch_shapes=[] if stage <= STEPS else [pltpu.VMEM((NODES, COLS), F32)],
-        input_output_aliases={1: 0} if 1 < stage <= STEPS else {},
-        compiler_params=SMALL if stage <= STEPS else BIG,
+        input_output_aliases={1: 0} if stage > 1 else {},
+        compiler_params=SMALL if stage < STEPS else BIG,
     )(*args, *bounds, scale)
+
+
+def last_cells(early, settled, edge, pot, mat, bounds, scale):
+    return pl.pallas_call(
+        functools.partial(cells_kernel, STEPS + 1),
+        name="last_cells",
+        out_shape=(
+            pltpu.VMEM((2 * FACE, COLS), F32),
+            jax.ShapeDtypeStruct((NODES, COLS), BF16),
+            jax.ShapeDtypeStruct((BANDS * BLOCK, COLS), BF16),
+        ),
+        in_specs=[VMEM] * 5 + [SMEM] * 3,
+        out_specs=(VMEM,) * 3,
+        scratch_shapes=[pltpu.VMEM((NODES, COLS), F32)] * 2,
+        compiler_params=pltpu.CompilerParams(vmem_limit_bytes=32 * 1024 * 1024),
+    )(early, settled, edge, pot, mat, *bounds, scale)
 
 
 def return_kernel(plain_ref, index_ref, out_ref, hot_ref, rhs_ref, field_ref):
@@ -485,7 +565,7 @@
     )(field, index)
 
 
-def product_kernel(states_ref, mixed_ref, position_ref, kept_ref, sent_ref, inner_ref, outer_ref):
+def product_kernel(factor, states_ref, mixed_ref, position_ref, kept_ref, sent_ref, inner_ref, outer_ref):
     odd = position_ref[0] % 2 == 1
     for band in range(BANDS):
         rows = slice(band * COLS, (band + 1) * COLS)
@@ -496,7 +576,7 @@
         inner = jnp.concatenate([states_ref[2 * i], states_ref[2 * i + 1]], axis=1)
         outer = jnp.concatenate([mixed_ref[2 * i, :OUTER_BLOCK, :], mixed_ref[2 * i + 1, :OUTER_BLOCK, :]], axis=1)
         product = jnp.dot(inner_ref[...], inner, preferred_element_type=F32)
-        product += jnp.dot(outer_ref[...], outer, preferred_element_type=F32)
+        product = (product + jnp.dot(outer_ref[...], outer, preferred_element_type=F32)) * factor
         half = COLS // 2
         for band in range(BANDS):
             for part in range(2):
@@ -513,9 +593,10 @@
 def project(states, mixed, position):
     count = lax.axis_size("space")
     halves = count // 2
+    factor = 1.0 / (FACE * ((EDGE - 1) * count + 1))
     shape = jax.ShapeDtypeStruct((halves, BANDS, COLS // 2, COLS), BF16)
     kept, sent = pl.pallas_call(
-        product_kernel,
+        functools.partial(product_kernel, factor),
         name="products",
         out_shape=(shape, shape),
         in_specs=[VMEM] * 2 + [SMEM],
@@ -551,25 +632,25 @@
     field, pot, mat, full, inner, outer = gather(states, potential, connectivity, cell_matrix, bounds)
     near, far = first_faces(field, full, cell_scale, position)
     prev = None
-    for stage in range(1, STEPS + 1):
+    for stage in range(1, STEPS):
         got = swap_faces(near, far)
-        part, sums, *early = cells(stage, field, prev, pot, mat, inner, bounds, cell_scale)
+        part, sums = cells(stage, field, prev, pot, mat, inner, bounds, cell_scale)
         prev = field
-        if early:
-            got, early = lax.optimization_barrier((got, early))
-        field, *plain, _, near, far = faces(stage, part, got, bounds, position, outer, cell_scale, sums)
+        field, _, near, far = faces(stage, part, got, bounds, position, outer, cell_scale, sums)
+    got = swap_faces(near, far)
+    _, sums, early, rim = cells(STEPS, field, prev, pot, mat, inner, bounds, cell_scale)
+    got, early = lax.optimization_barrier((got, early))
     node_states = lax.all_to_all(
-        early[0].reshape(BANDS, INNER_BLOCK, COLS), "band", split_axis=0, concat_axis=0, tiled=True)
-    current, edge = plain
+        early.reshape(BANDS, INNER_BLOCK, COLS), "band", split_axis=0, concat_axis=0, tiled=True)
+    settled, edge, _, near, far = faces(STEPS, rim, got, bounds, position, outer, cell_scale, sums)
     got = swap_faces(near, far)
-    part, blocks = cells(STEPS + 1, current, None, pot, mat, None, bounds, cell_scale, edge)
-    blocks, = faces(STEPS + 1, part, got, bounds, position, blocks=blocks)
+    rim, current, blocks = last_cells(early, settled, edge, pot, mat, bounds, cell_scale)
+    blocks, = faces(STEPS + 1, rim, got, bounds, position, blocks=blocks)
     blocks, current = lax.optimization_barrier((blocks, current))
     filtered = hand_back(current, connectivity)
     mixed = lax.all_to_all(blocks.reshape(BANDS, BLOCK, COLS), "band", split_axis=0, concat_axis=0, tiled=True)
     totals = project(node_states, mixed, position)
-    global_count = FACE * ((EDGE - 1) * count + 1)
-    return filtered, totals / global_count
+    return filtered, totals
 
 
 def solution(mesh):

time: 221 us -> 205 us (0.928)
  Pallas kernels: 112 us -> 94.1 us
  local copies, waits for them, and re-layouts: 15.3 us -> 7.97 us
  starting transfers between devices: 41.8 us -> 48.9 us
  waiting for transfers between devices: 6.89 us -> 11.3 us
    pallas_call x5 -> x4, Pallas kernels: 51.2 us -> 30 us  [cells(): pl.pallas_call(functools.partial(cells_kernel, stage), name='cells', out_...]
    pallas_call x1 -> x2, Pallas kernels: 5.7 us -> 16.8 us  [the longest x1 11.1 us: last_cells(): pl.pallas_call(functools.partial(cells_kernel, STEPS + 1), name='last_cel...]
    unnamed x28 -> x20, local copies, waits for them, and re-layouts: 14.2 us -> 6.9 us
    pallas_call x5, Pallas kernels: 22.5 us -> 15.5 us  [faces(): pl.pallas_call(functools.partial(faces_kernel, stage), name='faces', out_...]
    ppermute x5, starting transfers between devices: 23.3 us -> 28 us  [swap_faces(): from_far = lax.ppermute(far, 'space', both_ways(apart))]
    ppermute x5, waiting for transfers between devices: 1.23 us -> 5.63 us  [swap_faces(): from_far = lax.ppermute(far, 'space', both_ways(apart))]
    all_to_all x1, starting transfers between devices: 11.9 us -> 14.6 us  [project(): lax.all_to_all(both, ('space', 'band'), split_axis=0, concat_axis=0, tile...]
  transfers between devices with their start and end apart: 13 -> 13, of which waited for: 3 -> 6; matrix products, arithmetic and copies ran while one was open for 0% -> 0% of each run, Pallas kernels for 33% -> 29%
where the time goes in v4:
time: 205 us; the launch traced here: 204 us
  Pallas kernels  94.1 us (46%)
  starting transfers between devices  48.9 us (24%)
  blocking collectives  36.5 us (18%)
  waiting for transfers between devices  11.3 us (6%)
  local copies, waits for them, and re-layouts  7.97 us (4%)
  other arithmetic  3.37 us (2%)
  between operations  2.25 us (1%)
    all_to_all x1, blocking collectives, local(): lax.all_to_all(blocks.reshape(BANDS, BLOCK, COLS), 'band', split_axis=0,...  36.5 us
    pallas_call x4, Pallas kernels, cells(): pl.pallas_call(functools.partial(cells_kernel, stage), name='cells', out_...  30 us
    ppermute x5, starting transfers between devices, swap_faces(): from_far = lax.ppermute(far, 'space', both_ways(apart))  28 us
    pallas_call x5, Pallas kernels, faces(): pl.pallas_call(functools.partial(faces_kernel, stage), name='faces', out_...  15.5 us
    pallas_call x1, Pallas kernels, gather(): pl.pallas_call(gather_kernel, name='gather_states', out_shape=(pltpu.VMEM...  15 us
    pallas_call x1, Pallas kernels, hand_back(): pl.pallas_call(return_kernel, name='hand_back', out_shape=jax.ShapeDtypeS...  14.6 us
    all_to_all x1, starting transfers between devices, project(): lax.all_to_all(both, ('space', 'band'), split_axis=0, concat_axis=0, tile...  14.6 us
    pallas_call x1, Pallas kernels, last_cells(): pl.pallas_call(functools.partial(cells_kernel, STEPS + 1), name='last_cel...  11.1 us
  transfers between devices with their start and end apart: 13, of which 6 were waited for; matrix products, arithmetic and copies ran while one was open for 0% of the time, Pallas kernels for 29%

profile of v4, /device:TPU:1, one launch (start us, length us, event | category | flops | bytes accessed | tf_op | source)
XLA Modules:
  0.0 204.3 jit_solution(12936373860199553523)
XLA Ops:
  2.8 15.0 %gather_states.1 = (f32[10368,128]{1,0:T(8,128)S(1)}, f32[10368,128]{1,0:T(8,128)S(1)}, bf16[512,512]{1,0:T(8,128)(2,1)S(1)}, bf16[128,512]{1,0:T(8,128)(2,1)S(1...) custom-call(bf16[10368,128]{1,0:T(8,128)(2,1)} %states_hbm.1, f32[8,1296]{1,0:T(8,128)S(1)} %reshape.25.pot_ref, ...), custom_call_target="tpu_custom_call" | custom-call | tf_op jit(solution)/shard_map/gather_states/pallas_call | solution.py:118
  17.8 2.2 %first_faces.1 = (bf16[1296,128]{1,0:T(8,128)(2,1)S(1)}, bf16[1296,128]{1,0:T(8,128)(2,1)S(1)}) custom-call(f32[10368,128]{1,0:T(8,128)S(1)} %get-tuple-element.50.refs_0_.field_ref.refs_1_, bf16[128,512]{1,0:T(8,128)(2,1)S(1)} %get-tuple-element.55.full_ref, f32[25]{0:T(128)S(1)} %copy-done.8, s32[1]{0:T(128)} %bitcast.position_ref.refs_5_), custom_call_target="tpu_custom_call" | custom-call | tf_op jit(solution)/shard_map/first_faces/pallas_call | solution.py:218
  20.0 1.5 collective-permute-start
  21.5 5.5 %collective-permute-start.1 = (bf16[1296,128]{1,0:T(8,128)(2,1)S(1)}, bf16[1296,128]{1,0:T(8,128)(2,1)S(1)}, u32[]{:S(2)}, u32[]{:S(2)}) collective-permute-start(bf16[1296,128]{1,0:T(8,128)(2,1)S(1)} %get-tuple-element.57), channel_id=1, source_target_pairs={{8,16},{24,32},{40,48},{56,64},{72,80},{88,96},{104,112},{16,8},{3... | collective-permute-start | bytes 995336 | tf_op jit(solution)/shard_map/ppermute | solution.py:624
  27.0 7.1 %cells.4 = (f32[10368,128]{1,0:T(8,128)S(1)}, f32[2592,128]{1,0:T(8,128)S(1)}) custom-call(f32[10368,128]{1,0:T(8,128)S(1)} %get-tuple-element.50.refs_0_.field_ref.refs_1_, f32[10368,128]{1,0:T(8,128)S(1)} %get-tuple-element.51.refs_1_.refs_2_.refs_3_, bf16[512,512]{1,0:T(8,128)(2,1)S(1)} %get-tuple-element.52.refs_2_.refs_3_.refs_4_, ...), custom_call_target="tpu_custom_call" | custom-call | tf_op jit(solution)/shard_map/cells/pallas_call | solution.py:496
  34.6 3.7 %faces.5 = (f32[10368,128]{1,0:T(8,128)S(1)}, f32[2592,128]{1,0:T(8,128)S(1)}, bf16[1296,128]{1,0:T(8,128)(2,1)S(1)}, bf16[1296,128]{1,0:T(8,128)(2,1)S(1)}) custom-call(f32[10368,128]{1,0:T(8,128)S(1)} %get-tuple-element.54.refs_0_, bf16[1296,128]{1,0:T(8,128)(2,1)S(1)} %collective-permute-done.refs_1_, ...), custom_call_target="tpu_custom_call", output_to_operand_aliasing={{0}: (0, {}), {1}: (8, {})} | custom-call | tf_op jit(solution)/shard_map/faces/pallas_call | solution.py:366
  38.4 5.9 %collective-permute-start.3 = (bf16[1296,128]{1,0:T(8,128)(2,1)S(1)}, bf16[1296,128]{1,0:T(8,128)(2,1)S(1)}, u32[]{:S(2)}, u32[]{:S(2)}) collective-permute-start(bf16[1296,128]{1,0:T(8,128)(2,1)S(1)} %get-tuple-element.65), channel_id=1, source_target_pairs={{8,16},{24,32},{40,48},{56,64},{72,80},{88,96},{104,112},{16,8},{3... | collective-permute-start | bytes 995336 | tf_op jit(solution)/shard_map/ppermute | solution.py:624
  44.3 6.6 %cells.5 = (f32[10368,128]{1,0:T(8,128)S(1)}, f32[2592,128]{1,0:T(8,128)S(1)}) custom-call(f32[10368,128]{1,0:T(8,128)S(1)} %get-tuple-element.60.refs_0_.refs_1_, f32[10368,128]{1,0:T(8,128)S(1)} %get-tuple-element.50.refs_0_.field_ref.refs_1_, f32[10368,128]{1,0:T(8,128)S(1)} %get-tuple-element.51.refs_1_.refs_2_.refs_3_, ...), custom_call_target="tpu_custom_call", output_to_operand_aliasing={{0}: (1, {})} | custom-call | tf_op jit(solution)/shard_map/cells/pallas_call | solution.py:496
  51.9 3.7 %faces.6 = (f32[10368,128]{1,0:T(8,128)S(1)}, f32[2592,128]{1,0:T(8,128)S(1)}, bf16[1296,128]{1,0:T(8,128)(2,1)S(1)}, bf16[1296,128]{1,0:T(8,128)(2,1)S(1)}) custom-call(f32[10368,128]{1,0:T(8,128)S(1)} %get-tuple-element.61.refs_0_, bf16[1296,128]{1,0:T(8,128)(2,1)S(1)} %collective-permute-done.2.refs_1_, ...), custom_call_target="tpu_custom_call", output_to_operand_aliasing={{0}: (0, {}), {1}: (8, {})} | custom-call | tf_op jit(solution)/shard_map/faces/pallas_call | solution.py:366
  55.7 5.9 %collective-permute-start.5 = (bf16[1296,128]{1,0:T(8,128)(2,1)S(1)}, bf16[1296,128]{1,0:T(8,128)(2,1)S(1)}, u32[]{:S(2)}, u32[]{:S(2)}) collective-permute-start(bf16[1296,128]{1,0:T(8,128)(2,1)S(1)} %get-tuple-element.72), channel_id=1, source_target_pairs={{8,16},{24,32},{40,48},{56,64},{72,80},{88,96},{104,112},{16,8},{3... | collective-permute-start | bytes 995336 | tf_op jit(solution)/shard_map/ppermute | solution.py:624
  61.6 6.6 %cells.6 = (f32[10368,128]{1,0:T(8,128)S(1)}, f32[2592,128]{1,0:T(8,128)S(1)}) custom-call(f32[10368,128]{1,0:T(8,128)S(1)} %get-tuple-element.67.refs_0_.refs_1_, f32[10368,128]{1,0:T(8,128)S(1)} %get-tuple-element.60.refs_0_.refs_1_, f32[10368,128]{1,0:T(8,128)S(1)} %get-tuple-element.51.refs_1_.refs_2_.refs_3_, ...), custom_call_target="tpu_custom_call", output_to_operand_aliasing={{0}: (1, {})} | custom-call | tf_op jit(solution)/shard_map/cells/pallas_call | solution.py:496
  69.2 3.7 %faces.7 = (f32[10368,128]{1,0:T(8,128)S(1)}, f32[2592,128]{1,0:T(8,128)S(1)}, bf16[1296,128]{1,0:T(8,128)(2,1)S(1)}, bf16[1296,128]{1,0:T(8,128)(2,1)S(1)}) custom-call(f32[10368,128]{1,0:T(8,128)S(1)} %get-tuple-element.68.refs_0_, bf16[1296,128]{1,0:T(8,128)(2,1)S(1)} %collective-permute-done.4.refs_1_, ...), custom_call_target="tpu_custom_call", output_to_operand_aliasing={{0}: (0, {}), {1}: (8, {})} | custom-call | tf_op jit(solution)/shard_map/faces/pallas_call | solution.py:366
  73.0 6.1 %collective-permute-start.7 = (bf16[1296,128]{1,0:T(8,128)(2,1)S(1)}, bf16[1296,128]{1,0:T(8,128)(2,1)S(1)}, u32[]{:S(2)}, u32[]{:S(2)}) collective-permute-start(bf16[1296,128]{1,0:T(8,128)(2,1)S(1)} %get-tuple-element.77), channel_id=1, source_target_pairs={{8,16},{24,32},{40,48},{56,64},{72,80},{88,96},{104,112},{16,8},{3... | collective-permute-start | bytes 995336 | tf_op jit(solution)/shard_map/ppermute | solution.py:624
  79.1 9.7 %cells.7 = (f32[10368,128]{1,0:T(8,128)S(1)}, f32[2592,128]{1,0:T(8,128)}, bf16[7808,128]{1,0:T(8,128)(2,1)}, f32[2592,128]{1,0:T(8,128)}) custom-call(f32[10368,128]{1,0:T(8,128)S(1)} %get-tuple-element.78.refs_0_, f32[10368,128]{1,0:T(8,128)S(1)} %get-tuple-element.67.refs_0_.refs_1_, ...), custom_call_target="tpu_custom_call", output_to_operand_aliasing={{0}: (1, {})} | custom-call | tf_op jit(solution)/shard_map/cells/pallas_call | solution.py:496
  88.9 4.5 %all-to-all-start = ((bf16[8,976,128]{2,1,0:T(8,128)(2,1)}), bf16[8,976,128]{2,1,0:T(8,128)(2,1)}, u32[]{:S(2)}, u32[]{:S(2)}) async-start(bf16[8,976,128]{2,1,0:T(8,128)(2,1)} %bitcast.9), calls=%async_computation | async-start | bytes 3997696 | tf_op jit(solution)/shard_map/all_to_all | solution.py:643
  93.4 1.5 copy-done.6
  94.8 1.3 copy-done.7
  96.1 2.6 %faces.8 = (f32[2592,128]{1,0:T(8,128)S(1)}, bf16[2048,128]{1,0:T(8,128)(2,1)S(1)}, f32[2592,128]{1,0:T(8,128)S(1)}, bf16[1296,128]{1,0:T(8,128)(2,1)S(1)}, bf16[1296,128]{1,0:T(8,128)(2,1)S(1)}) custom-call(f32[2592,128]{1,0:T(8,128)S(1)} %copy-done.7, bf16[1296,128]{1,0:T(8,128)(2,1)S(1)} %collective-permute-done.6.refs_1_, ...), custom_call_target="tpu_custom_call", output_to_operand_aliasing={{2}: (8, {})} | custom-call | tf_op jit(solution)/shard_map/faces/pallas_call | solution.py:366
  98.8 4.6 %collective-permute-start.9 = (bf16[1296,128]{1,0:T(8,128)(2,1)S(1)}, bf16[1296,128]{1,0:T(8,128)(2,1)S(1)}, u32[]{:S(2)}, u32[]{:S(2)}) collective-permute-start(bf16[1296,128]{1,0:T(8,128)(2,1)S(1)} %get-tuple-element.91), channel_id=1, source_target_pairs={{8,16},{24,32},{40,48},{56,64},{72,80},{88,96},{104,112},{16,8},{3... | collective-permute-start | bytes 995336 | tf_op jit(solution)/shard_map/ppermute | solution.py:624
  103.5 2.5 %copy-done.1 = f32[10368,128]{1,0:T(8,128)S(1)} copy-done((f32[10368,128]{1,0:T(8,128)S(1)}, f32[10368,128]{1,0:T(8,128)}, u32[]{:S(2)}) %copy-start.1) | copy-done | bytes 5308440
  106.0 11.1 %last_cells.1 = (f32[2592,128]{1,0:T(8,128)S(1)}, bf16[10368,128]{1,0:T(8,128)(2,1)S(1)}, bf16[11904,128]{1,0:T(8,128)(2,1)S(1)}) custom-call(bf16[7808,128]{1,0:T(8,128)(2,1)S(1)} %copy-done.3, f32[2592,128]{1,0:T(8,128)S(1)} %get-tuple-element.85.refs_1_, bf16[2048,128]{1,0:T(8,128)(2,1)S(1)} %get-tuple-element.86.refs_2_, f32[10368,128]{1,0:T(8,128)S(1)} %copy-done.1, ...), custom_call_target="tpu_custom_call" | custom-call | tf_op jit(solution)/shard_map/last_cells/pallas_call | solution.py:508
  117.1 1.6 copy-done.2
  118.7 3.1 %collective-permute-done.9.refs_2_ = bf16[1296,128]{1,0:T(8,128)(2,1)S(1)} collective-permute-done((bf16[1296,128]{1,0:T(8,128)(2,1)S(1)}, bf16[1296,128]{1,0:T(8,128)(2,1)S(1)}, u32[]{:S(2)}, u32[]{:S(2)}) %collective-permute-start.9) | collective-permute-done | bytes 331808 | tf_op jit(solution)/shard_map/ppermute | solution.py:624
  121.8 1.8 faces.9
  123.7 36.5 %all_to_all.15.mixed_ref = bf16[8,1488,128]{2,1,0:T(8,128)(2,1)S(1)} all-to-all(bf16[8,1488,128]{2,1,0:T(8,128)(2,1)} %bitcast.8), channel_id=1, replica_groups=mesh['space'=16,'band'=8] {'band'}, dimensions={0} | all-to-all | bytes 6094848 | tf_op jit(solution)/shard_map/all_to_all | solution.py:651
  160.1 5.7 %products.1 = (bf16[8,8,64,128]{3,2,1,0:T(8,128)(2,1)S(1)}, bf16[8,8,64,128]{3,2,1,0:T(8,128)(2,1)S(1)}) custom-call(bf16[8,976,128]{2,1,0:T(8,128)(2,1)} %all-to-all-done.states_ref, bf16[8,1488,128]{2,1,0:T(8,128)(2,1)S(1)} %all_to_all.15.mixed_ref, s32[1]{0:T(128)} %bitcast.position_ref.refs_5_), custom_call_target="tpu_custom_call" | custom-call | tf_op jit(solution)/shard_map/products/pallas_call | solution.py:598
  165.9 2.6 %collective-permute-done.10 = bf16[8,8,64,128]{3,2,1,0:T(8,128)(2,1)S(1)} collective-permute-done((bf16[8,8,64,128]{3,2,1,0:T(8,128)(2,1)S(1)}, bf16[8,8,64,128]{3,2,1,0:T(8,128)(2,1)S(1)}, u32[]{:S(2)}, u32[]{:S(2)}) %collective-permute-start.10) | collective-permute-done | bytes 1048608 | tf_op jit(solution)/shard_map/ppermute | solution.py:610
  168.6 1.4 add_convert_fusion
  170.0 14.6 %all-to-all-start.2 = ((bf16[64,64,128]{2,1,0:T(8,128)(2,1)}), bf16[64,64,128]{2,1,0:T(8,128)(2,1)}, u32[]{:S(2)}, u32[]{:S(2)}) async-start(bf16[64,64,128]{2,1,0:T(8,128)(2,1)} %bitcast.10), calls=%async_computation.2 | async-start | bytes 2097152 | tf_op jit(solution)/shard_map/all_to_all | solution.py:613
  184.7 14.6 %hand_back.1 = bf16[10368,128]{1,0:T(8,128)(2,1)} custom-call(bf16[10368,128]{1,0:T(8,128)(2,1)S(1)} %copy-done.5, s32[8,1600]{1,0:T(8,128)S(1)} %reshape.28.index_ref), custom_call_target="tpu_custom_call" | custom-call | tf_op jit(solution)/shard_map/hand_back/pallas_call | solution.py:553
  199.3 3.0 %all-to-all-done.2 = bf16[64,64,128]{2,1,0:T(8,128)(2,1)} async-done(((bf16[64,64,128]{2,1,0:T(8,128)(2,1)}), bf16[64,64,128]{2,1,0:T(8,128)(2,1)}, u32[]{:S(2)}, u32[]{:S(2)}) %all-to-all-start.2) | async-done | bytes 1048608 | tf_op jit(solution)/shard_map/all_to_all | solution.py:613
  202.3 2.0 convert_reduce_fusion
  (35 shorter events, 4.0 us)
Async XLA Ops:
  0.6 17.2 %copy-start.8 = (f32[25]{0:T(128)S(1)}, f32[25]{0:T(128)}, u32[]{:S(2)}) copy-start(f32[25]{0:T(128)} %refs_7_.15) | copy-start | bytes 304
  17.8 61.3 %copy-start = (f32[10368,128]{1,0:T(8,128)}, f32[10368,128]{1,0:T(8,128)S(1)}, u32[]{:S(2)}) copy-start(f32[10368,128]{1,0:T(8,128)S(1)} %get-tuple-element.51.refs_1_.refs_2_.refs_3_) | copy-start | bytes 15925252
  20.0 14.1 %collective-permute-start = (bf16[1296,128]{1,0:T(8,128)(2,1)S(1)}, bf16[1296,128]{1,0:T(8,128)(2,1)S(1)}, u32[]{:S(2)}, u32[]{:S(2)}) collective-permute-start(bf16[1296,128]{1,0:T(8,128)(2,1)S(1)} %get-tuple-element.56), channel_id=1, source_target_pairs={{0,8},{16,24},{32,40},{48,56},{64,72},{80,88},{96,104},{112,120},{... | collective-permute-start | bytes 995336 | tf_op jit(solution)/shard_map/ppermute | solution.py:623
  21.5 13.1 %collective-permute-start.1 = (bf16[1296,128]{1,0:T(8,128)(2,1)S(1)}, bf16[1296,128]{1,0:T(8,128)(2,1)S(1)}, u32[]{:S(2)}, u32[]{:S(2)}) collective-permute-start(bf16[1296,128]{1,0:T(8,128)(2,1)S(1)} %get-tuple-element.57), channel_id=1, source_target_pairs={{8,16},{24,32},{40,48},{56,64},{72,80},{88,96},{104,112},{16,8},{3... | collective-permute-start | bytes 995336 | tf_op jit(solution)/shard_map/ppermute | solution.py:624
  38.3 12.6 %collective-permute-start.2 = (bf16[1296,128]{1,0:T(8,128)(2,1)S(1)}, bf16[1296,128]{1,0:T(8,128)(2,1)S(1)}, u32[]{:S(2)}, u32[]{:S(2)}) collective-permute-start(bf16[1296,128]{1,0:T(8,128)(2,1)S(1)} %get-tuple-element.64), channel_id=1, source_target_pairs={{0,8},{16,24},{32,40},{48,56},{64,72},{80,88},{96,104},{112,120},{... | collective-permute-start | bytes 995336 | tf_op jit(solution)/shard_map/ppermute | solution.py:623
  38.4 13.5 %collective-permute-start.3 = (bf16[1296,128]{1,0:T(8,128)(2,1)S(1)}, bf16[1296,128]{1,0:T(8,128)(2,1)S(1)}, u32[]{:S(2)}, u32[]{:S(2)}) collective-permute-start(bf16[1296,128]{1,0:T(8,128)(2,1)S(1)} %get-tuple-element.65), channel_id=1, source_target_pairs={{8,16},{24,32},{40,48},{56,64},{72,80},{88,96},{104,112},{16,8},{3... | collective-permute-start | bytes 995336 | tf_op jit(solution)/shard_map/ppermute | solution.py:624
  55.6 12.6 %collective-permute-start.4 = (bf16[1296,128]{1,0:T(8,128)(2,1)S(1)}, bf16[1296,128]{1,0:T(8,128)(2,1)S(1)}, u32[]{:S(2)}, u32[]{:S(2)}) collective-permute-start(bf16[1296,128]{1,0:T(8,128)(2,1)S(1)} %get-tuple-element.71), channel_id=1, source_target_pairs={{0,8},{16,24},{32,40},{48,56},{64,72},{80,88},{96,104},{112,120},{... | collective-permute-start | bytes 995336 | tf_op jit(solution)/shard_map/ppermute | solution.py:623
  55.7 13.5 %collective-permute-start.5 = (bf16[1296,128]{1,0:T(8,128)(2,1)S(1)}, bf16[1296,128]{1,0:T(8,128)(2,1)S(1)}, u32[]{:S(2)}, u32[]{:S(2)}) collective-permute-start(bf16[1296,128]{1,0:T(8,128)(2,1)S(1)} %get-tuple-element.72), channel_id=1, source_target_pairs={{8,16},{24,32},{40,48},{56,64},{72,80},{88,96},{104,112},{16,8},{3... | collective-permute-start | bytes 995336 | tf_op jit(solution)/shard_map/ppermute | solution.py:624
  72.9 15.9 %collective-permute-start.6 = (bf16[1296,128]{1,0:T(8,128)(2,1)S(1)}, bf16[1296,128]{1,0:T(8,128)(2,1)S(1)}, u32[]{:S(2)}, u32[]{:S(2)}) collective-permute-start(bf16[1296,128]{1,0:T(8,128)(2,1)S(1)} %get-tuple-element.76), channel_id=1, source_target_pairs={{0,8},{16,24},{32,40},{48,56},{64,72},{80,88},{96,104},{112,120},{... | collective-permute-start | bytes 995336 | tf_op jit(solution)/shard_map/ppermute | solution.py:623
  73.0 15.8 %collective-permute-start.7 = (bf16[1296,128]{1,0:T(8,128)(2,1)S(1)}, bf16[1296,128]{1,0:T(8,128)(2,1)S(1)}, u32[]{:S(2)}, u32[]{:S(2)}) collective-permute-start(bf16[1296,128]{1,0:T(8,128)(2,1)S(1)} %get-tuple-element.77), channel_id=1, source_target_pairs={{8,16},{24,32},{40,48},{56,64},{72,80},{88,96},{104,112},{16,8},{3... | collective-permute-start | bytes 995336 | tf_op jit(solution)/shard_map/ppermute | solution.py:624
  88.9 34.8 %all-to-all-start = ((bf16[8,976,128]{2,1,0:T(8,128)(2,1)}), bf16[8,976,128]{2,1,0:T(8,128)(2,1)}, u32[]{:S(2)}, u32[]{:S(2)}) async-start(bf16[8,976,128]{2,1,0:T(8,128)(2,1)} %bitcast.9), calls=%async_computation | async-start | bytes 3997696 | tf_op jit(solution)/shard_map/all_to_all | solution.py:643
  93.3 10.1 %copy-start.3 = (bf16[7808,128]{1,0:T(8,128)(2,1)S(1)}, bf16[7808,128]{1,0:T(8,128)(2,1)}, u32[]{:S(2)}) copy-start(bf16[7808,128]{1,0:T(8,128)(2,1)} %get-tuple-element.80.refs_0_) | copy-start | bytes 5996548
  93.4 1.5 copy-start.6
  94.8 1.3 copy-start.7
  98.7 19.9 %collective-permute-start.8 = (bf16[1296,128]{1,0:T(8,128)(2,1)S(1)}, bf16[1296,128]{1,0:T(8,128)(2,1)S(1)}, u32[]{:S(2)}, u32[]{:S(2)}) collective-permute-start(bf16[1296,128]{1,0:T(8,128)(2,1)S(1)} %get-tuple-element.90), channel_id=1, source_target_pairs={{0,8},{16,24},{32,40},{48,56},{64,72},{80,88},{96,104},{112,120},{... | collective-permute-start | bytes 995336 | tf_op jit(solution)/shard_map/ppermute | solution.py:623
  98.8 23.0 %collective-permute-start.9 = (bf16[1296,128]{1,0:T(8,128)(2,1)S(1)}, bf16[1296,128]{1,0:T(8,128)(2,1)S(1)}, u32[]{:S(2)}, u32[]{:S(2)}) collective-permute-start(bf16[1296,128]{1,0:T(8,128)(2,1)S(1)} %get-tuple-element.91), channel_id=1, source_target_pairs={{8,16},{24,32},{40,48},{56,64},{72,80},{88,96},{104,112},{16,8},{3... | collective-permute-start | bytes 995336 | tf_op jit(solution)/shard_map/ppermute | solution.py:624
  103.5 2.5 %copy-start.1 = (f32[10368,128]{1,0:T(8,128)S(1)}, f32[10368,128]{1,0:T(8,128)}, u32[]{:S(2)}) copy-start(f32[10368,128]{1,0:T(8,128)} %copy-done) | copy-start | bytes 15925252
  117.1 1.6 copy-start.2
  118.7 5.0 %copy-start.4 = (bf16[10368,128]{1,0:T(8,128)(2,1)}, bf16[10368,128]{1,0:T(8,128)(2,1)S(1)}, u32[]{:S(2)}) copy-start(bf16[10368,128]{1,0:T(8,128)(2,1)S(1)} %get-tuple-element.94.plain_ref) | copy-start | bytes 7962628
  165.9 2.7 %collective-permute-start.10 = (bf16[8,8,64,128]{3,2,1,0:T(8,128)(2,1)S(1)}, bf16[8,8,64,128]{3,2,1,0:T(8,128)(2,1)S(1)}, u32[]{:S(2)}, u32[]{:S(2)}) collective-permute-start(bf16[8,8,64,128]{3,2,1,0:T(8,128)(2,1)S(1)} %get-tuple-element.97), channel_id=1, source_target_pairs={{0,8},{8,0},{16,24},{24,16},{32,40},{40,32},{48,56},{56,48},{64,72... | collective-permute-start | bytes 3145736 | tf_op jit(solution)/shard_map/ppermute | solution.py:610
  168.6 15.9 %copy-start.9 = (s32[25,512]{1,0:T(8,128)S(1)}, s32[25,512]{1,0:T(8,128)}, u32[]{:S(2)}) copy-start(s32[25,512]{1,0:T(8,128)} %index_hbm.1) | copy-start | bytes 153604
  170.0 14.8 %copy-start.5 = (bf16[10368,128]{1,0:T(8,128)(2,1)S(1)}, bf16[10368,128]{1,0:T(8,128)(2,1)}, u32[]{:S(2)}) copy-start(bf16[10368,128]{1,0:T(8,128)(2,1)} %copy-done.4) | copy-start | bytes 7962628
  170.0 32.3 %all-to-all-start.2 = ((bf16[64,64,128]{2,1,0:T(8,128)(2,1)}), bf16[64,64,128]{2,1,0:T(8,128)(2,1)}, u32[]{:S(2)}, u32[]{:S(2)}) async-start(bf16[64,64,128]{2,1,0:T(8,128)(2,1)} %bitcast.10), calls=%async_computation.2 | async-start | bytes 2097152 | tf_op jit(solution)/shard_map/all_to_all | solution.py:613

commit v5 on v4

--- a/solution.py
+++ b/solution.py
@@ -6,6 +6,7 @@
 from jax.experimental import pallas as pl
 from jax.experimental.pallas import tpu as pltpu
 from jax.sharding import PartitionSpec as P
+
 
 EDGE = 8
 SLAB_XY = 5
@@ -260,31 +261,27 @@
 def faces_kernel(stage, *refs):
     late, spread = stage >= STEPS, stage <= STEPS
     refs = list(refs)
-    field_ref, near_in, far_in, low_ref, high_ref, position_ref = refs[:6]
+    rim_ref, near_in, far_in, low_ref, high_ref, position_ref = refs[:6]
     refs = refs[6:]
     if spread:
         outer_ref, scale_ref, _ = refs[:3]
         refs = refs[3:]
+        face_ref = refs.pop(0)
         if late:
-            face_ref, edge_ref, sums_ref, near_out, far_out = refs
-        else:
-            out_ref, sums_ref, near_out, far_out, face_ref = refs
+            edge_ref = refs.pop(0)
+        sums_ref, near_out, far_out = refs
     else:
         _, block_ref, face_ref, edge_ref, sems = refs
     odd = position_ref[0] % 2
     lead, _ = factors((low_ref, high_ref), stage)
 
     def settle_rows(i, _):
-        for face_in, plane, side in ((near_in, (EDGE - 1) * (1 - odd), 1 - odd), (far_in, (EDGE - 1) * odd, odd)):
+        for face_in, side in ((near_in, 1 - odd), (far_in, odd)):
             got = face_in[pl.ds(pl.multiple_of(i * GROUP, 16), GROUP), :].astype(F32)
             for part in range(GROUP // EDGE):
-                here = pl.ds(pl.multiple_of(side * FACE + i * GROUP + part * EDGE, EDGE), EDGE)
-                rows = here if late else pl.ds((i * (GROUP // EDGE) + part) * QUAD + plane, EDGE, stride=EDGE)
-                value = field_ref[rows, :] + lead * got[part * EDGE : (part + 1) * EDGE, :]
-                value = value.astype(BF16).astype(F32)
-                if not late:
-                    out_ref[rows, :] = value
-                face_ref[here, :] = value
+                rows = pl.ds(pl.multiple_of(side * FACE + i * GROUP + part * EDGE, EDGE), EDGE)
+                value = rim_ref[rows, :] + lead * got[part * EDGE : (part + 1) * EDGE, :]
+                face_ref[rows, :] = value.astype(BF16).astype(F32)
         return 0
 
     lax.fori_loop(0, FACE // GROUP, settle_rows, 0)
@@ -332,15 +329,14 @@
             copy.wait()
 
 
-def faces(stage, part, got, bounds, position, outer=None, scale=None, sums=None, blocks=None):
-    args = [part, *got, *bounds, position]
+def faces(stage, rim, got, bounds, position, outer=None, scale=None, sums=None, blocks=None):
+    args = [rim, *got, *bounds, position]
     specs = [VMEM] * 3 + [SMEM] * 3
     faces_shape = (2 * FACE, COLS)
     scratch = []
     if stage < STEPS:
-        outs = [pltpu.VMEM((NODES, COLS), F32), pltpu.VMEM(faces_shape, F32)]
+        outs = [pltpu.VMEM(faces_shape, F32), pltpu.VMEM(faces_shape, F32)]
         aliases = {0: 0, 8: 1}
-        scratch = [pltpu.VMEM(faces_shape, F32)]
     elif stage == STEPS:
         outs = [
             jax.ShapeDtypeStruct(faces_shape, F32),
@@ -406,12 +402,25 @@
                 edge_ref[band * OUTER_BLOCK : (band + 1) * OUTER_BLOCK, :])
         rebuild(early_ref, settled_ref, field_ref)
     else:
-        field_ref = refs.pop(0)
         if stage > 1:
-            refs.pop(0)
-        pot_ref, mat_ref, inner_ref, low_ref, high_ref, scale_ref, out_ref, sums_ref, *more = refs
-        if more:
-            early_ref, rim_ref = more
+            settled_ref = refs[2]
+            refs = refs[3:]
+        pot_ref, mat_ref, inner_ref, low_ref, high_ref, scale_ref, out_ref, sums_ref, rim_ref, *more = (
+            refs if stage > 1 else refs[1:])
+        if stage == STEPS:
+            early_ref = more.pop(0)
+        field_ref = more[0] if stage > 1 else refs[0]
+        if stage > 1:
+
+            def put_settled(i, _):
+                for side in range(2):
+                    for part in range(GROUP // EDGE):
+                        node = i * GROUP + part * EDGE
+                        rows = pl.ds(node * EDGE + side * (EDGE - 1), EDGE, stride=EDGE)
+                        field_ref[rows, :] = settled_ref[pl.ds(pl.multiple_of(side * FACE + node, EDGE), EDGE), :]
+                return 0
+
+            lax.fori_loop(0, FACE // GROUP, put_settled, 0)
     in_place = 1 < stage <= STEPS
     bounds = (low_ref, high_ref)
     lead, _ = factors(bounds, stage)
@@ -468,7 +477,7 @@
 
     if stage >= STEPS:
         put_inner(out_ref, put)
-        lax.fori_loop(0, FACE // GROUP, put_rim, 0)
+    lax.fori_loop(0, FACE // GROUP, put_rim, 0)
     if last:
 
         def emit_rows(i, _):
@@ -481,25 +490,24 @@
         spread_faces(out_ref, inner_ref, scale_ref, sums_ref)
 
 
-def cells(stage, field, prev, pot, mat, inner, bounds, scale):
-    args = [field] + ([prev] if stage > 1 else []) + [pot, mat, inner]
+def cells(stage, field, prev, settled, pot, mat, inner, bounds, scale):
+    args = [field] + ([prev, settled] if stage > 1 else []) + [pot, mat, inner]
     faces_shape = (2 * FACE, COLS)
-    outs = [pltpu.VMEM((NODES, COLS), F32)]
-    if stage < STEPS:
-        outs.append(pltpu.VMEM(faces_shape, F32))
-    else:
-        outs += [
-            pltpu.HBM(faces_shape, F32),
-            pltpu.HBM((BANDS * INNER_BLOCK, COLS), BF16),
-            pltpu.HBM(faces_shape, F32),
-        ]
+    kind = pltpu.VMEM if stage < STEPS else pltpu.HBM
+    outs = [pltpu.VMEM((NODES, COLS), F32), kind(faces_shape, F32), kind(faces_shape, F32)]
+    if stage == STEPS:
+        outs.append(pltpu.HBM((BANDS * INNER_BLOCK, COLS), BF16))
+    aliases = {}
+    if stage > 1:
+        aliases = {1: 0, 0: len(outs)}
+        outs.append(pltpu.VMEM((NODES, COLS), F32))
     return pl.pallas_call(
         functools.partial(cells_kernel, stage),
         name="cells",
         out_shape=tuple(outs),
         in_specs=[VMEM] * len(args) + [SMEM] * 3,
         out_specs=(VMEM,) * len(outs),
-        input_output_aliases={1: 0} if stage > 1 else {},
+        input_output_aliases=aliases,
         compiler_params=SMALL if stage < STEPS else BIG,
     )(*args, *bounds, scale)
 
@@ -620,25 +628,24 @@
     beside = [(i, i + 1) for i in range(0, count, 2)]
     both_ways = lambda pairs: pairs + [(j, i) for i, j in pairs]
     near, far = lax.optimization_barrier((near, far))
+    from_far = lax.ppermute(far, "space", both_ways(apart))
     from_near = lax.ppermute(near, "space", both_ways(beside))
-    from_far = lax.ppermute(far, "space", both_ways(apart))
     return from_near, from_far
 
 
 def local(states, potential, cell_matrix, cell_scale, connectivity, lower_bound, upper_bound):
     bounds = (lower_bound, upper_bound)
     position = lax.axis_index("space").astype(jnp.int32).reshape(1)
-    count = lax.axis_size("space")
     field, pot, mat, full, inner, outer = gather(states, potential, connectivity, cell_matrix, bounds)
     near, far = first_faces(field, full, cell_scale, position)
-    prev = None
+    prev = settled = None
     for stage in range(1, STEPS):
         got = swap_faces(near, far)
-        part, sums = cells(stage, field, prev, pot, mat, inner, bounds, cell_scale)
-        prev = field
-        field, _, near, far = faces(stage, part, got, bounds, position, outer, cell_scale, sums)
+        part, sums, rim, *patched = cells(stage, field, prev, settled, pot, mat, inner, bounds, cell_scale)
+        prev, field = (patched or [field])[0], part
+        settled, _, near, far = faces(stage, rim, got, bounds, position, outer, cell_scale, sums)
     got = swap_faces(near, far)
-    _, sums, early, rim = cells(STEPS, field, prev, pot, mat, inner, bounds, cell_scale)
+    _, sums, rim, early, _ = cells(STEPS, field, prev, settled, pot, mat, inner, bounds, cell_scale)
     got, early = lax.optimization_barrier((got, early))
     node_states = lax.all_to_all(
         early.reshape(BANDS, INNER_BLOCK, COLS), "band", split_axis=0, concat_axis=0, tiled=True)

time: 205 us -> 204 us (level)
  transfers between devices with their start and end apart: 13 -> 13, of which waited for: 6 -> 6; matrix products, arithmetic and copies ran while one was open for 0% -> 0% of each run, Pallas kernels for 29% -> 30%
where the time goes in v5:
time: 204 us; the launch traced here: 203 us
  Pallas kernels  94 us (46%)
  starting transfers between devices  49.5 us (24%)
  blocking collectives  36.5 us (18%)
  waiting for transfers between devices  9.72 us (5%)
  local copies, waits for them, and re-layouts  7.97 us (4%)
  other arithmetic  3.38 us (2%)
  between operations  2.25 us (1%)
    all_to_all x1, blocking collectives, local(): lax.all_to_all(blocks.reshape(BANDS, BLOCK, COLS), 'band', split_axis=0,...  36.5 us
    pallas_call x4, Pallas kernels, cells(): pl.pallas_call(functools.partial(cells_kernel, stage), name='cells', out_...  31.9 us
    ppermute x5, starting transfers between devices, swap_faces(): from_far = lax.ppermute(far, 'space', both_ways(apart))  28 us
    all_to_all x1, starting transfers between devices, project(): lax.all_to_all(both, ('space', 'band'), split_axis=0, concat_axis=0, tile...  15.2 us
    pallas_call x1, Pallas kernels, gather(): pl.pallas_call(gather_kernel, name='gather_states', out_shape=(pltpu.VMEM...  15 us
    pallas_call x1, Pallas kernels, hand_back(): pl.pallas_call(return_kernel, name='hand_back', out_shape=jax.ShapeDtypeS...  14.6 us
    pallas_call x5, Pallas kernels, faces(): pl.pallas_call(functools.partial(faces_kernel, stage), name='faces', out_...  13.5 us
    pallas_call x1, Pallas kernels, last_cells(): pl.pallas_call(functools.partial(cells_kernel, STEPS + 1), name='last_cel...  11.1 us
  transfers between devices with their start and end apart: 13, of which 6 were waited for; matrix products, arithmetic and copies ran while one was open for 0% of the time, Pallas kernels for 30%

profile of v5, /device:TPU:1, one launch (start us, length us, event | category | flops | bytes accessed | tf_op | source)
XLA Modules:
  0.0 203.3 jit_solution(320595822645700078)
XLA Ops:
  2.8 15.0 %gather_states.1 = (f32[10368,128]{1,0:T(8,128)S(1)}, f32[10368,128]{1,0:T(8,128)S(1)}, bf16[512,512]{1,0:T(8,128)(2,1)S(1)}, bf16[128,512]{1,0:T(8,128)(2,1)S(1...) custom-call(bf16[10368,128]{1,0:T(8,128)(2,1)} %states_hbm.1, f32[8,1296]{1,0:T(8,128)S(1)} %reshape.25.pot_ref, ...), custom_call_target="tpu_custom_call" | custom-call | tf_op jit(solution)/shard_map/gather_states/pallas_call | solution.py:119
  17.9 2.2 %first_faces.1 = (bf16[1296,128]{1,0:T(8,128)(2,1)S(1)}, bf16[1296,128]{1,0:T(8,128)(2,1)S(1)}) custom-call(f32[10368,128]{1,0:T(8,128)S(1)} %get-tuple-element.55.refs_0_.field_ref.refs_1_, bf16[128,512]{1,0:T(8,128)(2,1)S(1)} %get-tuple-element.61.full_ref, f32[25]{0:T(128)S(1)} %copy-done.8, s32[1]{0:T(128)} %bitcast.position_ref.refs_5_), custom_call_target="tpu_custom_call" | custom-call | tf_op jit(solution)/shard_map/first_faces/pallas_call | solution.py:219
  20.0 1.5 collective-permute-start
  21.5 5.5 %collective-permute-start.1 = (bf16[1296,128]{1,0:T(8,128)(2,1)S(1)}, bf16[1296,128]{1,0:T(8,128)(2,1)S(1)}, u32[]{:S(2)}, u32[]{:S(2)}) collective-permute-start(bf16[1296,128]{1,0:T(8,128)(2,1)S(1)} %get-tuple-element.63), channel_id=1, source_target_pairs={{8,16},{24,32},{40,48},{56,64},{72,80},{88,96},{104,112},{16,8},{3... | collective-permute-start | bytes 995336 | tf_op jit(solution)/shard_map/ppermute | solution.py:631
  27.0 7.4 %cells.4 = (f32[10368,128]{1,0:T(8,128)S(1)}, f32[2592,128]{1,0:T(8,128)S(1)}, f32[2592,128]{1,0:T(8,128)S(1)}) custom-call(f32[10368,128]{1,0:T(8,128)S(1)} %get-tuple-element.55.refs_0_.field_ref.refs_1_, f32[10368,128]{1,0:T(8,128)S(1)} %get-tuple-element.56.refs_1_.refs_3_, bf16[512,512]{1,0:T(8,128)(2,1)S(1)} %get-tuple-element.57.refs_2_.refs_4_, ...), custom_call_target="tpu_custom_call" | custom-call | tf_op jit(solution)/shard_map/cells/pallas_call | solution.py:504
  34.6 3.0 %faces.5 = (f32[2592,128]{1,0:T(8,128)S(1)}, f32[2592,128]{1,0:T(8,128)S(1)}, bf16[1296,128]{1,0:T(8,128)(2,1)S(1)}, bf16[1296,128]{1,0:T(8,128)(2,1)S(1)}) custom-call(f32[2592,128]{1,0:T(8,128)S(1)} %get-tuple-element.60.refs_0_, bf16[1296,128]{1,0:T(8,128)(2,1)S(1)} %collective-permute-done.refs_1_, ...), custom_call_target="tpu_custom_call", output_to_operand_aliasing={{0}: (0, {}), {1}: (8, {})} | custom-call | tf_op jit(solution)/shard_map/faces/pallas_call | solution.py:362
  37.8 5.9 %collective-permute-start.3 = (bf16[1296,128]{1,0:T(8,128)(2,1)S(1)}, bf16[1296,128]{1,0:T(8,128)(2,1)S(1)}, u32[]{:S(2)}, u32[]{:S(2)}) collective-permute-start(bf16[1296,128]{1,0:T(8,128)(2,1)S(1)} %get-tuple-element.73), channel_id=1, source_target_pairs={{8,16},{24,32},{40,48},{56,64},{72,80},{88,96},{104,112},{16,8},{3... | collective-permute-start | bytes 995336 | tf_op jit(solution)/shard_map/ppermute | solution.py:631
  43.7 7.2 %cells.5 = (f32[10368,128]{1,0:T(8,128)S(1)}, f32[2592,128]{1,0:T(8,128)S(1)}, f32[2592,128]{1,0:T(8,128)S(1)}, f32[10368,128]{1,0:T(8,128)S(1)}) custom-call(f32[10368,128]{1,0:T(8,128)S(1)} %get-tuple-element.59.refs_0_, f32[10368,128]{1,0:T(8,128)S(1)} %get-tuple-element.55.refs_0_.field_ref.refs_1_, ...), custom_call_target="tpu_custom_call", output_to_operand_aliasing={{0}: (1, {}), {3}: (0, {})} | custom-call | tf_op jit(solution)/shard_map/cells/pallas_call | solution.py:504
  51.3 3.0 %faces.6 = (f32[2592,128]{1,0:T(8,128)S(1)}, f32[2592,128]{1,0:T(8,128)S(1)}, bf16[1296,128]{1,0:T(8,128)(2,1)S(1)}, bf16[1296,128]{1,0:T(8,128)(2,1)S(1)}) custom-call(f32[2592,128]{1,0:T(8,128)S(1)} %get-tuple-element.69.refs_0_, bf16[1296,128]{1,0:T(8,128)(2,1)S(1)} %collective-permute-done.2.refs_1_, ...), custom_call_target="tpu_custom_call", output_to_operand_aliasing={{0}: (0, {}), {1}: (8, {})} | custom-call | tf_op jit(solution)/shard_map/faces/pallas_call | solution.py:362
  54.4 5.9 %collective-permute-start.5 = (bf16[1296,128]{1,0:T(8,128)(2,1)S(1)}, bf16[1296,128]{1,0:T(8,128)(2,1)S(1)}, u32[]{:S(2)}, u32[]{:S(2)}) collective-permute-start(bf16[1296,128]{1,0:T(8,128)(2,1)S(1)} %get-tuple-element.80), channel_id=1, source_target_pairs={{8,16},{24,32},{40,48},{56,64},{72,80},{88,96},{104,112},{16,8},{3... | collective-permute-start | bytes 995336 | tf_op jit(solution)/shard_map/ppermute | solution.py:631
  60.3 7.2 %cells.6 = (f32[10368,128]{1,0:T(8,128)S(1)}, f32[2592,128]{1,0:T(8,128)S(1)}, f32[2592,128]{1,0:T(8,128)S(1)}, f32[10368,128]{1,0:T(8,128)S(1)}) custom-call(f32[10368,128]{1,0:T(8,128)S(1)} %get-tuple-element.67.refs_0_, f32[10368,128]{1,0:T(8,128)S(1)} %get-tuple-element.68.refs_1_, ...), custom_call_target="tpu_custom_call", output_to_operand_aliasing={{0}: (1, {}), {3}: (0, {})} | custom-call | tf_op jit(solution)/shard_map/cells/pallas_call | solution.py:504
  67.9 3.0 %faces.7 = (f32[2592,128]{1,0:T(8,128)S(1)}, f32[2592,128]{1,0:T(8,128)S(1)}, bf16[1296,128]{1,0:T(8,128)(2,1)S(1)}, bf16[1296,128]{1,0:T(8,128)(2,1)S(1)}) custom-call(f32[2592,128]{1,0:T(8,128)S(1)} %get-tuple-element.76.refs_0_, bf16[1296,128]{1,0:T(8,128)(2,1)S(1)} %collective-permute-done.4.refs_1_, ...), custom_call_target="tpu_custom_call", output_to_operand_aliasing={{0}: (0, {}), {1}: (8, {})} | custom-call | tf_op jit(solution)/shard_map/faces/pallas_call | solution.py:362
  71.0 6.1 %collective-permute-start.7 = (bf16[1296,128]{1,0:T(8,128)(2,1)S(1)}, bf16[1296,128]{1,0:T(8,128)(2,1)S(1)}, u32[]{:S(2)}, u32[]{:S(2)}) collective-permute-start(bf16[1296,128]{1,0:T(8,128)(2,1)S(1)} %get-tuple-element.85), channel_id=1, source_target_pairs={{8,16},{24,32},{40,48},{56,64},{72,80},{88,96},{104,112},{16,8},{3... | collective-permute-start | bytes 995336 | tf_op jit(solution)/shard_map/ppermute | solution.py:631
  77.1 10.1 %cells.7 = (f32[10368,128]{1,0:T(8,128)S(1)}, f32[2592,128]{1,0:T(8,128)}, f32[2592,128]{1,0:T(8,128)}, bf16[7808,128]{1,0:T(8,128)(2,1)}, f32[10368,128]{1,0:T(8,128)S(1)}) custom-call(f32[10368,128]{1,0:T(8,128)S(1)} %get-tuple-element.86.refs_0_, f32[10368,128]{1,0:T(8,128)S(1)} %get-tuple-element.87.refs_1_, ...), custom_call_target="tpu_custom_call", output_to_operand_aliasing={{0}: (1, {}), {4}: (0, {})} | custom-call | tf_op jit(solution)/shard_map/cells/pallas_call | solution.py:504
  87.2 4.5 %all-to-all-start = ((bf16[8,976,128]{2,1,0:T(8,128)(2,1)}), bf16[8,976,128]{2,1,0:T(8,128)(2,1)}, u32[]{:S(2)}, u32[]{:S(2)}) async-start(bf16[8,976,128]{2,1,0:T(8,128)(2,1)} %bitcast.9), calls=%async_computation | async-start | bytes 3997696 | tf_op jit(solution)/shard_map/all_to_all | solution.py:650
  91.7 1.5 copy-done.6
  93.2 1.3 copy-done.7
  94.5 2.6 %faces.8 = (f32[2592,128]{1,0:T(8,128)S(1)}, bf16[2048,128]{1,0:T(8,128)(2,1)S(1)}, f32[2592,128]{1,0:T(8,128)S(1)}, bf16[1296,128]{1,0:T(8,128)(2,1)S(1)}, bf16[1296,128]{1,0:T(8,128)(2,1)S(1)}) custom-call(f32[2592,128]{1,0:T(8,128)S(1)} %copy-done.7, bf16[1296,128]{1,0:T(8,128)(2,1)S(1)} %collective-permute-done.6.refs_1_, ...), custom_call_target="tpu_custom_call", output_to_operand_aliasing={{2}: (8, {})} | custom-call | tf_op jit(solution)/shard_map/faces/pallas_call | solution.py:362
  97.2 4.6 %collective-permute-start.9 = (bf16[1296,128]{1,0:T(8,128)(2,1)S(1)}, bf16[1296,128]{1,0:T(8,128)(2,1)S(1)}, u32[]{:S(2)}, u32[]{:S(2)}) collective-permute-start(bf16[1296,128]{1,0:T(8,128)(2,1)S(1)} %get-tuple-element.101), channel_id=1, source_target_pairs={{8,16},{24,32},{40,48},{56,64},{72,80},{88,96},{104,112},{16,8},{3... | collective-permute-start | bytes 995336 | tf_op jit(solution)/shard_map/ppermute | solution.py:631
  101.8 2.5 %copy-done.1 = f32[10368,128]{1,0:T(8,128)S(1)} copy-done((f32[10368,128]{1,0:T(8,128)S(1)}, f32[10368,128]{1,0:T(8,128)}, u32[]{:S(2)}) %copy-start.1) | copy-done | bytes 5308440
  104.3 11.1 %last_cells.1 = (f32[2592,128]{1,0:T(8,128)S(1)}, bf16[10368,128]{1,0:T(8,128)(2,1)S(1)}, bf16[11904,128]{1,0:T(8,128)(2,1)S(1)}) custom-call(bf16[7808,128]{1,0:T(8,128)(2,1)S(1)} %copy-done.3, f32[2592,128]{1,0:T(8,128)S(1)} %get-tuple-element.95.refs_1_, bf16[2048,128]{1,0:T(8,128)(2,1)S(1)} %get-tuple-element.96.refs_2_, f32[10368,128]{1,0:T(8,128)S(1)} %copy-done.1, ...), custom_call_target="tpu_custom_call" | custom-call | tf_op jit(solution)/shard_map/last_cells/pallas_call | solution.py:516
  115.5 1.6 copy-done.2
  117.1 3.1 %collective-permute-done.9.refs_2_ = bf16[1296,128]{1,0:T(8,128)(2,1)S(1)} collective-permute-done((bf16[1296,128]{1,0:T(8,128)(2,1)S(1)}, bf16[1296,128]{1,0:T(8,128)(2,1)S(1)}, u32[]{:S(2)}, u32[]{:S(2)}) %collective-permute-start.9) | collective-permute-done | bytes 331808 | tf_op jit(solution)/shard_map/ppermute | solution.py:631
  120.2 1.8 faces.9
  122.0 36.5 %all_to_all.15.mixed_ref = bf16[8,1488,128]{2,1,0:T(8,128)(2,1)S(1)} all-to-all(bf16[8,1488,128]{2,1,0:T(8,128)(2,1)} %bitcast.8), channel_id=1, replica_groups=mesh['space'=16,'band'=8] {'band'}, dimensions={0} | all-to-all | bytes 6094848 | tf_op jit(solution)/shard_map/all_to_all | solution.py:658
  158.5 5.7 %products.1 = (bf16[8,8,64,128]{3,2,1,0:T(8,128)(2,1)S(1)}, bf16[8,8,64,128]{3,2,1,0:T(8,128)(2,1)S(1)}) custom-call(bf16[8,976,128]{2,1,0:T(8,128)(2,1)} %all-to-all-done.states_ref, bf16[8,1488,128]{2,1,0:T(8,128)(2,1)S(1)} %all_to_all.15.mixed_ref, s32[1]{0:T(128)} %bitcast.position_ref.refs_5_), custom_call_target="tpu_custom_call" | custom-call | tf_op jit(solution)/shard_map/products/pallas_call | solution.py:606
  164.3 2.6 %collective-permute-done.10 = bf16[8,8,64,128]{3,2,1,0:T(8,128)(2,1)S(1)} collective-permute-done((bf16[8,8,64,128]{3,2,1,0:T(8,128)(2,1)S(1)}, bf16[8,8,64,128]{3,2,1,0:T(8,128)(2,1)S(1)}, u32[]{:S(2)}, u32[]{:S(2)}) %collective-permute-start.10) | collective-permute-done | bytes 1048608 | tf_op jit(solution)/shard_map/ppermute | solution.py:618
  167.0 1.4 add_convert_fusion
  168.3 15.2 %all-to-all-start.2 = ((bf16[64,64,128]{2,1,0:T(8,128)(2,1)}), bf16[64,64,128]{2,1,0:T(8,128)(2,1)}, u32[]{:S(2)}, u32[]{:S(2)}) async-start(bf16[64,64,128]{2,1,0:T(8,128)(2,1)} %bitcast.10), calls=%async_computation.2 | async-start | bytes 2097152 | tf_op jit(solution)/shard_map/all_to_all | solution.py:621
  183.7 14.6 %hand_back.1 = bf16[10368,128]{1,0:T(8,128)(2,1)} custom-call(bf16[10368,128]{1,0:T(8,128)(2,1)S(1)} %copy-done.5, s32[8,1600]{1,0:T(8,128)S(1)} %reshape.28.index_ref), custom_call_target="tpu_custom_call" | custom-call | tf_op jit(solution)/shard_map/hand_back/pallas_call | solution.py:561
  198.3 3.0 %all-to-all-done.2 = bf16[64,64,128]{2,1,0:T(8,128)(2,1)} async-done(((bf16[64,64,128]{2,1,0:T(8,128)(2,1)}), bf16[64,64,128]{2,1,0:T(8,128)(2,1)}, u32[]{:S(2)}, u32[]{:S(2)}) %all-to-all-start.2) | async-done | bytes 1048608 | tf_op jit(solution)/shard_map/all_to_all | solution.py:621
  201.3 2.0 convert_reduce_fusion
  (35 shorter events, 2.5 us)
Async XLA Ops:
  0.6 17.2 %copy-start.8 = (f32[25]{0:T(128)S(1)}, f32[25]{0:T(128)}, u32[]{:S(2)}) copy-start(f32[25]{0:T(128)} %refs_7_.12) | copy-start | bytes 304
  17.8 59.3 %copy-start = (f32[10368,128]{1,0:T(8,128)}, f32[10368,128]{1,0:T(8,128)S(1)}, u32[]{:S(2)}) copy-start(f32[10368,128]{1,0:T(8,128)S(1)} %get-tuple-element.56.refs_1_.refs_3_) | copy-start | bytes 15925252
  20.0 14.4 %collective-permute-start = (bf16[1296,128]{1,0:T(8,128)(2,1)S(1)}, bf16[1296,128]{1,0:T(8,128)(2,1)S(1)}, u32[]{:S(2)}, u32[]{:S(2)}) collective-permute-start(bf16[1296,128]{1,0:T(8,128)(2,1)S(1)} %get-tuple-element.62), channel_id=1, source_target_pairs={{0,8},{16,24},{32,40},{48,56},{64,72},{80,88},{96,104},{112,120},{... | collective-permute-start | bytes 995336 | tf_op jit(solution)/shard_map/ppermute | solution.py:632
  21.5 13.1 %collective-permute-start.1 = (bf16[1296,128]{1,0:T(8,128)(2,1)S(1)}, bf16[1296,128]{1,0:T(8,128)(2,1)S(1)}, u32[]{:S(2)}, u32[]{:S(2)}) collective-permute-start(bf16[1296,128]{1,0:T(8,128)(2,1)S(1)} %get-tuple-element.63), channel_id=1, source_target_pairs={{8,16},{24,32},{40,48},{56,64},{72,80},{88,96},{104,112},{16,8},{3... | collective-permute-start | bytes 995336 | tf_op jit(solution)/shard_map/ppermute | solution.py:631
  37.7 13.2 %collective-permute-start.2 = (bf16[1296,128]{1,0:T(8,128)(2,1)S(1)}, bf16[1296,128]{1,0:T(8,128)(2,1)S(1)}, u32[]{:S(2)}, u32[]{:S(2)}) collective-permute-start(bf16[1296,128]{1,0:T(8,128)(2,1)S(1)} %get-tuple-element.72), channel_id=1, source_target_pairs={{0,8},{16,24},{32,40},{48,56},{64,72},{80,88},{96,104},{112,120},{... | collective-permute-start | bytes 995336 | tf_op jit(solution)/shard_map/ppermute | solution.py:632
  37.8 13.5 %collective-permute-start.3 = (bf16[1296,128]{1,0:T(8,128)(2,1)S(1)}, bf16[1296,128]{1,0:T(8,128)(2,1)S(1)}, u32[]{:S(2)}, u32[]{:S(2)}) collective-permute-start(bf16[1296,128]{1,0:T(8,128)(2,1)S(1)} %get-tuple-element.73), channel_id=1, source_target_pairs={{8,16},{24,32},{40,48},{56,64},{72,80},{88,96},{104,112},{16,8},{3... | collective-permute-start | bytes 995336 | tf_op jit(solution)/shard_map/ppermute | solution.py:631
  54.3 13.2 %collective-permute-start.4 = (bf16[1296,128]{1,0:T(8,128)(2,1)S(1)}, bf16[1296,128]{1,0:T(8,128)(2,1)S(1)}, u32[]{:S(2)}, u32[]{:S(2)}) collective-permute-start(bf16[1296,128]{1,0:T(8,128)(2,1)S(1)} %get-tuple-element.79), channel_id=1, source_target_pairs={{0,8},{16,24},{32,40},{48,56},{64,72},{80,88},{96,104},{112,120},{... | collective-permute-start | bytes 995336 | tf_op jit(solution)/shard_map/ppermute | solution.py:632
  54.4 13.5 %collective-permute-start.5 = (bf16[1296,128]{1,0:T(8,128)(2,1)S(1)}, bf16[1296,128]{1,0:T(8,128)(2,1)S(1)}, u32[]{:S(2)}, u32[]{:S(2)}) collective-permute-start(bf16[1296,128]{1,0:T(8,128)(2,1)S(1)} %get-tuple-element.80), channel_id=1, source_target_pairs={{8,16},{24,32},{40,48},{56,64},{72,80},{88,96},{104,112},{16,8},{3... | collective-permute-start | bytes 995336 | tf_op jit(solution)/shard_map/ppermute | solution.py:631
  70.9 16.3 %collective-permute-start.6 = (bf16[1296,128]{1,0:T(8,128)(2,1)S(1)}, bf16[1296,128]{1,0:T(8,128)(2,1)S(1)}, u32[]{:S(2)}, u32[]{:S(2)}) collective-permute-start(bf16[1296,128]{1,0:T(8,128)(2,1)S(1)} %get-tuple-element.84), channel_id=1, source_target_pairs={{0,8},{16,24},{32,40},{48,56},{64,72},{80,88},{96,104},{112,120},{... | collective-permute-start | bytes 995336 | tf_op jit(solution)/shard_map/ppermute | solution.py:632
  71.0 16.2 %collective-permute-start.7 = (bf16[1296,128]{1,0:T(8,128)(2,1)S(1)}, bf16[1296,128]{1,0:T(8,128)(2,1)S(1)}, u32[]{:S(2)}, u32[]{:S(2)}) collective-permute-start(bf16[1296,128]{1,0:T(8,128)(2,1)S(1)} %get-tuple-element.85), channel_id=1, source_target_pairs={{8,16},{24,32},{40,48},{56,64},{72,80},{88,96},{104,112},{16,8},{3... | collective-permute-start | bytes 995336 | tf_op jit(solution)/shard_map/ppermute | solution.py:631
  87.2 34.8 %all-to-all-start = ((bf16[8,976,128]{2,1,0:T(8,128)(2,1)}), bf16[8,976,128]{2,1,0:T(8,128)(2,1)}, u32[]{:S(2)}, u32[]{:S(2)}) async-start(bf16[8,976,128]{2,1,0:T(8,128)(2,1)} %bitcast.9), calls=%async_computation | async-start | bytes 3997696 | tf_op jit(solution)/shard_map/all_to_all | solution.py:650
  91.7 10.1 %copy-start.3 = (bf16[7808,128]{1,0:T(8,128)(2,1)S(1)}, bf16[7808,128]{1,0:T(8,128)(2,1)}, u32[]{:S(2)}) copy-start(bf16[7808,128]{1,0:T(8,128)(2,1)} %get-tuple-element.90.refs_0_) | copy-start | bytes 5996548
  91.7 1.5 copy-start.6
  93.2 1.3 copy-start.7
  97.1 20.0 %collective-permute-start.8 = (bf16[1296,128]{1,0:T(8,128)(2,1)S(1)}, bf16[1296,128]{1,0:T(8,128)(2,1)S(1)}, u32[]{:S(2)}, u32[]{:S(2)}) collective-permute-start(bf16[1296,128]{1,0:T(8,128)(2,1)S(1)} %get-tuple-element.100), channel_id=1, source_target_pairs={{0,8},{16,24},{32,40},{48,56},{64,72},{80,88},{96,104},{112,120},{... | collective-permute-start | bytes 995336 | tf_op jit(solution)/shard_map/ppermute | solution.py:632
  97.2 23.0 %collective-permute-start.9 = (bf16[1296,128]{1,0:T(8,128)(2,1)S(1)}, bf16[1296,128]{1,0:T(8,128)(2,1)S(1)}, u32[]{:S(2)}, u32[]{:S(2)}) collective-permute-start(bf16[1296,128]{1,0:T(8,128)(2,1)S(1)} %get-tuple-element.101), channel_id=1, source_target_pairs={{8,16},{24,32},{40,48},{56,64},{72,80},{88,96},{104,112},{16,8},{3... | collective-permute-start | bytes 995336 | tf_op jit(solution)/shard_map/ppermute | solution.py:631
  101.8 2.5 %copy-start.1 = (f32[10368,128]{1,0:T(8,128)S(1)}, f32[10368,128]{1,0:T(8,128)}, u32[]{:S(2)}) copy-start(f32[10368,128]{1,0:T(8,128)} %copy-done) | copy-start | bytes 15925252
  115.5 1.6 copy-start.2
  117.1 5.0 %copy-start.4 = (bf16[10368,128]{1,0:T(8,128)(2,1)}, bf16[10368,128]{1,0:T(8,128)(2,1)S(1)}, u32[]{:S(2)}) copy-start(bf16[10368,128]{1,0:T(8,128)(2,1)S(1)} %get-tuple-element.104.plain_ref) | copy-start | bytes 7962628
  164.2 2.7 %collective-permute-start.10 = (bf16[8,8,64,128]{3,2,1,0:T(8,128)(2,1)S(1)}, bf16[8,8,64,128]{3,2,1,0:T(8,128)(2,1)S(1)}, u32[]{:S(2)}, u32[]{:S(2)}) collective-permute-start(bf16[8,8,64,128]{3,2,1,0:T(8,128)(2,1)S(1)} %get-tuple-element.107), channel_id=1, source_target_pairs={{0,8},{8,0},{16,24},{24,16},{32,40},{40,32},{48,56},{56,48},{64,72... | collective-permute-start | bytes 3145736 | tf_op jit(solution)/shard_map/ppermute | solution.py:618
  167.0 16.5 %copy-start.9 = (s32[25,512]{1,0:T(8,128)S(1)}, s32[25,512]{1,0:T(8,128)}, u32[]{:S(2)}) copy-start(s32[25,512]{1,0:T(8,128)} %index_hbm.1) | copy-start | bytes 153604
  168.3 15.4 %copy-start.5 = (bf16[10368,128]{1,0:T(8,128)(2,1)S(1)}, bf16[10368,128]{1,0:T(8,128)(2,1)}, u32[]{:S(2)}) copy-start(bf16[10368,128]{1,0:T(8,128)(2,1)} %copy-done.4) | copy-start | bytes 7962628
  168.3 33.0 %all-to-all-start.2 = ((bf16[64,64,128]{2,1,0:T(8,128)(2,1)}), bf16[64,64,128]{2,1,0:T(8,128)(2,1)}, u32[]{:S(2)}, u32[]{:S(2)}) async-start(bf16[64,64,128]{2,1,0:T(8,128)(2,1)} %bitcast.10), calls=%async_computation.2 | async-start | bytes 2097152 | tf_op jit(solution)/shard_map/all_to_all | solution.py:621

commit v6 on v5

--- a/solution.py
+++ b/solution.py
@@ -186,11 +186,15 @@
 
 def add_faces(sums_ref, product, pair, scale_ref):
     for half, cell_y, cell_x, scale in pair_cells(pair, scale_ref):
+        fresh = []
         for side in range(2):
             for j in range(EDGE):
                 at = side * QUAD + j * EDGE
                 rows = pl.ds(side * FACE + ((EDGE - 1) * cell_y + j) * SIDE + (EDGE - 1) * cell_x, EDGE)
-                sums_ref[rows, :] += scale * product[at : at + EDGE, half * COLS : (half + 1) * COLS]
+                value = scale * product[at : at + EDGE, half * COLS : (half + 1) * COLS]
+                fresh.append((rows, sums_ref[rows, :] + value))
+        for rows, value in fresh:
+            sums_ref[rows, :] = value
 
 
 def spread_faces(field_ref, matrix_ref, scale_ref, sums_ref):
@@ -276,12 +280,13 @@
     lead, _ = factors((low_ref, high_ref), stage)
 
     def settle_rows(i, _):
+        here = pl.ds(pl.multiple_of(i * GROUP, 16), GROUP)
+        settled = []
         for face_in, side in ((near_in, 1 - odd), (far_in, odd)):
-            got = face_in[pl.ds(pl.multiple_of(i * GROUP, 16), GROUP), :].astype(F32)
-            for part in range(GROUP // EDGE):
-                rows = pl.ds(pl.multiple_of(side * FACE + i * GROUP + part * EDGE, EDGE), EDGE)
-                value = rim_ref[rows, :] + lead * got[part * EDGE : (part + 1) * EDGE, :]
-                face_ref[rows, :] = value.astype(BF16).astype(F32)
+            rows = pl.ds(pl.multiple_of(side * FACE + i * GROUP, 16), GROUP)
+            settled.append((rows, (rim_ref[rows, :] + lead * face_in[here, :].astype(F32)).astype(BF16).astype(F32)))
+        for rows, value in settled:
+            face_ref[rows, :] = value
         return 0
 
     lax.fori_loop(0, FACE // GROUP, settle_rows, 0)

time: 204 us -> 201 us (0.985)
  Pallas kernels: 94 us -> 90.6 us
    pallas_call x5, Pallas kernels: 13.5 us -> 10.1 us  [faces(): pl.pallas_call(functools.partial(faces_kernel, stage), name='faces', out_...]
  transfers between devices with their start and end apart: 13 -> 13, of which waited for: 6 -> 6; matrix products, arithmetic and copies ran while one was open for 0% -> 0% of each run, Pallas kernels for 30% -> 31%
where the time goes in v6:
time: 201 us; the launch traced here: 200 us
  Pallas kernels  90.6 us (45%)
  starting transfers between devices  49.2 us (24%)
  blocking collectives  36.5 us (18%)
  waiting for transfers between devices  9.74 us (5%)
  local copies, waits for them, and re-layouts  7.97 us (4%)
  other arithmetic  3.38 us (2%)
  between operations  2.27 us (1%)
    all_to_all x1, blocking collectives, local(): lax.all_to_all(blocks.reshape(BANDS, BLOCK, COLS), 'band', split_axis=0,...  36.5 us
    pallas_call x4, Pallas kernels, cells(): pl.pallas_call(functools.partial(cells_kernel, stage), name='cells', out_...  31.9 us
    ppermute x5, starting transfers between devices, swap_faces(): from_far = lax.ppermute(far, 'space', both_ways(apart))  27.7 us
    all_to_all x1, starting transfers between devices, project(): lax.all_to_all(both, ('space', 'band'), split_axis=0, concat_axis=0, tile...  15 us
    pallas_call x1, Pallas kernels, gather(): pl.pallas_call(gather_kernel, name='gather_states', out_shape=(pltpu.VMEM...  15 us
    pallas_call x1, Pallas kernels, hand_back(): pl.pallas_call(return_kernel, name='hand_back', out_shape=jax.ShapeDtypeS...  14.6 us
    pallas_call x1, Pallas kernels, last_cells(): pl.pallas_call(functools.partial(cells_kernel, STEPS + 1), name='last_cel...  11.1 us
    pallas_call x5, Pallas kernels, faces(): pl.pallas_call(functools.partial(faces_kernel, stage), name='faces', out_...  10.1 us
  transfers between devices with their start and end apart: 13, of which 6 were waited for; matrix products, arithmetic and copies ran while one was open for 0% of the time, Pallas kernels for 31%

profile of v6, /device:TPU:1, one launch (start us, length us, event | category | flops | bytes accessed | tf_op | source)
XLA Modules:
  0.0 199.6 jit_solution(7554354258787272977)
XLA Ops:
  2.8 15.0 %gather_states.1 = (f32[10368,128]{1,0:T(8,128)S(1)}, f32[10368,128]{1,0:T(8,128)S(1)}, bf16[512,512]{1,0:T(8,128)(2,1)S(1)}, bf16[128,512]{1,0:T(8,128)(2,1)S(1...) custom-call(bf16[10368,128]{1,0:T(8,128)(2,1)} %states_hbm.1, f32[8,1296]{1,0:T(8,128)S(1)} %reshape.25.pot_ref, ...), custom_call_target="tpu_custom_call" | custom-call | tf_op jit(solution)/shard_map/gather_states/pallas_call | solution.py:119
  17.9 2.2 %first_faces.1 = (bf16[1296,128]{1,0:T(8,128)(2,1)S(1)}, bf16[1296,128]{1,0:T(8,128)(2,1)S(1)}) custom-call(f32[10368,128]{1,0:T(8,128)S(1)} %get-tuple-element.55.refs_0_.field_ref.refs_1_, bf16[128,512]{1,0:T(8,128)(2,1)S(1)} %get-tuple-element.61.full_ref, f32[25]{0:T(128)S(1)} %copy-done.8, s32[1]{0:T(128)} %bitcast.position_ref.refs_5_), custom_call_target="tpu_custom_call" | custom-call | tf_op jit(solution)/shard_map/first_faces/pallas_call | solution.py:223
  20.0 1.5 collective-permute-start
  21.5 5.5 %collective-permute-start.1 = (bf16[1296,128]{1,0:T(8,128)(2,1)S(1)}, bf16[1296,128]{1,0:T(8,128)(2,1)S(1)}, u32[]{:S(2)}, u32[]{:S(2)}) collective-permute-start(bf16[1296,128]{1,0:T(8,128)(2,1)S(1)} %get-tuple-element.63), channel_id=1, source_target_pairs={{8,16},{24,32},{40,48},{56,64},{72,80},{88,96},{104,112},{16,8},{3... | collective-permute-start | bytes 995336 | tf_op jit(solution)/shard_map/ppermute | solution.py:636
  27.0 7.4 %cells.4 = (f32[10368,128]{1,0:T(8,128)S(1)}, f32[2592,128]{1,0:T(8,128)S(1)}, f32[2592,128]{1,0:T(8,128)S(1)}) custom-call(f32[10368,128]{1,0:T(8,128)S(1)} %get-tuple-element.55.refs_0_.field_ref.refs_1_, f32[10368,128]{1,0:T(8,128)S(1)} %get-tuple-element.56.refs_1_.refs_3_, bf16[512,512]{1,0:T(8,128)(2,1)S(1)} %get-tuple-element.57.refs_2_.refs_4_, ...), custom_call_target="tpu_custom_call" | custom-call | tf_op jit(solution)/shard_map/cells/pallas_call | solution.py:509
  34.6 1.9 faces.5
  36.6 5.9 %collective-permute-start.3 = (bf16[1296,128]{1,0:T(8,128)(2,1)S(1)}, bf16[1296,128]{1,0:T(8,128)(2,1)S(1)}, u32[]{:S(2)}, u32[]{:S(2)}) collective-permute-start(bf16[1296,128]{1,0:T(8,128)(2,1)S(1)} %get-tuple-element.73), channel_id=1, source_target_pairs={{8,16},{24,32},{40,48},{56,64},{72,80},{88,96},{104,112},{16,8},{3... | collective-permute-start | bytes 995336 | tf_op jit(solution)/shard_map/ppermute | solution.py:636
  42.5 7.2 %cells.5 = (f32[10368,128]{1,0:T(8,128)S(1)}, f32[2592,128]{1,0:T(8,128)S(1)}, f32[2592,128]{1,0:T(8,128)S(1)}, f32[10368,128]{1,0:T(8,128)S(1)}) custom-call(f32[10368,128]{1,0:T(8,128)S(1)} %get-tuple-element.59.refs_0_, f32[10368,128]{1,0:T(8,128)S(1)} %get-tuple-element.55.refs_0_.field_ref.refs_1_, ...), custom_call_target="tpu_custom_call", output_to_operand_aliasing={{0}: (1, {}), {3}: (0, {})} | custom-call | tf_op jit(solution)/shard_map/cells/pallas_call | solution.py:509
  50.1 1.9 faces.6
  52.2 5.9 %collective-permute-start.5 = (bf16[1296,128]{1,0:T(8,128)(2,1)S(1)}, bf16[1296,128]{1,0:T(8,128)(2,1)S(1)}, u32[]{:S(2)}, u32[]{:S(2)}) collective-permute-start(bf16[1296,128]{1,0:T(8,128)(2,1)S(1)} %get-tuple-element.80), channel_id=1, source_target_pairs={{8,16},{24,32},{40,48},{56,64},{72,80},{88,96},{104,112},{16,8},{3... | collective-permute-start | bytes 995336 | tf_op jit(solution)/shard_map/ppermute | solution.py:636
  58.1 7.2 %cells.6 = (f32[10368,128]{1,0:T(8,128)S(1)}, f32[2592,128]{1,0:T(8,128)S(1)}, f32[2592,128]{1,0:T(8,128)S(1)}, f32[10368,128]{1,0:T(8,128)S(1)}) custom-call(f32[10368,128]{1,0:T(8,128)S(1)} %get-tuple-element.67.refs_0_, f32[10368,128]{1,0:T(8,128)S(1)} %get-tuple-element.68.refs_1_, ...), custom_call_target="tpu_custom_call", output_to_operand_aliasing={{0}: (1, {}), {3}: (0, {})} | custom-call | tf_op jit(solution)/shard_map/cells/pallas_call | solution.py:509
  65.7 1.9 faces.7
  67.7 5.9 %collective-permute-start.7 = (bf16[1296,128]{1,0:T(8,128)(2,1)S(1)}, bf16[1296,128]{1,0:T(8,128)(2,1)S(1)}, u32[]{:S(2)}, u32[]{:S(2)}) collective-permute-start(bf16[1296,128]{1,0:T(8,128)(2,1)S(1)} %get-tuple-element.85), channel_id=1, source_target_pairs={{8,16},{24,32},{40,48},{56,64},{72,80},{88,96},{104,112},{16,8},{3... | collective-permute-start | bytes 995336 | tf_op jit(solution)/shard_map/ppermute | solution.py:636
  73.6 10.1 %cells.7 = (f32[10368,128]{1,0:T(8,128)S(1)}, f32[2592,128]{1,0:T(8,128)}, f32[2592,128]{1,0:T(8,128)}, bf16[7808,128]{1,0:T(8,128)(2,1)}, f32[10368,128]{1,0:T(8,128)S(1)}) custom-call(f32[10368,128]{1,0:T(8,128)S(1)} %get-tuple-element.86.refs_0_, f32[10368,128]{1,0:T(8,128)S(1)} %get-tuple-element.87.refs_1_, ...), custom_call_target="tpu_custom_call", output_to_operand_aliasing={{0}: (1, {}), {4}: (0, {})} | custom-call | tf_op jit(solution)/shard_map/cells/pallas_call | solution.py:509
  83.7 4.5 %all-to-all-start = ((bf16[8,976,128]{2,1,0:T(8,128)(2,1)}), bf16[8,976,128]{2,1,0:T(8,128)(2,1)}, u32[]{:S(2)}, u32[]{:S(2)}) async-start(bf16[8,976,128]{2,1,0:T(8,128)(2,1)} %bitcast.9), calls=%async_computation | async-start | bytes 3997696 | tf_op jit(solution)/shard_map/all_to_all | solution.py:655
  88.3 1.5 copy-done.6
  89.7 1.3 copy-done.7
  91.0 2.5 %faces.8 = (f32[2592,128]{1,0:T(8,128)S(1)}, bf16[2048,128]{1,0:T(8,128)(2,1)S(1)}, f32[2592,128]{1,0:T(8,128)S(1)}, bf16[1296,128]{1,0:T(8,128)(2,1)S(1)}, bf16[1296,128]{1,0:T(8,128)(2,1)S(1)}) custom-call(f32[2592,128]{1,0:T(8,128)S(1)} %copy-done.7, bf16[1296,128]{1,0:T(8,128)(2,1)S(1)} %collective-permute-done.6.refs_1_, ...), custom_call_target="tpu_custom_call", output_to_operand_aliasing={{2}: (8, {})} | custom-call | tf_op jit(solution)/shard_map/faces/pallas_call | solution.py:367
  93.7 4.5 %collective-permute-start.9 = (bf16[1296,128]{1,0:T(8,128)(2,1)S(1)}, bf16[1296,128]{1,0:T(8,128)(2,1)S(1)}, u32[]{:S(2)}, u32[]{:S(2)}) collective-permute-start(bf16[1296,128]{1,0:T(8,128)(2,1)S(1)} %get-tuple-element.101), channel_id=1, source_target_pairs={{8,16},{24,32},{40,48},{56,64},{72,80},{88,96},{104,112},{16,8},{3... | collective-permute-start | bytes 995336 | tf_op jit(solution)/shard_map/ppermute | solution.py:636
  98.3 2.5 %copy-done.1 = f32[10368,128]{1,0:T(8,128)S(1)} copy-done((f32[10368,128]{1,0:T(8,128)S(1)}, f32[10368,128]{1,0:T(8,128)}, u32[]{:S(2)}) %copy-start.1) | copy-done | bytes 5308440
  100.8 11.1 %last_cells.1 = (f32[2592,128]{1,0:T(8,128)S(1)}, bf16[10368,128]{1,0:T(8,128)(2,1)S(1)}, bf16[11904,128]{1,0:T(8,128)(2,1)S(1)}) custom-call(bf16[7808,128]{1,0:T(8,128)(2,1)S(1)} %copy-done.3, f32[2592,128]{1,0:T(8,128)S(1)} %get-tuple-element.95.refs_1_, bf16[2048,128]{1,0:T(8,128)(2,1)S(1)} %get-tuple-element.96.refs_2_, f32[10368,128]{1,0:T(8,128)S(1)} %copy-done.1, ...), custom_call_target="tpu_custom_call" | custom-call | tf_op jit(solution)/shard_map/last_cells/pallas_call | solution.py:521
  111.9 1.6 copy-done.2
  113.5 3.1 %collective-permute-done.9.refs_2_ = bf16[1296,128]{1,0:T(8,128)(2,1)S(1)} collective-permute-done((bf16[1296,128]{1,0:T(8,128)(2,1)S(1)}, bf16[1296,128]{1,0:T(8,128)(2,1)S(1)}, u32[]{:S(2)}, u32[]{:S(2)}) %collective-permute-start.9) | collective-permute-done | bytes 331808 | tf_op jit(solution)/shard_map/ppermute | solution.py:636
  116.6 1.8 faces.9
  118.5 36.5 %all_to_all.15.mixed_ref = bf16[8,1488,128]{2,1,0:T(8,128)(2,1)S(1)} all-to-all(bf16[8,1488,128]{2,1,0:T(8,128)(2,1)} %bitcast.8), channel_id=1, replica_groups=mesh['space'=16,'band'=8] {'band'}, dimensions={0} | all-to-all | bytes 6094848 | tf_op jit(solution)/shard_map/all_to_all | solution.py:663
  154.9 5.7 %products.1 = (bf16[8,8,64,128]{3,2,1,0:T(8,128)(2,1)S(1)}, bf16[8,8,64,128]{3,2,1,0:T(8,128)(2,1)S(1)}) custom-call(bf16[8,976,128]{2,1,0:T(8,128)(2,1)} %all-to-all-done.states_ref, bf16[8,1488,128]{2,1,0:T(8,128)(2,1)S(1)} %all_to_all.15.mixed_ref, s32[1]{0:T(128)} %bitcast.position_ref.refs_5_), custom_call_target="tpu_custom_call" | custom-call | tf_op jit(solution)/shard_map/products/pallas_call | solution.py:611
  160.7 2.6 %collective-permute-done.10 = bf16[8,8,64,128]{3,2,1,0:T(8,128)(2,1)S(1)} collective-permute-done((bf16[8,8,64,128]{3,2,1,0:T(8,128)(2,1)S(1)}, bf16[8,8,64,128]{3,2,1,0:T(8,128)(2,1)S(1)}, u32[]{:S(2)}, u32[]{:S(2)}) %collective-permute-start.10) | collective-permute-done | bytes 1048608 | tf_op jit(solution)/shard_map/ppermute | solution.py:623
  163.4 1.4 add_convert_fusion
  164.7 15.0 %all-to-all-start.2 = ((bf16[64,64,128]{2,1,0:T(8,128)(2,1)}), bf16[64,64,128]{2,1,0:T(8,128)(2,1)}, u32[]{:S(2)}, u32[]{:S(2)}) async-start(bf16[64,64,128]{2,1,0:T(8,128)(2,1)} %bitcast.10), calls=%async_computation.2 | async-start | bytes 2097152 | tf_op jit(solution)/shard_map/all_to_all | solution.py:626
  180.0 14.6 %hand_back.1 = bf16[10368,128]{1,0:T(8,128)(2,1)} custom-call(bf16[10368,128]{1,0:T(8,128)(2,1)S(1)} %copy-done.5, s32[8,1600]{1,0:T(8,128)S(1)} %reshape.28.index_ref), custom_call_target="tpu_custom_call" | custom-call | tf_op jit(solution)/shard_map/hand_back/pallas_call | solution.py:566
  194.6 3.0 %all-to-all-done.2 = bf16[64,64,128]{2,1,0:T(8,128)(2,1)} async-done(((bf16[64,64,128]{2,1,0:T(8,128)(2,1)}), bf16[64,64,128]{2,1,0:T(8,128)(2,1)}, u32[]{:S(2)}, u32[]{:S(2)}) %all-to-all-start.2) | async-done | bytes 1048608 | tf_op jit(solution)/shard_map/all_to_all | solution.py:626
  197.5 2.0 %convert_reduce_fusion = f32[64,128]{1,0:T(8,128)} fusion(bf16[64,64,128]{2,1,0:T(8,128)(2,1)} %all-to-all-done.2), kind=kLoop, calls=%fused_computation | loop fusion | flops 1040384 | bytes 1081344 | tf_op jit(solution)/shard_map/reduce_sum | solution.py:627
  (35 shorter events, 2.5 us)
Async XLA Ops:
  0.6 17.2 %copy-start.8 = (f32[25]{0:T(128)S(1)}, f32[25]{0:T(128)}, u32[]{:S(2)}) copy-start(f32[25]{0:T(128)} %refs_7_.12) | copy-start | bytes 304
  17.8 55.7 %copy-start = (f32[10368,128]{1,0:T(8,128)}, f32[10368,128]{1,0:T(8,128)S(1)}, u32[]{:S(2)}) copy-start(f32[10368,128]{1,0:T(8,128)S(1)} %get-tuple-element.56.refs_1_.refs_3_) | copy-start | bytes 15925252
  20.0 14.4 %collective-permute-start = (bf16[1296,128]{1,0:T(8,128)(2,1)S(1)}, bf16[1296,128]{1,0:T(8,128)(2,1)S(1)}, u32[]{:S(2)}, u32[]{:S(2)}) collective-permute-start(bf16[1296,128]{1,0:T(8,128)(2,1)S(1)} %get-tuple-element.62), channel_id=1, source_target_pairs={{0,8},{16,24},{32,40},{48,56},{64,72},{80,88},{96,104},{112,120},{... | collective-permute-start | bytes 995336 | tf_op jit(solution)/shard_map/ppermute | solution.py:637
  21.5 13.1 %collective-permute-start.1 = (bf16[1296,128]{1,0:T(8,128)(2,1)S(1)}, bf16[1296,128]{1,0:T(8,128)(2,1)S(1)}, u32[]{:S(2)}, u32[]{:S(2)}) collective-permute-start(bf16[1296,128]{1,0:T(8,128)(2,1)S(1)} %get-tuple-element.63), channel_id=1, source_target_pairs={{8,16},{24,32},{40,48},{56,64},{72,80},{88,96},{104,112},{16,8},{3... | collective-permute-start | bytes 995336 | tf_op jit(solution)/shard_map/ppermute | solution.py:636
  36.5 13.2 %collective-permute-start.2 = (bf16[1296,128]{1,0:T(8,128)(2,1)S(1)}, bf16[1296,128]{1,0:T(8,128)(2,1)S(1)}, u32[]{:S(2)}, u32[]{:S(2)}) collective-permute-start(bf16[1296,128]{1,0:T(8,128)(2,1)S(1)} %get-tuple-element.72), channel_id=1, source_target_pairs={{0,8},{16,24},{32,40},{48,56},{64,72},{80,88},{96,104},{112,120},{... | collective-permute-start | bytes 995336 | tf_op jit(solution)/shard_map/ppermute | solution.py:637
  36.6 13.5 %collective-permute-start.3 = (bf16[1296,128]{1,0:T(8,128)(2,1)S(1)}, bf16[1296,128]{1,0:T(8,128)(2,1)S(1)}, u32[]{:S(2)}, u32[]{:S(2)}) collective-permute-start(bf16[1296,128]{1,0:T(8,128)(2,1)S(1)} %get-tuple-element.73), channel_id=1, source_target_pairs={{8,16},{24,32},{40,48},{56,64},{72,80},{88,96},{104,112},{16,8},{3... | collective-permute-start | bytes 995336 | tf_op jit(solution)/shard_map/ppermute | solution.py:636
  52.1 13.2 %collective-permute-start.4 = (bf16[1296,128]{1,0:T(8,128)(2,1)S(1)}, bf16[1296,128]{1,0:T(8,128)(2,1)S(1)}, u32[]{:S(2)}, u32[]{:S(2)}) collective-permute-start(bf16[1296,128]{1,0:T(8,128)(2,1)S(1)} %get-tuple-element.79), channel_id=1, source_target_pairs={{0,8},{16,24},{32,40},{48,56},{64,72},{80,88},{96,104},{112,120},{... | collective-permute-start | bytes 995336 | tf_op jit(solution)/shard_map/ppermute | solution.py:637
  52.2 13.5 %collective-permute-start.5 = (bf16[1296,128]{1,0:T(8,128)(2,1)S(1)}, bf16[1296,128]{1,0:T(8,128)(2,1)S(1)}, u32[]{:S(2)}, u32[]{:S(2)}) collective-permute-start(bf16[1296,128]{1,0:T(8,128)(2,1)S(1)} %get-tuple-element.80), channel_id=1, source_target_pairs={{8,16},{24,32},{40,48},{56,64},{72,80},{88,96},{104,112},{16,8},{3... | collective-permute-start | bytes 995336 | tf_op jit(solution)/shard_map/ppermute | solution.py:636
  67.6 16.1 %collective-permute-start.6 = (bf16[1296,128]{1,0:T(8,128)(2,1)S(1)}, bf16[1296,128]{1,0:T(8,128)(2,1)S(1)}, u32[]{:S(2)}, u32[]{:S(2)}) collective-permute-start(bf16[1296,128]{1,0:T(8,128)(2,1)S(1)} %get-tuple-element.84), channel_id=1, source_target_pairs={{0,8},{16,24},{32,40},{48,56},{64,72},{80,88},{96,104},{112,120},{... | collective-permute-start | bytes 995336 | tf_op jit(solution)/shard_map/ppermute | solution.py:637
  67.7 16.0 %collective-permute-start.7 = (bf16[1296,128]{1,0:T(8,128)(2,1)S(1)}, bf16[1296,128]{1,0:T(8,128)(2,1)S(1)}, u32[]{:S(2)}, u32[]{:S(2)}) collective-permute-start(bf16[1296,128]{1,0:T(8,128)(2,1)S(1)} %get-tuple-element.85), channel_id=1, source_target_pairs={{8,16},{24,32},{40,48},{56,64},{72,80},{88,96},{104,112},{16,8},{3... | collective-permute-start | bytes 995336 | tf_op jit(solution)/shard_map/ppermute | solution.py:636
  83.7 34.8 %all-to-all-start = ((bf16[8,976,128]{2,1,0:T(8,128)(2,1)}), bf16[8,976,128]{2,1,0:T(8,128)(2,1)}, u32[]{:S(2)}, u32[]{:S(2)}) async-start(bf16[8,976,128]{2,1,0:T(8,128)(2,1)} %bitcast.9), calls=%async_computation | async-start | bytes 3997696 | tf_op jit(solution)/shard_map/all_to_all | solution.py:655
  88.2 10.0 %copy-start.3 = (bf16[7808,128]{1,0:T(8,128)(2,1)S(1)}, bf16[7808,128]{1,0:T(8,128)(2,1)}, u32[]{:S(2)}) copy-start(bf16[7808,128]{1,0:T(8,128)(2,1)} %get-tuple-element.90.refs_0_) | copy-start | bytes 5996548
  88.2 1.5 copy-start.6
  89.7 1.3 copy-start.7
  93.6 19.9 %collective-permute-start.8 = (bf16[1296,128]{1,0:T(8,128)(2,1)S(1)}, bf16[1296,128]{1,0:T(8,128)(2,1)S(1)}, u32[]{:S(2)}, u32[]{:S(2)}) collective-permute-start(bf16[1296,128]{1,0:T(8,128)(2,1)S(1)} %get-tuple-element.100), channel_id=1, source_target_pairs={{0,8},{16,24},{32,40},{48,56},{64,72},{80,88},{96,104},{112,120},{... | collective-permute-start | bytes 995336 | tf_op jit(solution)/shard_map/ppermute | solution.py:637
  93.7 23.0 %collective-permute-start.9 = (bf16[1296,128]{1,0:T(8,128)(2,1)S(1)}, bf16[1296,128]{1,0:T(8,128)(2,1)S(1)}, u32[]{:S(2)}, u32[]{:S(2)}) collective-permute-start(bf16[1296,128]{1,0:T(8,128)(2,1)S(1)} %get-tuple-element.101), channel_id=1, source_target_pairs={{8,16},{24,32},{40,48},{56,64},{72,80},{88,96},{104,112},{16,8},{3... | collective-permute-start | bytes 995336 | tf_op jit(solution)/shard_map/ppermute | solution.py:636
  98.2 2.5 %copy-start.1 = (f32[10368,128]{1,0:T(8,128)S(1)}, f32[10368,128]{1,0:T(8,128)}, u32[]{:S(2)}) copy-start(f32[10368,128]{1,0:T(8,128)} %copy-done) | copy-start | bytes 15925252
  111.9 1.6 copy-start.2
  113.5 5.0 %copy-start.4 = (bf16[10368,128]{1,0:T(8,128)(2,1)}, bf16[10368,128]{1,0:T(8,128)(2,1)S(1)}, u32[]{:S(2)}) copy-start(bf16[10368,128]{1,0:T(8,128)(2,1)S(1)} %get-tuple-element.104.plain_ref) | copy-start | bytes 7962628
  160.6 2.7 %collective-permute-start.10 = (bf16[8,8,64,128]{3,2,1,0:T(8,128)(2,1)S(1)}, bf16[8,8,64,128]{3,2,1,0:T(8,128)(2,1)S(1)}, u32[]{:S(2)}, u32[]{:S(2)}) collective-permute-start(bf16[8,8,64,128]{3,2,1,0:T(8,128)(2,1)S(1)} %get-tuple-element.107), channel_id=1, source_target_pairs={{0,8},{8,0},{16,24},{24,16},{32,40},{40,32},{48,56},{56,48},{64,72... | collective-permute-start | bytes 3145736 | tf_op jit(solution)/shard_map/ppermute | solution.py:623
  163.4 16.4 %copy-start.9 = (s32[25,512]{1,0:T(8,128)S(1)}, s32[25,512]{1,0:T(8,128)}, u32[]{:S(2)}) copy-start(s32[25,512]{1,0:T(8,128)} %index_hbm.1) | copy-start | bytes 153604
  164.7 15.2 %copy-start.5 = (bf16[10368,128]{1,0:T(8,128)(2,1)S(1)}, bf16[10368,128]{1,0:T(8,128)(2,1)}, u32[]{:S(2)}) copy-start(bf16[10368,128]{1,0:T(8,128)(2,1)} %copy-done.4) | copy-start | bytes 7962628
  164.7 32.8 %all-to-all-start.2 = ((bf16[64,64,128]{2,1,0:T(8,128)(2,1)}), bf16[64,64,128]{2,1,0:T(8,128)(2,1)}, u32[]{:S(2)}, u32[]{:S(2)}) async-start(bf16[64,64,128]{2,1,0:T(8,128)(2,1)} %bitcast.10), calls=%async_computation.2 | async-start | bytes 2097152 | tf_op jit(solution)/shard_map/all_to_all | solution.py:626

commit v7 on v6

--- a/solution.py
+++ b/solution.py
@@ -247,8 +247,9 @@
 
 def put_outer(face_ref, odd, far_weight, store):
     def rows(i, _):
-        for part in range(4):
-            row = (i * 4 + part) * 16
+        ready = []
+        for part in range(8):
+            row = (i * 8 + part) * 16
             far = row < FACE
             near_at = (1 - odd) * FACE + odd * (FACE // 2) + row - FACE
             at = jnp.where(far, odd * FACE + row, jnp.minimum(near_at, 2 * FACE - 16))
@@ -256,10 +257,12 @@
             if far_weight is not None:
                 value = value * jnp.where(far, far_weight, 1.0)
             index = lax.broadcasted_iota(jnp.int32, (16, COLS), 0) + row
-            store(row, jnp.where(index < OUTER, value, 0.0).astype(BF16))
-        return 0
-
-    lax.fori_loop(0, BANDS * OUTER_BLOCK // 64, rows, 0)
+            ready.append((row, jnp.where(index < OUTER, value, 0.0).astype(BF16)))
+        for row, value in ready:
+            store(row, value)
+        return 0
+
+    lax.fori_loop(0, BANDS * OUTER_BLOCK // 128, rows, 0)
 
 
 def faces_kernel(stage, *refs):
@@ -603,6 +606,14 @@
     lax.fori_loop(0, BANDS // 2, step, 0)
 
 
+def total_kernel(parts_ref, total_ref):
+    for row in range(0, COLS // 2, 16):
+        sums = [jnp.zeros((16, COLS), F32)] * 4
+        for part in range(parts_ref.shape[0]):
+            sums[part % 4] = sums[part % 4] + parts_ref[part, row : row + 16, :].astype(F32)
+        total_ref[row : row + 16, :] = (sums[0] + sums[1]) + (sums[2] + sums[3])
+
+
 def project(states, mixed, position):
     count = lax.axis_size("space")
     halves = count // 2
@@ -624,7 +635,14 @@
     both = (kept.astype(F32) + got.astype(F32)).astype(BF16).reshape(halves * BANDS, COLS // 2, COLS)
     groups = [[(2 * half + part) * BANDS + band for half in range(halves) for band in range(BANDS)] for part in range(2)]
     arrived = lax.all_to_all(both, ("space", "band"), split_axis=0, concat_axis=0, tiled=True, axis_index_groups=groups)
-    return arrived.astype(F32).sum(axis=0).T
+    return pl.pallas_call(
+        total_kernel,
+        name="total",
+        out_shape=jax.ShapeDtypeStruct((COLS // 2, COLS), F32),
+        in_specs=[VMEM],
+        out_specs=VMEM,
+        compiler_params=SMALL,
+    )(arrived).T
 
 
 def swap_faces(near, far):

time: 201 us -> 199 us (0.990)
    reduce_sum x1 -> x0, other arithmetic: 2.01 us -> none  [project(): return arrived.astype(F32).sum(axis=0).T]
where the time goes in v7:
time: 199 us; the launch traced here: 198 us
  Pallas kernels  91.1 us (46%)
  starting transfers between devices  48.8 us (25%)
  blocking collectives  36.3 us (18%)
  local copies, waits for them, and re-layouts  9.7 us (5%)
  waiting for transfers between devices  8.34 us (4%)
  between operations  2.27 us (1%)
    all_to_all x1, blocking collectives, local(): lax.all_to_all(blocks.reshape(BANDS, BLOCK, COLS), 'band', split_axis=0,...  36.3 us
    pallas_call x4, Pallas kernels, cells(): pl.pallas_call(functools.partial(cells_kernel, stage), name='cells', out_...  31.8 us
    ppermute x5, starting transfers between devices, swap_faces(): from_far = lax.ppermute(far, 'space', both_ways(apart))  27.8 us
    pallas_call x1, Pallas kernels, gather(): pl.pallas_call(gather_kernel, name='gather_states', out_shape=(pltpu.VMEM...  15 us
    all_to_all x1, starting transfers between devices, project(): lax.all_to_all(both, ('space', 'band'), split_axis=0, concat_axis=0, tile...  14.6 us
    pallas_call x1, Pallas kernels, hand_back(): pl.pallas_call(return_kernel, name='hand_back', out_shape=jax.ShapeDtypeS...  14.6 us
    pallas_call x1, Pallas kernels, last_cells(): pl.pallas_call(functools.partial(cells_kernel, STEPS + 1), name='last_cel...  11.1 us
    pallas_call x5, Pallas kernels, faces(): pl.pallas_call(functools.partial(faces_kernel, stage), name='faces', out_...  9.89 us
  transfers between devices with their start and end apart: 13, of which 6 were waited for; matrix products, arithmetic and copies ran while one was open for 0% of the time, Pallas kernels for 31%

profile of v7, /device:TPU:1, one launch (start us, length us, event | category | flops | bytes accessed | tf_op | source)
XLA Modules:
  0.0 197.9 jit_solution(777087417126272991)
XLA Ops:
  2.8 15.0 %gather_states.1 = (f32[10368,128]{1,0:T(8,128)S(1)}, f32[10368,128]{1,0:T(8,128)S(1)}, bf16[512,512]{1,0:T(8,128)(2,1)S(1)}, bf16[128,512]{1,0:T(8,128)(2,1)S(1...) custom-call(bf16[10368,128]{1,0:T(8,128)(2,1)} %states_hbm.1, f32[8,1296]{1,0:T(8,128)S(1)} %reshape.25.pot_ref, ...), custom_call_target="tpu_custom_call" | custom-call | tf_op jit(solution)/shard_map/gather_states/pallas_call | solution.py:119
  17.8 2.2 %first_faces.1 = (bf16[1296,128]{1,0:T(8,128)(2,1)S(1)}, bf16[1296,128]{1,0:T(8,128)(2,1)S(1)}) custom-call(f32[10368,128]{1,0:T(8,128)S(1)} %get-tuple-element.55.refs_0_.field_ref.refs_1_, bf16[128,512]{1,0:T(8,128)(2,1)S(1)} %get-tuple-element.61.full_ref, f32[25]{0:T(128)S(1)} %copy-done.8, s32[1]{0:T(128)} %bitcast.position_ref.refs_5_), custom_call_target="tpu_custom_call" | custom-call | tf_op jit(solution)/shard_map/first_faces/pallas_call | solution.py:223
  20.0 1.5 collective-permute-start
  21.5 5.5 %collective-permute-start.1 = (bf16[1296,128]{1,0:T(8,128)(2,1)S(1)}, bf16[1296,128]{1,0:T(8,128)(2,1)S(1)}, u32[]{:S(2)}, u32[]{:S(2)}) collective-permute-start(bf16[1296,128]{1,0:T(8,128)(2,1)S(1)} %get-tuple-element.63), channel_id=1, source_target_pairs={{8,16},{24,32},{40,48},{56,64},{72,80},{88,96},{104,112},{16,8},{3... | collective-permute-start | bytes 995336 | tf_op jit(solution)/shard_map/ppermute | solution.py:654
  27.0 7.3 %cells.4 = (f32[10368,128]{1,0:T(8,128)S(1)}, f32[2592,128]{1,0:T(8,128)S(1)}, f32[2592,128]{1,0:T(8,128)S(1)}) custom-call(f32[10368,128]{1,0:T(8,128)S(1)} %get-tuple-element.55.refs_0_.field_ref.refs_1_, f32[10368,128]{1,0:T(8,128)S(1)} %get-tuple-element.56.refs_1_.refs_3_, bf16[512,512]{1,0:T(8,128)(2,1)S(1)} %get-tuple-element.57.refs_2_.refs_4_, ...), custom_call_target="tpu_custom_call" | custom-call | tf_op jit(solution)/shard_map/cells/pallas_call | solution.py:512
  34.6 1.9 faces.5
  36.6 5.9 %collective-permute-start.3 = (bf16[1296,128]{1,0:T(8,128)(2,1)S(1)}, bf16[1296,128]{1,0:T(8,128)(2,1)S(1)}, u32[]{:S(2)}, u32[]{:S(2)}) collective-permute-start(bf16[1296,128]{1,0:T(8,128)(2,1)S(1)} %get-tuple-element.73), channel_id=1, source_target_pairs={{8,16},{24,32},{40,48},{56,64},{72,80},{88,96},{104,112},{16,8},{3... | collective-permute-start | bytes 995336 | tf_op jit(solution)/shard_map/ppermute | solution.py:654
  42.5 7.2 %cells.5 = (f32[10368,128]{1,0:T(8,128)S(1)}, f32[2592,128]{1,0:T(8,128)S(1)}, f32[2592,128]{1,0:T(8,128)S(1)}, f32[10368,128]{1,0:T(8,128)S(1)}) custom-call(f32[10368,128]{1,0:T(8,128)S(1)} %get-tuple-element.59.refs_0_, f32[10368,128]{1,0:T(8,128)S(1)} %get-tuple-element.55.refs_0_.field_ref.refs_1_, ...), custom_call_target="tpu_custom_call", output_to_operand_aliasing={{0}: (1, {}), {3}: (0, {})} | custom-call | tf_op jit(solution)/shard_map/cells/pallas_call | solution.py:512
  50.1 1.9 faces.6
  52.2 5.9 %collective-permute-start.5 = (bf16[1296,128]{1,0:T(8,128)(2,1)S(1)}, bf16[1296,128]{1,0:T(8,128)(2,1)S(1)}, u32[]{:S(2)}, u32[]{:S(2)}) collective-permute-start(bf16[1296,128]{1,0:T(8,128)(2,1)S(1)} %get-tuple-element.80), channel_id=1, source_target_pairs={{8,16},{24,32},{40,48},{56,64},{72,80},{88,96},{104,112},{16,8},{3... | collective-permute-start | bytes 995336 | tf_op jit(solution)/shard_map/ppermute | solution.py:654
  58.1 7.2 %cells.6 = (f32[10368,128]{1,0:T(8,128)S(1)}, f32[2592,128]{1,0:T(8,128)S(1)}, f32[2592,128]{1,0:T(8,128)S(1)}, f32[10368,128]{1,0:T(8,128)S(1)}) custom-call(f32[10368,128]{1,0:T(8,128)S(1)} %get-tuple-element.67.refs_0_, f32[10368,128]{1,0:T(8,128)S(1)} %get-tuple-element.68.refs_1_, ...), custom_call_target="tpu_custom_call", output_to_operand_aliasing={{0}: (1, {}), {3}: (0, {})} | custom-call | tf_op jit(solution)/shard_map/cells/pallas_call | solution.py:512
  65.7 1.9 faces.7
  67.7 5.9 %collective-permute-start.7 = (bf16[1296,128]{1,0:T(8,128)(2,1)S(1)}, bf16[1296,128]{1,0:T(8,128)(2,1)S(1)}, u32[]{:S(2)}, u32[]{:S(2)}) collective-permute-start(bf16[1296,128]{1,0:T(8,128)(2,1)S(1)} %get-tuple-element.85), channel_id=1, source_target_pairs={{8,16},{24,32},{40,48},{56,64},{72,80},{88,96},{104,112},{16,8},{3... | collective-permute-start | bytes 995336 | tf_op jit(solution)/shard_map/ppermute | solution.py:654
  73.6 10.1 %cells.7 = (f32[10368,128]{1,0:T(8,128)S(1)}, f32[2592,128]{1,0:T(8,128)}, f32[2592,128]{1,0:T(8,128)}, bf16[7808,128]{1,0:T(8,128)(2,1)}, f32[10368,128]{1,0:T(8,128)S(1)}) custom-call(f32[10368,128]{1,0:T(8,128)S(1)} %get-tuple-element.86.refs_0_, f32[10368,128]{1,0:T(8,128)S(1)} %get-tuple-element.87.refs_1_, ...), custom_call_target="tpu_custom_call", output_to_operand_aliasing={{0}: (1, {}), {4}: (0, {})} | custom-call | tf_op jit(solution)/shard_map/cells/pallas_call | solution.py:512
  83.7 4.5 %all-to-all-start = ((bf16[8,976,128]{2,1,0:T(8,128)(2,1)}), bf16[8,976,128]{2,1,0:T(8,128)(2,1)}, u32[]{:S(2)}, u32[]{:S(2)}) async-start(bf16[8,976,128]{2,1,0:T(8,128)(2,1)} %bitcast.9), calls=%async_computation | async-start | bytes 3997696 | tf_op jit(solution)/shard_map/all_to_all | solution.py:673
  88.2 1.5 copy-done.6
  89.7 1.3 copy-done.7
  91.0 2.4 %faces.8 = (f32[2592,128]{1,0:T(8,128)S(1)}, bf16[2048,128]{1,0:T(8,128)(2,1)S(1)}, f32[2592,128]{1,0:T(8,128)S(1)}, bf16[1296,128]{1,0:T(8,128)(2,1)S(1)}, bf16[1296,128]{1,0:T(8,128)(2,1)S(1)}) custom-call(f32[2592,128]{1,0:T(8,128)S(1)} %copy-done.7, bf16[1296,128]{1,0:T(8,128)(2,1)S(1)} %collective-permute-done.6.refs_1_, ...), custom_call_target="tpu_custom_call", output_to_operand_aliasing={{2}: (8, {})} | custom-call | tf_op jit(solution)/shard_map/faces/pallas_call | solution.py:370
  93.6 4.6 %collective-permute-start.9 = (bf16[1296,128]{1,0:T(8,128)(2,1)S(1)}, bf16[1296,128]{1,0:T(8,128)(2,1)S(1)}, u32[]{:S(2)}, u32[]{:S(2)}) collective-permute-start(bf16[1296,128]{1,0:T(8,128)(2,1)S(1)} %get-tuple-element.101), channel_id=1, source_target_pairs={{8,16},{24,32},{40,48},{56,64},{72,80},{88,96},{104,112},{16,8},{3... | collective-permute-start | bytes 995336 | tf_op jit(solution)/shard_map/ppermute | solution.py:654
  98.2 2.5 %copy-done.1 = f32[10368,128]{1,0:T(8,128)S(1)} copy-done((f32[10368,128]{1,0:T(8,128)S(1)}, f32[10368,128]{1,0:T(8,128)}, u32[]{:S(2)}) %copy-start.1) | copy-done | bytes 5308440
  100.7 11.1 %last_cells.1 = (f32[2592,128]{1,0:T(8,128)S(1)}, bf16[10368,128]{1,0:T(8,128)(2,1)S(1)}, bf16[11904,128]{1,0:T(8,128)(2,1)S(1)}) custom-call(bf16[7808,128]{1,0:T(8,128)(2,1)S(1)} %copy-done.3, f32[2592,128]{1,0:T(8,128)S(1)} %get-tuple-element.95.refs_1_, bf16[2048,128]{1,0:T(8,128)(2,1)S(1)} %get-tuple-element.96.refs_2_, f32[10368,128]{1,0:T(8,128)S(1)} %copy-done.1, ...), custom_call_target="tpu_custom_call" | custom-call | tf_op jit(solution)/shard_map/last_cells/pallas_call | solution.py:524
  111.8 1.6 copy-done.2
  113.4 3.3 %collective-permute-done.9.refs_2_ = bf16[1296,128]{1,0:T(8,128)(2,1)S(1)} collective-permute-done((bf16[1296,128]{1,0:T(8,128)(2,1)S(1)}, bf16[1296,128]{1,0:T(8,128)(2,1)S(1)}, u32[]{:S(2)}, u32[]{:S(2)}) %collective-permute-start.9) | collective-permute-done | bytes 331808 | tf_op jit(solution)/shard_map/ppermute | solution.py:654
  116.6 1.7 faces.9
  118.3 36.3 %all_to_all.15.mixed_ref = bf16[8,1488,128]{2,1,0:T(8,128)(2,1)S(1)} all-to-all(bf16[8,1488,128]{2,1,0:T(8,128)(2,1)} %bitcast.8), channel_id=1, replica_groups=mesh['space'=16,'band'=8] {'band'}, dimensions={0} | all-to-all | bytes 6094848 | tf_op jit(solution)/shard_map/all_to_all | solution.py:681
  154.7 5.7 %products.1 = (bf16[8,8,64,128]{3,2,1,0:T(8,128)(2,1)S(1)}, bf16[8,8,64,128]{3,2,1,0:T(8,128)(2,1)S(1)}) custom-call(bf16[8,976,128]{2,1,0:T(8,128)(2,1)} %all-to-all-done.states_ref, bf16[8,1488,128]{2,1,0:T(8,128)(2,1)S(1)} %all_to_all.15.mixed_ref, s32[1]{0:T(128)} %bitcast.position_ref.refs_5_), custom_call_target="tpu_custom_call" | custom-call | tf_op jit(solution)/shard_map/products/pallas_call | solution.py:622
  160.5 2.6 %collective-permute-done.10 = bf16[8,8,64,128]{3,2,1,0:T(8,128)(2,1)S(1)} collective-permute-done((bf16[8,8,64,128]{3,2,1,0:T(8,128)(2,1)S(1)}, bf16[8,8,64,128]{3,2,1,0:T(8,128)(2,1)S(1)}, u32[]{:S(2)}, u32[]{:S(2)}) %collective-permute-start.10) | collective-permute-done | bytes 1048608 | tf_op jit(solution)/shard_map/ppermute | solution.py:634
  163.1 1.4 add_convert_fusion
  164.5 14.6 %all-to-all-start.2 = ((bf16[64,64,128]{2,1,0:T(8,128)(2,1)}), bf16[64,64,128]{2,1,0:T(8,128)(2,1)S(1)}, u32[]{:S(2)}, u32[]{:S(2)}) async-start(bf16[64,64,128]{2,1,0:T(8,128)(2,1)} %bitcast.4), calls=%async_computation.2 | async-start | bytes 2097152 | tf_op jit(solution)/shard_map/all_to_all | solution.py:637
  179.4 1.7 copy-done.5
  181.1 14.6 %hand_back.1 = bf16[10368,128]{1,0:T(8,128)(2,1)} custom-call(bf16[10368,128]{1,0:T(8,128)(2,1)S(1)} %copy-done.5, s32[8,1600]{1,0:T(8,128)S(1)} %reshape.28.index_ref), custom_call_target="tpu_custom_call" | custom-call | tf_op jit(solution)/shard_map/hand_back/pallas_call | solution.py:569
  195.7 1.4 all-to-all-done.2.parts_ref
  (35 shorter events, 3.3 us)
Async XLA Ops:
  0.6 17.2 %copy-start.8 = (f32[25]{0:T(128)S(1)}, f32[25]{0:T(128)}, u32[]{:S(2)}) copy-start(f32[25]{0:T(128)} %refs_7_.12) | copy-start | bytes 304
  17.8 55.8 %copy-start = (f32[10368,128]{1,0:T(8,128)}, f32[10368,128]{1,0:T(8,128)S(1)}, u32[]{:S(2)}) copy-start(f32[10368,128]{1,0:T(8,128)S(1)} %get-tuple-element.56.refs_1_.refs_3_) | copy-start | bytes 15925252
  20.0 14.3 %collective-permute-start = (bf16[1296,128]{1,0:T(8,128)(2,1)S(1)}, bf16[1296,128]{1,0:T(8,128)(2,1)S(1)}, u32[]{:S(2)}, u32[]{:S(2)}) collective-permute-start(bf16[1296,128]{1,0:T(8,128)(2,1)S(1)} %get-tuple-element.62), channel_id=1, source_target_pairs={{0,8},{16,24},{32,40},{48,56},{64,72},{80,88},{96,104},{112,120},{... | collective-permute-start | bytes 995336 | tf_op jit(solution)/shard_map/ppermute | solution.py:655
  21.5 13.1 %collective-permute-start.1 = (bf16[1296,128]{1,0:T(8,128)(2,1)S(1)}, bf16[1296,128]{1,0:T(8,128)(2,1)S(1)}, u32[]{:S(2)}, u32[]{:S(2)}) collective-permute-start(bf16[1296,128]{1,0:T(8,128)(2,1)S(1)} %get-tuple-element.63), channel_id=1, source_target_pairs={{8,16},{24,32},{40,48},{56,64},{72,80},{88,96},{104,112},{16,8},{3... | collective-permute-start | bytes 995336 | tf_op jit(solution)/shard_map/ppermute | solution.py:654
  36.6 13.2 %collective-permute-start.2 = (bf16[1296,128]{1,0:T(8,128)(2,1)S(1)}, bf16[1296,128]{1,0:T(8,128)(2,1)S(1)}, u32[]{:S(2)}, u32[]{:S(2)}) collective-permute-start(bf16[1296,128]{1,0:T(8,128)(2,1)S(1)} %get-tuple-element.72), channel_id=1, source_target_pairs={{0,8},{16,24},{32,40},{48,56},{64,72},{80,88},{96,104},{112,120},{... | collective-permute-start | bytes 995336 | tf_op jit(solution)/shard_map/ppermute | solution.py:655
  36.6 13.5 %collective-permute-start.3 = (bf16[1296,128]{1,0:T(8,128)(2,1)S(1)}, bf16[1296,128]{1,0:T(8,128)(2,1)S(1)}, u32[]{:S(2)}, u32[]{:S(2)}) collective-permute-start(bf16[1296,128]{1,0:T(8,128)(2,1)S(1)} %get-tuple-element.73), channel_id=1, source_target_pairs={{8,16},{24,32},{40,48},{56,64},{72,80},{88,96},{104,112},{16,8},{3... | collective-permute-start | bytes 995336 | tf_op jit(solution)/shard_map/ppermute | solution.py:654
  52.1 13.2 %collective-permute-start.4 = (bf16[1296,128]{1,0:T(8,128)(2,1)S(1)}, bf16[1296,128]{1,0:T(8,128)(2,1)S(1)}, u32[]{:S(2)}, u32[]{:S(2)}) collective-permute-start(bf16[1296,128]{1,0:T(8,128)(2,1)S(1)} %get-tuple-element.79), channel_id=1, source_target_pairs={{0,8},{16,24},{32,40},{48,56},{64,72},{80,88},{96,104},{112,120},{... | collective-permute-start | bytes 995336 | tf_op jit(solution)/shard_map/ppermute | solution.py:655
  52.2 13.5 %collective-permute-start.5 = (bf16[1296,128]{1,0:T(8,128)(2,1)S(1)}, bf16[1296,128]{1,0:T(8,128)(2,1)S(1)}, u32[]{:S(2)}, u32[]{:S(2)}) collective-permute-start(bf16[1296,128]{1,0:T(8,128)(2,1)S(1)} %get-tuple-element.80), channel_id=1, source_target_pairs={{8,16},{24,32},{40,48},{56,64},{72,80},{88,96},{104,112},{16,8},{3... | collective-permute-start | bytes 995336 | tf_op jit(solution)/shard_map/ppermute | solution.py:654
  67.6 16.1 %collective-permute-start.6 = (bf16[1296,128]{1,0:T(8,128)(2,1)S(1)}, bf16[1296,128]{1,0:T(8,128)(2,1)S(1)}, u32[]{:S(2)}, u32[]{:S(2)}) collective-permute-start(bf16[1296,128]{1,0:T(8,128)(2,1)S(1)} %get-tuple-element.84), channel_id=1, source_target_pairs={{0,8},{16,24},{32,40},{48,56},{64,72},{80,88},{96,104},{112,120},{... | collective-permute-start | bytes 995336 | tf_op jit(solution)/shard_map/ppermute | solution.py:655
  67.7 16.0 %collective-permute-start.7 = (bf16[1296,128]{1,0:T(8,128)(2,1)S(1)}, bf16[1296,128]{1,0:T(8,128)(2,1)S(1)}, u32[]{:S(2)}, u32[]{:S(2)}) collective-permute-start(bf16[1296,128]{1,0:T(8,128)(2,1)S(1)} %get-tuple-element.85), channel_id=1, source_target_pairs={{8,16},{24,32},{40,48},{56,64},{72,80},{88,96},{104,112},{16,8},{3... | collective-permute-start | bytes 995336 | tf_op jit(solution)/shard_map/ppermute | solution.py:654
  83.7 34.7 %all-to-all-start = ((bf16[8,976,128]{2,1,0:T(8,128)(2,1)}), bf16[8,976,128]{2,1,0:T(8,128)(2,1)}, u32[]{:S(2)}, u32[]{:S(2)}) async-start(bf16[8,976,128]{2,1,0:T(8,128)(2,1)} %bitcast.9), calls=%async_computation | async-start | bytes 3997696 | tf_op jit(solution)/shard_map/all_to_all | solution.py:673
  88.2 9.9 %copy-start.3 = (bf16[7808,128]{1,0:T(8,128)(2,1)S(1)}, bf16[7808,128]{1,0:T(8,128)(2,1)}, u32[]{:S(2)}) copy-start(bf16[7808,128]{1,0:T(8,128)(2,1)} %get-tuple-element.90.refs_0_) | copy-start | bytes 5996548
  88.2 1.5 copy-start.6
  89.7 1.3 copy-start.7
  93.5 19.9 %collective-permute-start.8 = (bf16[1296,128]{1,0:T(8,128)(2,1)S(1)}, bf16[1296,128]{1,0:T(8,128)(2,1)S(1)}, u32[]{:S(2)}, u32[]{:S(2)}) collective-permute-start(bf16[1296,128]{1,0:T(8,128)(2,1)S(1)} %get-tuple-element.100), channel_id=1, source_target_pairs={{0,8},{16,24},{32,40},{48,56},{64,72},{80,88},{96,104},{112,120},{... | collective-permute-start | bytes 995336 | tf_op jit(solution)/shard_map/ppermute | solution.py:655
  93.6 23.1 %collective-permute-start.9 = (bf16[1296,128]{1,0:T(8,128)(2,1)S(1)}, bf16[1296,128]{1,0:T(8,128)(2,1)S(1)}, u32[]{:S(2)}, u32[]{:S(2)}) collective-permute-start(bf16[1296,128]{1,0:T(8,128)(2,1)S(1)} %get-tuple-element.101), channel_id=1, source_target_pairs={{8,16},{24,32},{40,48},{56,64},{72,80},{88,96},{104,112},{16,8},{3... | collective-permute-start | bytes 995336 | tf_op jit(solution)/shard_map/ppermute | solution.py:654
  98.1 2.5 %copy-start.1 = (f32[10368,128]{1,0:T(8,128)S(1)}, f32[10368,128]{1,0:T(8,128)}, u32[]{:S(2)}) copy-start(f32[10368,128]{1,0:T(8,128)} %copy-done) | copy-start | bytes 15925252
  111.7 1.6 copy-start.2
  113.3 5.0 %copy-start.4 = (bf16[10368,128]{1,0:T(8,128)(2,1)}, bf16[10368,128]{1,0:T(8,128)(2,1)S(1)}, u32[]{:S(2)}) copy-start(bf16[10368,128]{1,0:T(8,128)(2,1)S(1)} %get-tuple-element.104.plain_ref) | copy-start | bytes 7962628
  160.4 2.7 %collective-permute-start.10 = (bf16[8,8,64,128]{3,2,1,0:T(8,128)(2,1)S(1)}, bf16[8,8,64,128]{3,2,1,0:T(8,128)(2,1)S(1)}, u32[]{:S(2)}, u32[]{:S(2)}) collective-permute-start(bf16[8,8,64,128]{3,2,1,0:T(8,128)(2,1)S(1)} %get-tuple-element.107), channel_id=1, source_target_pairs={{0,8},{8,0},{16,24},{24,16},{32,40},{40,32},{48,56},{56,48},{64,72... | collective-permute-start | bytes 3145736 | tf_op jit(solution)/shard_map/ppermute | solution.py:634
  163.1 16.0 %copy-start.9 = (s32[25,512]{1,0:T(8,128)S(1)}, s32[25,512]{1,0:T(8,128)}, u32[]{:S(2)}) copy-start(s32[25,512]{1,0:T(8,128)} %index_hbm.1) | copy-start | bytes 153604
  164.5 32.6 %all-to-all-start.2 = ((bf16[64,64,128]{2,1,0:T(8,128)(2,1)}), bf16[64,64,128]{2,1,0:T(8,128)(2,1)S(1)}, u32[]{:S(2)}, u32[]{:S(2)}) async-start(bf16[64,64,128]{2,1,0:T(8,128)(2,1)} %bitcast.4), calls=%async_computation.2 | async-start | bytes 2097152 | tf_op jit(solution)/shard_map/all_to_all | solution.py:637
  179.4 1.8 copy-start.5
